TPU v7x, 32 devices: a whole 2x2x4 slice. The times are simulated.
32 devices in a mesh: dp: 2 (over core), seq: 4 (over y, x), tensor: 4 (over z).
Axes of the slice: x: 2, y: 2, z: 4, core: 2. Of those that a mesh axis runs over, the one named last changes fastest.
Arguments:
- hidden: float32 [2, 3120, 1536], P('dp', 'seq'), may hold values from -6 to 6
- teacher: float32 [2, 3120, 1536], P('dp', 'seq'), may hold values from -6 to 6
- text: float32 [2, 512, 1536], P('dp', 'seq'), may hold values from -6 to 6
- time_embed: float32 [2, 6, 1536], P('dp'), may hold values from -3 to 3
- lengths: int32 [2], replicated, may hold values from 780 to 3120, as said below
- positions: int32 [3, 2, 3120], P(None, 'dp', 'seq'), may hold values from 0 to 63
- modulation: float32 [6, 1536], replicated, may hold values from -2 to 2
- self_in: bfloat16 [3, 1536, 1536], P(None, None, 'tensor'), may hold values from -0.15625 to 0.15625
- self_bias: float32 [3, 1536], P(None, 'tensor'), may hold values from -2 to 2
- self_out: bfloat16 [1536, 1536], P('tensor'), may hold values from -0.875 to 0.875
- norm_gains: float32 [4, 1536], P(None, 'tensor'), may hold values from 1 to 2
- cross_gain: float32 [1536], replicated, may hold values from 0.5 to 1.5
- cross_shift: float32 [1536], replicated, may hold values from -2 to 2
- cross_q: bfloat16 [1536, 1536], P(None, 'tensor'), may hold values from -0.15625 to 0.15625
- cross_kv: bfloat16 [2, 1536, 1536], P(None, None, 'tensor'), may hold values from -0.15625 to 0.15625
- cross_bias: float32 [3, 1536], P(None, 'tensor'), may hold values from -2 to 2
- cross_out: bfloat16 [1536, 1536], P('tensor'), may hold values from -0.4375 to 0.4375
- ffn_in: bfloat16 [1536, 8960], P(None, 'tensor'), may hold values from -0.15625 to 0.15625
- ffn_in_bias: float32 [8960], P('tensor'), may hold values from -2 to 2
- ffn_out: bfloat16 [8960, 1536], P('tensor'), may hold values from -0.0625 to 0.0625
- out_bias: float32 [3, 1536], replicated, may hold values from -2 to 2
Outputs:
- result: float32 [2, 3120, 1536], P('dp', 'seq')
- loss: float32 [], replicated
- grad_hidden: float32 [2, 3120, 1536], P('dp', 'seq')
- grad_text: float32 [2, 512, 1536], P('dp', 'seq')
- grad_time: float32 [2, 6, 1536], P('dp')
- grad_modulation: float32 [6, 1536], replicated
- grad_self_in: float32 [3, 1536, 1536], P(None, ('dp', 'seq'), 'tensor')
- grad_self_bias: float32 [3, 1536], P(None, 'tensor')
- grad_self_out: float32 [1536, 1536], P('tensor', ('dp', 'seq'))
- grad_norm_gains: float32 [4, 1536], P(None, 'tensor')
- grad_cross_gain: float32 [1536], replicated
- grad_cross_shift: float32 [1536], replicated
- grad_cross_q: float32 [1536, 1536], P(('dp', 'seq'), 'tensor')
- grad_cross_kv: float32 [2, 1536, 1536], P(None, ('dp', 'seq'), 'tensor')
- grad_cross_bias: float32 [3, 1536], P(None, 'tensor')
- grad_cross_out: float32 [1536, 1536], P('tensor', ('dp', 'seq'))
- grad_ffn_in: float32 [1536, 8960], P(('dp', 'seq'), 'tensor')
- grad_ffn_in_bias: float32 [8960], P('tensor')
- grad_ffn_out: float32 [8960, 1536], P('tensor', ('dp', 'seq'))
- grad_out_bias: float32 [3, 1536], replicated
Inputs may be any that keep to these rules, and one draw needn't show every extreme that they name: Each clip's first lengths slots are valid and the rest are padding; some clip is full (3120 slots) and some clip has exactly 780.
All inputs are finite; a program needn't handle non-finite values.
Results may differ from a plain program's by a relative error of at most 0.017.
The roundings to bfloat16 on the way count: a program that leaves them out, or rounds other values in their place, can miss the bound.
Values may be sent and summed in bfloat16 or wider, within the bound.
A program may use at most 448 MiB of HBM per device.

v0:
```python
import functools
import math

import jax
import jax.numpy as jnp
from jax import lax
from jax.sharding import PartitionSpec as P

HEAD_DIM = 128


eps_norm = 1e-06


def layer_norm(values):
    centred = values - jnp.mean(values, axis=-1, keepdims=True)
    return centred * lax.rsqrt(jnp.mean(centred * centred, axis=-1, keepdims=True) + eps_norm)


def gelu_tanh(values):
    return (
        0.5
        * values
        * (1.0 + jnp.tanh(0.7978845608028654 * (values + 0.044715 * values * values * values)))
    )


def rope_tables(positions, head_size):
    sixth_part = head_size // 6
    part_spans = (head_size - 4 * sixth_part, 2 * sixth_part, 2 * sixth_part)
    pieces = []
    for axis_no in range(3):
        span_now = part_spans[axis_no]
        inverse = 1.0 / 10000.0 ** (jnp.arange(0, span_now, 2).astype(jnp.float32) / span_now)
        pieces.append(positions[axis_no].astype(jnp.float32)[..., None] * inverse)
    angles = jnp.concatenate(pieces, axis=-1)
    cosine_rep = jnp.repeat(jnp.cos(angles), 2, axis=-1)[..., None, :]
    sine_rep = jnp.repeat(jnp.sin(angles), 2, axis=-1)[..., None, :]
    return (cosine_rep, sine_rep)


def swap_table(head_size):
    row_no = jnp.arange(head_size)[:, None]
    col_no = jnp.arange(head_size)[None, :]
    upward = jnp.where((row_no % 2 == 0) & (col_no == row_no + 1), 1.0, 0.0)
    downward = jnp.where((row_no % 2 == 1) & (col_no == row_no - 1), -1.0, 0.0)
    return (upward + downward).astype(jnp.float32)


def rotate(values, cosine_rep, sine_rep, swap_matrix):
    swapped = jnp.matmul(values, swap_matrix, precision=lax.Precision.HIGHEST)
    return values * cosine_rep + swapped * sine_rep


def tensor_pair(first_term, second_term):
    return lax.psum((first_term, second_term), "tensor")


def stream_sum(partial_out):
    return lax.psum(partial_out, "tensor")


def head_forward(query, keys, values, key_ok, score_scale):
    scores = (
        jnp.einsum("csh,clh->csl", query, keys, preferred_element_type=jnp.float32) * score_scale
    )
    scores = jnp.where(key_ok[:, None, :], scores, -jnp.inf)
    row_peak = jnp.max(scores, axis=-1, keepdims=True)
    exp_terms = jnp.exp(scores - row_peak)
    summed = jnp.sum(exp_terms, axis=-1, keepdims=True)
    probs_low = (exp_terms / summed).astype(jnp.bfloat16)
    attended = jnp.einsum("csl,clh->csh", probs_low, values, preferred_element_type=jnp.float32)
    return (attended, row_peak[..., 0] + jnp.log(summed[..., 0]))


def head_backward(query, keys, values, key_ok, log_total, grad_att, score_scale):
    scores = (
        jnp.einsum("csh,clh->csl", query, keys, preferred_element_type=jnp.float32) * score_scale
    )
    probs = jnp.where(key_ok[:, None, :], jnp.exp(scores - log_total[..., None]), 0.0)
    grad_probs = jnp.einsum("csh,clh->csl", grad_att, values, preferred_element_type=jnp.float32)
    centre = jnp.sum(probs * grad_probs, axis=-1)
    grad_scores = (probs * (grad_probs - centre[..., None])).astype(jnp.bfloat16)
    grad_query = (
        jnp.einsum("csl,clh->csh", grad_scores, keys, preferred_element_type=jnp.float32)
        * score_scale
    )
    grad_keys = (
        jnp.einsum("csl,csh->clh", grad_scores, query, preferred_element_type=jnp.float32)
        * score_scale
    )
    grad_values = jnp.einsum(
        "csl,csh->clh", probs.astype(jnp.bfloat16), grad_att, preferred_element_type=jnp.float32
    )
    return (grad_query, centre, grad_keys, grad_values)


def shards(
    hidden,
    teacher,
    text,
    time_embed,
    lengths,
    positions,
    modulation,
    self_in,
    self_bias,
    self_out,
    norm_gains,
    cross_gain,
    cross_shift,
    cross_q,
    cross_kv,
    cross_bias,
    cross_out,
    ffn_in,
    ffn_in_bias,
    ffn_out,
    out_bias,
):
    low_type = jnp.bfloat16
    wide_type = jnp.float32
    clip_count, seq_rows, model_width = hidden.shape
    local_width = self_in.shape[2]
    local_heads = local_width // HEAD_DIM
    text_local = text.shape[1]
    seq_count = lax.axis_size("seq")
    slot_count = seq_rows * seq_count
    text_count = text_local * seq_count
    flat_rows = clip_count * seq_rows
    score_scale = 1.0 / math.sqrt(HEAD_DIM)
    seq_place = lax.axis_index("seq")
    clip_first = lax.axis_index("dp") * clip_count
    clip_lengths = lax.dynamic_slice_in_dim(lengths, clip_first, clip_count)
    key_valid = jnp.arange(slot_count, dtype=jnp.int32)[None, :] < clip_lengths[:, None]
    row_ids = seq_place * seq_rows + jnp.arange(seq_rows, dtype=jnp.int32)
    row_valid = row_ids[None, :] < clip_lengths[:, None]
    text_valid = jnp.ones((clip_count, text_count), dtype=jnp.bool_)
    valid_total = jnp.sum(lengths).astype(wide_type)
    modulated = modulation[None] + time_embed
    cosine_rep, sine_rep = rope_tables(positions, HEAD_DIM)
    rotate_now = functools.partial(
        rotate, cosine_rep=cosine_rep, sine_rep=sine_rep, swap_matrix=swap_table(HEAD_DIM)
    )
    head_shape = (clip_count, seq_rows, local_heads, HEAD_DIM)
    clip_ids = jnp.arange(flat_rows, dtype=jnp.int32) // seq_rows
    clip_table = (clip_ids[:, None] == jnp.arange(clip_count, dtype=jnp.int32)[None, :]).astype(
        wide_type
    )
    valid_rows = row_valid.reshape(flat_rows)
    hidden_rows = hidden.reshape(flat_rows, model_width)
    teacher_rows = teacher.reshape(flat_rows, model_width)

    def per_row(index_no):
        return jnp.dot(clip_table, modulated[:, index_no], precision=lax.Precision.HIGHEST)

    def per_clip(values):
        return jnp.dot(clip_table.T, values, precision=lax.Precision.HIGHEST)

    scale_one = per_row(1)
    gate_one = per_row(2)
    scale_two = per_row(4)
    gate_two = per_row(5)
    normed_one = layer_norm(hidden_rows)
    attn_in = (normed_one * (1.0 + scale_one) + per_row(0)).astype(low_type)
    projected = (
        jnp.einsum("rd,kde->kre", attn_in, self_in, preferred_element_type=wide_type)
        + self_bias[:, None, :]
    )
    query_pre = projected[0]
    key_pre = projected[1]
    value_pre = projected[2]
    query_sq, key_sq = tensor_pair(
        jnp.sum(query_pre * query_pre, axis=-1), jnp.sum(key_pre * key_pre, axis=-1)
    )
    query_rate = lax.rsqrt(query_sq / model_width + eps_norm)[:, None]
    key_rate = lax.rsqrt(key_sq / model_width + eps_norm)[:, None]
    query_norm = (query_pre * query_rate * norm_gains[0]).reshape(head_shape)
    key_norm = (key_pre * key_rate * norm_gains[1]).reshape(head_shape)
    query_low = rotate_now(query_norm).astype(low_type)
    key_low = rotate_now(key_norm).astype(low_type)
    value_low = value_pre.astype(low_type).reshape(head_shape)
    local_kv = jnp.stack(
        [
            key_low.reshape(clip_count, seq_rows, local_width),
            value_low.reshape(clip_count, seq_rows, local_width),
        ]
    )
    whole_kv = lax.all_gather(local_kv, "seq", axis=2, tiled=True)
    keys_all = whole_kv[0].reshape(clip_count, slot_count, local_heads, HEAD_DIM)
    values_all = whole_kv[1].reshape(clip_count, slot_count, local_heads, HEAD_DIM)
    att_heads = []
    total_heads = []
    for head_no in range(local_heads):
        attended, log_total = head_forward(
            query_low[:, :, head_no],
            keys_all[:, :, head_no],
            values_all[:, :, head_no],
            key_valid,
            score_scale,
        )
        att_heads.append(attended)
        total_heads.append(log_total)
    attn_low = jnp.stack(att_heads, axis=2).astype(low_type).reshape(flat_rows, local_width)
    self_totals = jnp.stack(total_heads)
    branch_one = (
        stream_sum(jnp.dot(attn_low, self_out, preferred_element_type=wide_type)) + out_bias[0]
    )
    after_one = hidden_rows + branch_one * gate_one
    normed_three = layer_norm(after_one)
    cross_in = (normed_three * cross_gain + cross_shift).astype(low_type)
    cross_query_pre = jnp.dot(cross_in, cross_q, preferred_element_type=wide_type) + cross_bias[0]
    text_low = text.astype(low_type)
    text_start = seq_place * text_local
    text_all = lax.all_gather(text_low, "seq", axis=1, tiled=True)
    text_proj = (
        jnp.einsum("ctd,kde->kcte", text_all, cross_kv, preferred_element_type=wide_type)
        + cross_bias[1:, None, None, :]
    )
    cross_sq, text_sq = tensor_pair(
        jnp.sum(cross_query_pre * cross_query_pre, axis=-1),
        jnp.sum(text_proj[0] * text_proj[0], axis=-1),
    )
    text_rate_all = lax.rsqrt(text_sq / model_width + eps_norm)[..., None]
    text_key_low = (text_proj[0] * text_rate_all * norm_gains[3]).astype(low_type)
    text_value_low = text_proj[1].astype(low_type)
    text_key_pre = lax.dynamic_slice_in_dim(text_proj[0], text_start, text_local, 1)
    text_key_rate = lax.dynamic_slice_in_dim(text_rate_all, text_start, text_local, 1)
    cross_rate = lax.rsqrt(cross_sq / model_width + eps_norm)[:, None]
    cross_query_low = (
        (cross_query_pre * cross_rate * norm_gains[2]).astype(low_type).reshape(head_shape)
    )
    text_key_heads = text_key_low.reshape(clip_count, text_count, local_heads, HEAD_DIM)
    text_value_heads = text_value_low.reshape(clip_count, text_count, local_heads, HEAD_DIM)
    cross_heads = []
    cross_total_heads = []
    for head_no in range(local_heads):
        attended, log_total = head_forward(
            cross_query_low[:, :, head_no],
            text_key_heads[:, :, head_no],
            text_value_heads[:, :, head_no],
            text_valid,
            score_scale,
        )
        cross_heads.append(attended)
        cross_total_heads.append(log_total)
    cross_att_low = jnp.stack(cross_heads, axis=2).astype(low_type).reshape(flat_rows, local_width)
    cross_totals = jnp.stack(cross_total_heads)
    branch_two = (
        stream_sum(jnp.dot(cross_att_low, cross_out, preferred_element_type=wide_type))
        + out_bias[1]
    )
    after_two = after_one + branch_two
    normed_two = layer_norm(after_two)
    ffn_input = (normed_two * (1.0 + scale_two) + per_row(3)).astype(low_type)
    pre_act = jnp.dot(ffn_input, ffn_in, preferred_element_type=wide_type) + ffn_in_bias
    act_low = gelu_tanh(pre_act).astype(low_type)
    branch_three = (
        stream_sum(jnp.dot(act_low, ffn_out, preferred_element_type=wide_type)) + out_bias[2]
    )
    result = after_two + branch_three * gate_two
    residue = jnp.where(valid_rows[:, None], result - teacher_rows, 0.0)
    grad_three = residue * gate_two
    grad_three_low = grad_three.astype(low_type)
    grad_ffn_out = jnp.dot(act_low.T, grad_three_low, preferred_element_type=wide_type)
    grad_act = jnp.dot(grad_three_low, ffn_out.T, preferred_element_type=wide_type)
    grad_pre = jax.vjp(gelu_tanh, pre_act)[1](grad_act)[0]
    grad_pre_low = grad_pre.astype(low_type)
    grad_ffn_in = jnp.dot(ffn_input.T, grad_pre_low, preferred_element_type=wide_type)
    grad_ffn_bias = jnp.sum(grad_pre, axis=0)
    grad_ffn_input = stream_sum(jnp.dot(grad_pre_low, ffn_in.T, preferred_element_type=wide_type))
    grad_after_two = (
        residue + jax.vjp(layer_norm, after_two)[1](grad_ffn_input * (1.0 + scale_two))[0]
    )
    grad_two_low = grad_after_two.astype(low_type)
    grad_cross_out = jnp.dot(cross_att_low.T, grad_two_low, preferred_element_type=wide_type)
    grad_cross_att = (
        jnp.dot(grad_two_low, cross_out.T, preferred_element_type=wide_type)
        .astype(low_type)
        .reshape(head_shape)
    )
    cross_query_grads = []
    text_key_grads = []
    text_value_grads = []
    for head_no in range(local_heads):
        head_grads = head_backward(
            cross_query_low[:, :, head_no],
            text_key_heads[:, :, head_no],
            text_value_heads[:, :, head_no],
            text_valid,
            cross_totals[head_no],
            grad_cross_att[:, :, head_no],
            score_scale,
        )
        cross_query_grads.append(head_grads[0])
        text_key_grads.append(head_grads[2])
        text_value_grads.append(head_grads[3])
    grad_cross_query = jnp.stack(cross_query_grads, axis=2).reshape(flat_rows, local_width)
    text_grads_all = jnp.stack(
        [
            jnp.stack(text_key_grads, axis=2).reshape(clip_count, text_count, local_width),
            jnp.stack(text_value_grads, axis=2).reshape(clip_count, text_count, local_width),
        ]
    )
    text_grads = lax.psum_scatter(
        text_grads_all.astype(jnp.bfloat16), "seq", scatter_dimension=2, tiled=True
    ).astype(jnp.float32)
    query_term, key_term = tensor_pair(
        jnp.sum(grad_cross_query * norm_gains[2] * cross_query_pre, axis=-1),
        jnp.sum(text_grads[0] * norm_gains[3] * text_key_pre, axis=-1),
    )
    grad_cross_query_pre = (
        grad_cross_query * norm_gains[2] * cross_rate
        - cross_query_pre * cross_rate**3 * query_term[:, None] / model_width
    )
    grad_text_key_pre = (
        text_grads[0] * norm_gains[3] * text_key_rate
        - text_key_pre * text_key_rate**3 * key_term[..., None] / model_width
    )
    gain_cross_query = jnp.sum(grad_cross_query * cross_query_pre * cross_rate, axis=0)
    gain_text_key = jnp.sum(text_grads[0] * text_key_pre * text_key_rate, axis=(0, 1))
    grad_cross_bias = jnp.stack(
        [
            jnp.sum(grad_cross_query_pre, axis=0),
            jnp.sum(grad_text_key_pre, axis=(0, 1)),
            jnp.sum(text_grads[1], axis=(0, 1)),
        ]
    )
    grad_cross_query_low = grad_cross_query_pre.astype(low_type)
    text_grad_low = jnp.stack([grad_text_key_pre, text_grads[1]]).astype(low_type)
    grad_cross_q = jnp.dot(cross_in.T, grad_cross_query_low, preferred_element_type=wide_type)
    grad_cross_kv = jnp.einsum(
        "ctd,kcte->kde", text_low, text_grad_low, preferred_element_type=wide_type
    )
    grad_text = lax.psum(
        jnp.einsum(
            "kcte,kde->ctd", text_grad_low, cross_kv, preferred_element_type=wide_type
        ).astype(jnp.bfloat16),
        "tensor",
    ).astype(jnp.float32)
    grad_cross_in = stream_sum(
        jnp.dot(grad_cross_query_low, cross_q.T, preferred_element_type=wide_type)
    )
    grad_cross_gain = jnp.sum(grad_cross_in * normed_three, axis=0)
    grad_cross_shift = jnp.sum(grad_cross_in, axis=0)
    grad_after_one = (
        grad_after_two + jax.vjp(layer_norm, after_one)[1](grad_cross_in * cross_gain)[0]
    )
    grad_one = grad_after_one * gate_one
    grad_one_low = grad_one.astype(low_type)
    grad_self_out = jnp.dot(attn_low.T, grad_one_low, preferred_element_type=wide_type)
    grad_attn = (
        jnp.dot(grad_one_low, self_out.T, preferred_element_type=wide_type)
        .astype(low_type)
        .reshape(head_shape)
    )
    query_grads = []
    key_grads = []
    value_grads = []
    for head_no in range(local_heads):
        head_grads = head_backward(
            query_low[:, :, head_no],
            keys_all[:, :, head_no],
            values_all[:, :, head_no],
            key_valid,
            self_totals[head_no],
            grad_attn[:, :, head_no],
            score_scale,
        )
        query_grads.append(head_grads[0])
        key_grads.append(head_grads[2])
        value_grads.append(head_grads[3])
    full_grads = jnp.stack(
        [
            jnp.stack(key_grads, axis=2).reshape(clip_count, slot_count, local_width),
            jnp.stack(value_grads, axis=2).reshape(clip_count, slot_count, local_width),
        ]
    )
    kv_grads = lax.psum_scatter(
        full_grads.astype(jnp.bfloat16), "seq", scatter_dimension=2, tiled=True
    ).astype(jnp.float32)
    rotate_back = jax.vjp(rotate_now, query_norm)[1]
    grad_query_norm = rotate_back(jnp.stack(query_grads, axis=2))[0].reshape(flat_rows, local_width)
    grad_key_norm = rotate_back(kv_grads[0].reshape(head_shape))[0].reshape(flat_rows, local_width)
    query_back, key_back = tensor_pair(
        jnp.sum(grad_query_norm * norm_gains[0] * query_pre, axis=-1),
        jnp.sum(grad_key_norm * norm_gains[1] * key_pre, axis=-1),
    )
    grad_query_pre = (
        grad_query_norm * norm_gains[0] * query_rate
        - query_pre * query_rate**3 * query_back[:, None] / model_width
    )
    grad_key_pre = (
        grad_key_norm * norm_gains[1] * key_rate
        - key_pre * key_rate**3 * key_back[:, None] / model_width
    )
    gain_query = jnp.sum(grad_query_norm * query_pre * query_rate, axis=0)
    gain_key = jnp.sum(grad_key_norm * key_pre * key_rate, axis=0)
    grad_proj = jnp.stack(
        [grad_query_pre, grad_key_pre, kv_grads[1].reshape(flat_rows, local_width)]
    )
    grad_self_bias = jnp.sum(grad_proj, axis=1)
    grad_proj_low = grad_proj.astype(low_type)
    grad_self_in = jnp.einsum(
        "rd,kre->kde", attn_in, grad_proj_low, preferred_element_type=wide_type
    )
    grad_attn_in = stream_sum(
        jnp.einsum("kre,kde->rd", grad_proj_low, self_in, preferred_element_type=wide_type)
    )
    grad_hidden = (
        grad_after_one + jax.vjp(layer_norm, hidden_rows)[1](grad_attn_in * (1.0 + scale_one))[0]
    )
    grad_time_local = jnp.stack(
        [
            per_clip(grad_attn_in),
            per_clip(grad_attn_in * normed_one),
            per_clip(grad_after_one * branch_one),
            per_clip(grad_ffn_input),
            per_clip(grad_ffn_input * normed_two),
            per_clip(residue * branch_three),
        ],
        axis=1,
    )
    grad_out_bias = jnp.stack(
        [jnp.sum(grad_one, axis=0), jnp.sum(grad_after_two, axis=0), jnp.sum(grad_three, axis=0)]
    )
    stream_values = (
        grad_time_local,
        grad_cross_gain,
        grad_cross_shift,
        grad_out_bias,
        jnp.sum(residue * residue),
    )
    grad_time_local, grad_cross_gain, grad_cross_shift, grad_out_bias, square_local = stream_values
    grad_time = lax.psum(grad_time_local.astype(jnp.bfloat16), "seq").astype(jnp.float32)
    grad_norm_gains = jnp.stack([gain_query, gain_key, gain_cross_query, gain_text_key])
    (
        sum_self_bias,
        sum_gains,
        sum_cross_gain,
        sum_cross_shift,
        sum_cross_bias,
        sum_ffn_bias,
        sum_out_bias,
        sum_modulation,
        square_sum,
    ) = (
        lax.psum(grad_self_bias.astype(jnp.bfloat16), ("dp", "seq")).astype(jnp.float32),
        lax.psum(grad_norm_gains.astype(jnp.bfloat16), ("dp", "seq")).astype(jnp.float32),
        lax.psum(grad_cross_gain.astype(jnp.bfloat16), ("dp", "seq")).astype(jnp.float32),
        lax.psum(grad_cross_shift.astype(jnp.bfloat16), ("dp", "seq")).astype(jnp.float32),
        lax.psum(grad_cross_bias.astype(jnp.bfloat16), ("dp", "seq")).astype(jnp.float32),
        lax.psum(grad_ffn_bias.astype(jnp.bfloat16), ("dp", "seq")).astype(jnp.float32),
        lax.psum(grad_out_bias.astype(jnp.bfloat16), ("dp", "seq")).astype(jnp.float32),
        lax.psum(jnp.sum(grad_time_local, axis=0).astype(jnp.bfloat16), ("dp", "seq")).astype(
            jnp.float32
        ),
        lax.psum(square_local.astype(jnp.bfloat16), ("dp", "seq")).astype(jnp.float32),
    )
    loss = square_sum / (valid_total * model_width)
    (
        part_self_in,
        part_self_out,
        part_cross_q,
        part_cross_kv,
        part_cross_out,
        part_ffn_in,
        part_ffn_out,
    ) = (
        lax.psum_scatter(
            grad_self_in.astype(jnp.bfloat16), ("dp", "seq"), scatter_dimension=1, tiled=True
        ).astype(jnp.float32),
        lax.psum_scatter(
            grad_self_out.astype(jnp.bfloat16), ("dp", "seq"), scatter_dimension=1, tiled=True
        ).astype(jnp.float32),
        lax.psum_scatter(
            grad_cross_q.astype(jnp.bfloat16), ("dp", "seq"), scatter_dimension=0, tiled=True
        ).astype(jnp.float32),
        lax.psum_scatter(
            grad_cross_kv.astype(jnp.bfloat16), ("dp", "seq"), scatter_dimension=1, tiled=True
        ).astype(jnp.float32),
        lax.psum_scatter(
            grad_cross_out.astype(jnp.bfloat16), ("dp", "seq"), scatter_dimension=1, tiled=True
        ).astype(jnp.float32),
        lax.psum_scatter(
            grad_ffn_in.astype(jnp.bfloat16), ("dp", "seq"), scatter_dimension=0, tiled=True
        ).astype(jnp.float32),
        lax.psum_scatter(
            grad_ffn_out.astype(jnp.bfloat16), ("dp", "seq"), scatter_dimension=1, tiled=True
        ).astype(jnp.float32),
    )
    result_out = result.reshape(clip_count, seq_rows, model_width)
    grad_hidden_out = grad_hidden.reshape(clip_count, seq_rows, model_width)
    return (
        result_out,
        loss,
        grad_hidden_out,
        grad_text,
        grad_time,
        sum_modulation,
        part_self_in,
        sum_self_bias,
        part_self_out,
        sum_gains,
        sum_cross_gain,
        sum_cross_shift,
        part_cross_q,
        part_cross_kv,
        sum_cross_bias,
        part_cross_out,
        part_ffn_in,
        sum_ffn_bias,
        part_ffn_out,
        sum_out_bias,
    )


def solution(mesh):
    placed = (
        P("dp", "seq", None),
        P("dp", "seq", None),
        P("dp", "seq", None),
        P("dp", None, None),
        P(),
        P(None, "dp", "seq"),
        P(),
        P(None, None, "tensor"),
        P(None, "tensor"),
        P("tensor", None),
        P(None, "tensor"),
        P(),
        P(),
        P(None, "tensor"),
        P(None, None, "tensor"),
        P(None, "tensor"),
        P("tensor", None),
        P(None, "tensor"),
        P("tensor"),
        P("tensor", None),
        P(),
    )
    return jax.shard_map(
        shards,
        mesh=mesh,
        in_specs=placed,
        out_specs=(
            P("dp", "seq", None),
            P(),
            P("dp", "seq", None),
            P("dp", "seq", None),
            P("dp", None, None),
            P(),
            P(None, ("dp", "seq"), "tensor"),
            P(None, "tensor"),
            P("tensor", ("dp", "seq")),
            P(None, "tensor"),
            P(),
            P(),
            P(("dp", "seq"), "tensor"),
            P(None, ("dp", "seq"), "tensor"),
            P(None, "tensor"),
            P("tensor", ("dp", "seq")),
            P(("dp", "seq"), "tensor"),
            P("tensor"),
            P("tensor", ("dp", "seq")),
            P(),
        ),
        check_vma=False,
    )
```

profile of v0, /device:TPU:0, one launch (start us, length us, event | category | flops | bytes accessed | tf_op | source)
XLA Modules:
  0.0 2147.2 jit_solution(10150921818489820520)
XLA Ops:
  9.4 6.4 reduce_sum.488
  46.4 14.5 all-reduce.4
  87.9 42.1 %all-gather.3.cloned.1.call-done = bf16[2,1,3120,384]{3,0,1,2:T(2,128)(2,1)} async-done(((bf16[2,1,780,384]{3,0,1,2:T(2,128)(2,1)}), bf16[2,1,3120,384]{3,0,1,2:T(2,128)(2,1)}) %all-gather.3.cloned.1.call-update) | async-done | bytes 4792336 | tf_op jit(solution)/shard_map/all_gather | solution.py:189
  130.0 11.0 fusion.285
  140.9 10.5 copy.134
  151.4 10.6 copy.132
  164.9 5.8 select_reduce_fusion.2
  170.7 10.3 fusion
  181.1 7.8 fusion.1
  191.4 6.2 fusion.138
  203.1 5.1 fusion.293
  215.9 167.6 %all-reduce.16.cloned.1.call-done = f32[780,1536]{1,0:T(8,128)} async-done(((f32[780,1536]{1,0:T(8,128)}), f32[780,1536]{1,0:T(8,128)}) %all-reduce.16.cloned.1.call-update) | async-done | bytes 4792336 | tf_op jit(solution)/shard_map/psum | solution.py:60
  394.3 10.2 all-reduce.3
  423.5 5.2 fusion.294
  428.9 173.6 %all-reduce.18.cloned.1.call-done = f32[780,1536]{1,0:T(8,128)} async-done(((f32[780,1536]{1,0:T(8,128)}), f32[780,1536]{1,0:T(8,128)}) %all-reduce.18.cloned.1.call-update) | async-done | bytes 4792336 | tf_op jit(solution)/shard_map/psum | solution.py:60
  610.4 9.1 fusion.274
  619.5 10.2 fusion.273
  631.4 172.6 %all-reduce.20.cloned.1.call-done = f32[780,1536]{1,0:T(8,128)} async-done(((f32[780,1536]{1,0:T(8,128)}), f32[780,1536]{1,0:T(8,128)}) %all-reduce.20.cloned.1.call-update) | async-done | bytes 4792336 | tf_op jit(solution)/shard_map/psum | solution.py:60
  804.0 8.4 fusion.25
  812.4 16.9 fusion.292
  831.1 9.4 fusion.95
  844.6 170.1 %all-reduce.22.cloned.1.call-done = f32[780,1536]{1,0:T(8,128)} async-done(((f32[780,1536]{1,0:T(8,128)}), f32[780,1536]{1,0:T(8,128)}) %all-reduce.22.cloned.1.call-update) | async-done | bytes 4792336 | tf_op jit(solution)/shard_map/psum | solution.py:60
  1014.8 5.1 multiply_reduce_fusion.6
  1050.2 10.1 psum.186
  1063.7 4.9 fusion.170
  1085.8 6.8 bitcast_reduce_fusion
  1094.1 148.3 %all-reduce.24.cloned.1.call-done = f32[780,1536]{1,0:T(8,128)} async-done(((f32[780,1536]{1,0:T(8,128)}), f32[780,1536]{1,0:T(8,128)}) %all-reduce.24.cloned.1.call-update) | async-done | bytes 4792336 | tf_op jit(solution)/shard_map/psum | solution.py:60
  1242.5 6.1 multiply_reduce_fusion.3
  1259.6 7.2 fusion.160
  1266.8 6.5 fusion.158
  1284.3 22.2 %multiply_reduce_fusion.2 = (f32[780]{0:T(1024)}, f32[780]{0:T(1024)}, f32[780]{0:T(1024)}, f32[780,3120]{1,0:T(8,128)}) fusion(f32[780,3120]{1,0:T(8,128)} %get-tuple-element.177, f32[780]{0:T(1024)S(1)} %copy-done.85, pred[3120]{0:T(1024)(128)(4,1)S(1)} %copy-done.59, f32[780,3120]{1,0:T(8,128)} %fusion.158, f32[780]{0:T(1024)S(1)} %copy-done.86, ...), kind=kOutput, calls=%fused_computation.13 | convolution fusion | flops 659503296 | bytes 59480720 | tf_op jit(solution)/shard_map/csh,clh->csl/dot_general | solution.py:81
  1306.5 27.8 %multiply_convert_fusion.2 = (bf16[780,3120]{1,0:T(8,128)(2,1)}, bf16[780,3120]{1,0:T(8,128)(2,1)}, bf16[780,3120]{1,0:T(8,128)(2,1)}) fusion(f32[780,3120]{1,0:T(8,128)} %get-tuple-element.193, f32[780,3120]{1,0:T(8,128)} %get-tuple-element.177, f32[780]{0:T(1024)} %get-tuple-element.111, f32[780]{0:T(1024)S(1)} %copy-done.85, ...), kind=kLoop, calls=%fused_computation.12 | loop fusion | flops 43804800 | bytes 73029840 | tf_op jit(solution)/shard_map/convert_element_type | solution.py:83
  1334.3 5.4 fusion.50
  1360.5 5.1 pad_maximum_fusion
  1365.6 14.1 copy.163
  1379.7 5.4 convolution_convert_fusion.4
  1389.9 15.0 convolution_convert_fusion
  1405.6 13.3 convolution_convert_fusion.1
  1448.1 5.4 convolution_convert_fusion.6
  1453.8 38.9 %all-reduce.30.cloned.1.call-done = bf16[2,1,3120,384]{3,0,1,2:T(2,128)(2,1)} async-done(((bf16[2,1,3120,384]{3,0,1,2:T(2,128)(2,1)}), bf16[2,1,3120,384]{3,0,1,2:T(2,128)(2,1)}) %all-reduce.30.cloned.1.call-update) | async-done | bytes 4792336
  1502.1 5.3 multiply_reduce_fusion.15
  1516.3 12.8 all-reduce.2
  1537.6 6.9 copy.177
  1554.7 5.2 convolution_bitcast_fusion
  1563.1 9.5 copy.178
  1572.6 6.5 fusion.91
  1579.2 7.3 fusion.88
  1586.6 6.5 fusion.69
  1593.1 8.1 copy.187
  1601.2 4.9 copy.243
  1617.9 6.5 fusion.85
  1624.4 17.6 reduce-scatter.20.cloned.1.call-done
  1644.5 66.6 %reduce-scatter.18.cloned.1.call-done = bf16[192,2240]{1,0:T(8,128)(2,1)} async-done(((bf16[1536,2240]{1,0:T(8,128)(2,1)}), bf16[192,2240]{1,0:T(8,128)(2,1)}) %reduce-scatter.18.cloned.1.call-update) | async-done | bytes 860176 | tf_op jit(solution)/shard_map/reduce_scatter | solution.py:485
  1713.5 37.3 %reduce-scatter.12.cloned.1.call-done = bf16[384,192]{0,1:T(8,128)(2,1)} async-done(((bf16[384,1536]{0,1:T(8,128)(2,1)}), bf16[384,192]{0,1:T(8,128)(2,1)}) %reduce-scatter.12.cloned.1.call-update) | async-done | bytes 147472 | tf_op jit(solution)/shard_map/reduce_scatter | solution.py:473
  1759.9 30.7 %all-reduce.28.cloned.1.call-done = bf16[1,128,1536]{2,1,0:T(8,128)(2,1)} async-done(((bf16[1,128,1536]{2,1,0:T(8,128)(2,1)}), bf16[1,128,1536]{2,1,0:T(8,128)(2,1)}) %all-reduce.28.cloned.1.call-update) | async-done | bytes 393232 | tf_op jit(solution)/shard_map/psum | solution.py:335
  1792.5 63.9 %all-reduce.32.cloned.1.call-done = bf16[2,1536,384]{2,0,1:T(2,128)(2,1)} async-done(((bf16[2,1536,384]{2,0,1:T(2,128)(2,1)}), bf16[2,1536,384]{2,0,1:T(2,128)(2,1)}) %all-reduce.32.cloned.1.call-update) | async-done | bytes 2359312
  1858.5 174.7 %all-reduce.26.cloned.1.call-done = f32[780,1536]{1,0:T(8,128)} async-done(((f32[780,1536]{1,0:T(8,128)}), f32[780,1536]{1,0:T(8,128)}) %all-reduce.26.cloned.1.call-update) | async-done | bytes 4792336 | tf_op jit(solution)/shard_map/psum | solution.py:60
  2033.2 9.2 fusion.66
  2045.9 5.6 fusion.82
  2054.2 31.3 %all-reduce.5 = (bf16[]{:T(256)}, bf16[6,1536]{1,0:T(8,128)(2,1)}, bf16[3,384]{1,0:T(4,128)(2,1)}, bf16[4,384]{1,0:T(4,128)(2,1)}, bf16[1536]{0:T(1024)(128)(2,1...) all-reduce(bf16[]{:T(256)} %get-tuple-element.83, ...), channel_id=1, replica_groups=mesh['dp'=2,'seq'=4,'tensor'=4] {'dp','seq'}, use_global_device_ids=true, to_apply=%region_30.31 | all-reduce | flops 22977 | bytes 91908 | tf_op jit(solution)/shard_map/psum | solution.py:458
  2086.3 5.4 fusion.277
  2091.7 5.1 add_bitcast_fusion
  2096.8 9.5 copy.179
  2106.3 15.2 psum.194
  (585 shorter events, 344.2 us)
Async XLA Ops:
  7.2 13.3 copy-start
  7.2 122.7 %all-gather.3.cloned.1.call-start = ((), (), s32[]{:S(2)}) async-start(), calls=%async_computation.7 | async-start | bytes 5990400 | tf_op jit(solution)/shard_map/all_gather | solution.py:189
  9.4 11.1 copy-start.137
  15.8 8.2 copy-start.62
  28.2 34.0 %copy-start.104 = (f32[384]{0:T(512)}, f32[384]{0:T(512)S(1)}, u32[]{:S(2)}) copy-start(f32[384]{0:T(512)S(1)} %get-tuple-element.106) | copy-start | bytes 4612
  62.2 11.8 copy-start.99
  62.2 21.6 %copy-start.91 = (f32[780]{0:T(1024)}, f32[780]{0:T(1024)S(1)}, u32[]{:S(2)}) copy-start(f32[780]{0:T(1024)S(1)} %get-tuple-element.202) | copy-start | bytes 9364
  72.0 11.8 copy-start.105
  74.0 136.6 %all-gather.5.cloned.1.call-start = ((), (), s32[]{:S(2)}) async-start(), calls=%async_computation.9 | async-start | bytes 1966080 | tf_op jit(solution)/shard_map/all_gather | solution.py:215
  76.0 307.5 %all-reduce.16.cloned.1.call-start = ((), (), s32[]{:S(2)}) async-start(), calls=%async_computation.8 | async-start | bytes 9633792 | tf_op jit(solution)/shard_map/psum | solution.py:60
  77.9 119.7 %copy-start.58 = (pred[3120]{0:T(1024)(128)(4,1)}, pred[3120]{0:T(1024)(128)(4,1)S(1)}, u32[]{:S(2)}) copy-start(pred[3120]{0:T(1024)(128)(4,1)S(1)} %iota_compare_fusion.2) | copy-start | bytes 9364
  164.9 24.1 %copy-start.1 = (f32[780,3120]{1,0:T(8,128)}, f32[780,3120]{1,0:T(8,128)S(1)}, u32[]{:S(2)}) copy-start(f32[780,3120]{1,0:T(8,128)S(1)} %fusion.159) | copy-start | bytes 29203204
  170.7 26.9 %copy-start.106 = (f32[780]{0:T(1024)}, f32[780]{0:T(1024)S(1)}, u32[]{:S(2)}) copy-start(f32[780]{0:T(1024)S(1)} %get-tuple-element.176) | copy-start | bytes 9364
  181.1 10.3 copy-start.112
  181.1 16.5 copy-start.125
  181.1 7.9 copy-start.20
  189.0 8.6 slice-start.5
  189.0 8.6 slice-start.6
  208.2 394.3 %all-reduce.18.cloned.1.call-start = ((), (), s32[]{:S(2)}) async-start(), calls=%async_computation.10 | async-start | bytes 9633792 | tf_op jit(solution)/shard_map/psum | solution.py:60
  210.5 173.0 %copy-start.64 = (f32[1536]{0:T(1024)}, f32[1536]{0:T(1024)S(1)}, u32[]{:S(2)}) copy-start(f32[1536]{0:T(1024)S(1)} %get-tuple-element.100) | copy-start | bytes 18436
  428.7 375.3 %all-reduce.20.cloned.1.call-start = ((), (), s32[]{:S(2)}) async-start(), calls=%async_computation.11 | async-start | bytes 9633792 | tf_op jit(solution)/shard_map/psum | solution.py:60
  602.5 16.9 slice-start.20
  607.1 12.4 copy-start.3
  607.1 412.8 %copy-start.60 = (f32[780]{0:T(1024)}, f32[780]{0:T(1024)S(1)}, u32[]{:S(2)}) copy-start(f32[780]{0:T(1024)S(1)} %broadcast_multiply_fusion.3) | copy-start | bytes 9364
  607.8 11.7 copy-start.97
  607.8 11.7 copy-start.81
  610.4 9.1 slice-start.21
  610.4 9.1 copy-start.135
  629.7 385.0 %all-reduce.22.cloned.1.call-start = ((), (), s32[]{:S(2)}) async-start(), calls=%async_computation.12 | async-start | bytes 9633792 | tf_op jit(solution)/shard_map/psum | solution.py:60
  804.0 8.4 copy-start.68
  804.0 8.4 copy-start.136
  812.4 16.9 copy-start.5
  840.6 401.9 %all-reduce.24.cloned.1.call-start = ((), (), s32[]{:S(2)}) async-start(), calls=%async_computation.13 | async-start | bytes 9633792 | tf_op jit(solution)/shard_map/psum | solution.py:60
  1014.8 9.5 slice-start.14
  1068.6 353.4 %reduce-scatter.22.cloned.1.call-start = ((), (), s32[]{:S(2)}) async-start(), calls=%async_computation.21 | async-start | bytes 983040
  1068.9 10.2 copy-start.38
  1068.9 10.1 copy-start.44
  1068.9 10.5 copy-start.40
  1068.9 10.8 copy-start.42
  1080.0 162.4 %copy-start.78 = (f32[780]{0:T(1024)S(1)}, f32[780]{0:T(1024)}, u32[]{:S(2)}) copy-start(f32[780]{0:T(1024)} %copy-done.77) | copy-start | bytes 9364
  1093.7 154.9 %copy-start.96 = (f32[780]{0:T(1024)S(1)}, f32[780]{0:T(1024)}, u32[]{:S(2)}) copy-start(f32[780]{0:T(1024)} %copy-done.95) | copy-start | bytes 9364
  1093.7 399.0 %all-reduce.30.cloned.1.call-start = ((), (), s32[]{:S(2)}) async-start(), calls=%async_computation.23 | async-start | bytes 9584640
  1242.5 9.9 slice-start.18
  1259.6 13.7 slice-start
  1259.6 13.7 slice-start.1
  1266.8 10.1 slice-start.11
  1266.8 10.1 slice-start.12
  1379.7 233.7 %reduce-scatter.16.cloned.1.call-start = ((), (), s32[]{:S(2)}) async-start(), calls=%async_computation.18 | async-start | bytes 1327104 | tf_op jit(solution)/shard_map/reduce_scatter | solution.py:482
  1385.2 229.9 %reduce-scatter.14.cloned.1.call-start = ((), (), s32[]{:S(2)}) async-start(), calls=%async_computation.17 | async-start | bytes 1327104 | tf_op jit(solution)/shard_map/reduce_scatter | solution.py:476
  1389.9 252.1 %reduce-scatter.20.cloned.1.call-start = ((), (), s32[]{:S(2)}) async-start(), calls=%async_computation.20 | async-start | bytes 7962624 | tf_op jit(solution)/shard_map/reduce_scatter | solution.py:488
  1404.9 306.1 %reduce-scatter.18.cloned.1.call-start = ((), (), s32[]{:S(2)}) async-start(), calls=%async_computation.19 | async-start | bytes 7962624 | tf_op jit(solution)/shard_map/reduce_scatter | solution.py:485
  1418.9 8.0 copy-start.79
  1418.9 331.9 %reduce-scatter.12.cloned.1.call-start = ((), (), s32[]{:S(2)}) async-start(), calls=%async_computation.16 | async-start | bytes 1327104 | tf_op jit(solution)/shard_map/reduce_scatter | solution.py:473
  1429.2 8.4 slice-start.16
  1453.5 337.0 %all-reduce.28.cloned.1.call-start = ((), (), s32[]{:S(2)}) async-start(), calls=%async_computation.15 | async-start | bytes 786432 | tf_op jit(solution)/shard_map/psum | solution.py:335
  1534.3 322.2 %all-reduce.32.cloned.1.call-start = ((), (), s32[]{:S(2)}) async-start(), calls=%async_computation.24 | async-start | bytes 4718592
  1544.6 488.6 %all-reduce.26.cloned.1.call-start = ((), (), s32[]{:S(2)}) async-start(), calls=%async_computation.14 | async-start | bytes 9633792 | tf_op jit(solution)/shard_map/psum | solution.py:60
  1559.9 572.6 %reduce-scatter.24.cloned.1.call-start = ((), (), s32[]{:S(2)}) async-start(), calls=%async_computation.22 | async-start | bytes 3981312
  1572.6 13.9 slice-start.3
  1624.4 128.7 %copy-start.80 = (f32[384]{0:T(512)S(1)}, f32[384]{0:T(512)}, u32[]{:S(2)}) copy-start(f32[384]{0:T(512)} %get-tuple-element.105) | copy-start | bytes 4612
  2033.2 10.4 copy-start.7
  2045.9 39.7 %copy-start.94 = (f32[780]{0:T(1024)S(1)}, f32[780]{0:T(1024)}, u32[]{:S(2)}) copy-start(f32[780]{0:T(1024)} %copy-done.93) | copy-start | bytes 9364
  2096.8 31.3 %copy-start.126 = (bf16[1536]{0:T(1024)(128)(2,1)S(1)}, bf16[1536]{0:T(1024)(128)(2,1)}, u32[]{:S(2)}) copy-start(bf16[1536]{0:T(1024)(128)(2,1)} %get-tuple-element.131) | copy-start | bytes 9220
  2096.8 34.5 %copy-start.115 = (bf16[3,1536]{1,0:T(4,128)(2,1)S(1)}, bf16[3,1536]{1,0:T(4,128)(2,1)}, u32[]{:S(2)}) copy-start(bf16[3,1536]{1,0:T(4,128)(2,1)} %get-tuple-element.134) | copy-start | bytes 27652
  (120 other events, 475.5 us)
Sparse Core Ops, SparseCore 0:
  74.1 55.8 all-gather.2
  131.8 30.8 all-gather.4
  208.3 175.1 all-reduce.15
  428.8 173.6 all-reduce.17
  629.9 174.0 all-reduce.19
  840.7 174.0 all-reduce.21
  1068.8 173.6 all-reduce.23
  1245.4 25.0 reduce-scatter.21
  1379.8 112.8 all-reduce.29
  1495.7 37.2 reduce-scatter.15
  1536.3 36.6 reduce-scatter.13
  1576.4 65.4 reduce-scatter.19
  1645.5 65.4 reduce-scatter.17
  1714.1 36.6 reduce-scatter.11
  1753.6 36.9 all-reduce.27
  1793.7 62.7 all-reduce.31
  1858.7 174.4 all-reduce.25
  2036.5 48.1 reduce-scatter.23
where the time goes:
time: 2160 us; the launch traced here: 2150 us
  waiting for transfers between devices  1300 us (60%)
  matrix products  305 us (14%)
  local copies, waits for them, and re-layouts  224 us (10%)
  other arithmetic  196 us (9%)
  blocking collectives  94.2 us (4%)
    psum x6, waiting for transfers between devices, stream_sum(): return lax.psum(partial_out, 'tensor')  1010 us
    unnamed x22, waiting for transfers between devices  103 us
    unnamed x351, local copies, waits for them, and re-layouts  79.1 us
    reduce_scatter x1, waiting for transfers between devices, shards(): lax.psum_scatter(grad_ffn_in.astype(jnp.bfloat16), ('dp', 'seq'), scatter...  66.6 us
    psum x4, blocking collectives, tensor_pair(): return lax.psum((first_term, second_term), 'tensor')  47.6 us
  transfers between devices with their start and end apart: 18, of which 13 were waited for; matrix products, arithmetic and copies ran while one was open for 24% of the time, Pallas kernels for 0%

commit v1 on v0

--- a/solution.py
+++ b/solution.py
@@ -57,7 +57,7 @@
 
 
 def stream_sum(partial_out):
-    return lax.psum(partial_out, "tensor")
+    return lax.psum(partial_out.astype(jnp.bfloat16), "tensor").astype(jnp.float32)
 
 
 def head_forward(query, keys, values, key_ok, score_scale):
@@ -370,15 +370,28 @@
         query_grads.append(head_grads[0])
         key_grads.append(head_grads[2])
         value_grads.append(head_grads[3])
-    full_grads = jnp.stack(
+    owner_grads = [
+        jnp.stack(parts, axis=2)
+        .astype(jnp.bfloat16)
+        .reshape(clip_count, seq_count, seq_rows, local_width)
+        for parts in (key_grads, value_grads)
+    ]
+    owner_grads = jnp.concatenate(
         [
-            jnp.stack(key_grads, axis=2).reshape(clip_count, slot_count, local_width),
-            jnp.stack(value_grads, axis=2).reshape(clip_count, slot_count, local_width),
-        ]
-    )
-    kv_grads = lax.psum_scatter(
-        full_grads.astype(jnp.bfloat16), "seq", scatter_dimension=2, tiled=True
-    ).astype(jnp.float32)
+            jnp.swapaxes(part, 0, 1).reshape(seq_count, flat_rows, local_width)
+            for part in owner_grads
+        ],
+        axis=-1,
+    )
+    pad_rows = -flat_rows % 16
+    owner_grads = jnp.pad(owner_grads, ((0, 0), (0, pad_rows), (0, 0)))
+    kv_rows = lax.psum_scatter(
+        owner_grads.reshape(seq_count * (flat_rows + pad_rows), 2 * local_width),
+        "seq",
+        scatter_dimension=0,
+        tiled=True,
+    )[:flat_rows].astype(jnp.float32)
+    kv_grads = (kv_rows[:, :local_width], kv_rows[:, local_width:])
     rotate_back = jax.vjp(rotate_now, query_norm)[1]
     grad_query_norm = rotate_back(jnp.stack(query_grads, axis=2))[0].reshape(flat_rows, local_width)
     grad_key_norm = rotate_back(kv_grads[0].reshape(head_shape))[0].reshape(flat_rows, local_width)
@@ -477,7 +490,10 @@
             grad_cross_q.astype(jnp.bfloat16), ("dp", "seq"), scatter_dimension=0, tiled=True
         ).astype(jnp.float32),
         lax.psum_scatter(
-            grad_cross_kv.astype(jnp.bfloat16), ("dp", "seq"), scatter_dimension=1, tiled=True
+            jnp.concatenate([grad_cross_kv[0], grad_cross_kv[1]], axis=-1).astype(jnp.bfloat16),
+            ("dp", "seq"),
+            scatter_dimension=0,
+            tiled=True,
         ).astype(jnp.float32),
         lax.psum_scatter(
             grad_cross_out.astype(jnp.bfloat16), ("dp", "seq"), scatter_dimension=1, tiled=True
@@ -489,6 +505,7 @@
             grad_ffn_out.astype(jnp.bfloat16), ("dp", "seq"), scatter_dimension=1, tiled=True
         ).astype(jnp.float32),
     )
+    part_cross_kv = jnp.stack([part_cross_kv[:, :local_width], part_cross_kv[:, local_width:]])
     result_out = result.reshape(clip_count, seq_rows, model_width)
     grad_hidden_out = grad_hidden.reshape(clip_count, seq_rows, model_width)
     return (

time: 2160 us -> 1580 us (0.73)
  waiting for transfers between devices: 1300 us -> 696 us
    psum x7 -> x6, waiting for transfers between devices: 1040 us -> 540 us  [stream_sum(): lax.psum(partial_out.astype(jnp.bfloat16), 'tensor').astype(jnp.float32)]
    unnamed x22 -> x20, waiting for transfers between devices: 103 us -> 0.3 us
    reduce_scatter x1, waiting for transfers between devices: 37.3 us -> 0.01 us  [shards(): lax.psum_scatter(grad_self_out.astype(jnp.bfloat16), ('dp', 'seq'), scatt...]
    reduce_scatter x1, waiting for transfers between devices: 17.6 us -> 47 us  [shards(): lax.psum_scatter(grad_ffn_out.astype(jnp.bfloat16), ('dp', 'seq'), scatte...]
    unnamed x351 -> x319, local copies, waits for them, and re-layouts: 79.1 us -> 93 us
  transfers between devices with their start and end apart: 18 -> 17, of which waited for: 13 -> 9; matrix products, arithmetic and copies ran while one was open for 24% -> 35% of each run, Pallas kernels for 0% -> 0%
where the time goes in v1:
time: 1580 us; the launch traced here: 1570 us
  waiting for transfers between devices  696 us (44%)
  matrix products  301 us (19%)
  local copies, waits for them, and re-layouts  236 us (15%)
  other arithmetic  211 us (13%)
  blocking collectives  103 us (7%)
  between operations  18.5 us (1%)
    psum x6, waiting for transfers between devices, stream_sum(): lax.psum(partial_out.astype(jnp.bfloat16), 'tensor').astype(jnp.float32)  540 us
    unnamed x319, local copies, waits for them, and re-layouts  93 us
    reduce_scatter x1, waiting for transfers between devices, shards(): lax.psum_scatter(grad_ffn_in.astype(jnp.bfloat16), ('dp', 'seq'), scatter...  66.4 us
    psum x4, blocking collectives, tensor_pair(): return lax.psum((first_term, second_term), 'tensor')  55.8 us
    reduce_scatter x1, waiting for transfers between devices, shards(): lax.psum_scatter(grad_ffn_out.astype(jnp.bfloat16), ('dp', 'seq'), scatte...  47 us
    all_gather x1, waiting for transfers between devices, shards(): whole_kv = lax.all_gather(local_kv, 'seq', axis=2, tiled=True)  42.1 us
    dot_general x6, matrix products, head_backward(): jnp.einsum('csh,clh->csl', grad_att, values, preferred_element_type=jnp.f...  39.5 us
  transfers between devices with their start and end apart: 17, of which 9 were waited for; matrix products, arithmetic and copies ran while one was open for 35% of the time, Pallas kernels for 0%

profile of v1, /device:TPU:0, one launch (start us, length us, event | category | flops | bytes accessed | tf_op | source)
XLA Modules:
  0.0 1568.1 jit_solution(919943598599520812)
XLA Ops:
  9.4 6.4 reduce_sum.491
  46.6 24.2 %all-reduce.3 = (f32[780]{0:T(1024)}, f32[780]{0:T(1024)}) all-reduce(f32[780]{0:T(1024)} %get-tuple-element.87, f32[780]{0:T(1024)S(1)} %copy-done.100), channel_id=1, replica_groups=mesh['dp'=2,'seq'=4,'tensor'=4] {'tensor'}, use_global_device_ids=true, to_apply=%region_5.6 | all-reduce | flops 1560 | bytes 12480 | tf_op jit(solution)/shard_map/psum | solution.py:56
  97.7 42.1 %all-gather.3.cloned.1.call-done = bf16[2,1,3120,384]{3,0,1,2:T(2,128)(2,1)} async-done(((bf16[2,1,780,384]{3,0,1,2:T(2,128)(2,1)}), bf16[2,1,3120,384]{3,0,1,2:T(2,128)(2,1)}) %all-gather.3.cloned.1.call-update) | async-done | bytes 4792336 | tf_op jit(solution)/shard_map/all_gather | solution.py:189
  139.8 10.9 fusion.276
  150.7 10.5 copy.131
  161.2 10.5 copy.129
  174.6 5.9 select_reduce_fusion.2
  180.5 10.3 fusion
  190.8 7.6 fusion.1
  200.9 6.2 fusion.132
  227.2 86.7 %all-reduce.13.cloned.1.call-done = bf16[780,1536]{1,0:T(8,128)(2,1)} async-done(((bf16[780,1536]{1,0:T(8,128)(2,1)}), bf16[780,1536]{1,0:T(8,128)(2,1)}) %all-reduce.13.cloned.1.call-update) | async-done | bytes 2396176 | tf_op jit(solution)/shard_map/psum | solution.py:60
  324.1 10.5 all-reduce.2
  354.7 4.4 convolution_convert_fusion.6
  359.3 94.9 %all-reduce.15.cloned.1.call-done = bf16[780,1536]{1,0:T(8,128)(2,1)} async-done(((bf16[780,1536]{1,0:T(8,128)(2,1)}), bf16[780,1536]{1,0:T(8,128)(2,1)}) %all-reduce.15.cloned.1.call-update) | async-done | bytes 2396176 | tf_op jit(solution)/shard_map/psum | solution.py:60
  461.5 9.0 fusion.267
  470.6 13.2 convolution_convert_fusion.5
  485.3 94.2 %all-reduce.17.cloned.1.call-done = bf16[780,1536]{1,0:T(8,128)(2,1)} async-done(((bf16[780,1536]{1,0:T(8,128)(2,1)}), bf16[780,1536]{1,0:T(8,128)(2,1)}) %all-reduce.17.cloned.1.call-update) | async-done | bytes 2396176 | tf_op jit(solution)/shard_map/psum | solution.py:60
  579.5 7.6 fusion.31
  587.1 16.9 %fusion.283 = (bf16[2240]{0:T(1024)(128)(2,1)}, bf16[780,2240]{1,0:T(8,128)(2,1)S(1)}) fusion(bf16[2240,1536]{1,0:T(8,128)(2,1)} %param.40, f32[780,1536]{1,0:T(8,128)S(1)} %get-tuple-element.150, f32[1536]{0:T(1024)S(1)} %copy-done.63, f32[780]{0:T(1024)S(1)} %fusion.228, f32[780,2240]{1,0:T(8,128)} %fusion.267, f32[2240]{0:T(1024)S(1)} %copy-done.126), kind=kOutput, calls=%fused_computation.498 | convolution fusion | flops 5416412160 | bytes 22179504 | tf_op jit(solution)/shard_map/dot_general | solution.py:266
  605.8 9.9 convolution_convert_fusion.4
  620.1 91.4 %all-reduce.19.cloned.1.call-done = bf16[780,1536]{1,0:T(8,128)(2,1)} async-done(((bf16[780,1536]{1,0:T(8,128)(2,1)}), bf16[780,1536]{1,0:T(8,128)(2,1)}) %all-reduce.19.cloned.1.call-update) | async-done | bytes 2396176 | tf_op jit(solution)/shard_map/psum | solution.py:60
  711.5 4.5 multiply_reduce_fusion.4
  746.2 10.3 psum.186
  776.2 4.8 copy.180
  781.0 6.8 bitcast_reduce_fusion
  788.9 70.3 %all-reduce.21.cloned.1.call-done = bf16[780,1536]{1,0:T(8,128)(2,1)} async-done(((bf16[780,1536]{1,0:T(8,128)(2,1)}), bf16[780,1536]{1,0:T(8,128)(2,1)}) %all-reduce.21.cloned.1.call-update) | async-done | bytes 2396176 | tf_op jit(solution)/shard_map/psum | solution.py:60
  863.5 5.1 fusion.27
  868.6 5.2 add_add_fusion.3
  880.5 7.3 fusion.154
  887.9 6.5 fusion.152
  905.6 22.2 %multiply_reduce_fusion.2 = (f32[780]{0:T(1024)}, f32[780]{0:T(1024)}, f32[780]{0:T(1024)}, f32[780,3120]{1,0:T(8,128)}) fusion(f32[780,3120]{1,0:T(8,128)} %get-tuple-element.180, f32[780]{0:T(1024)S(1)} %copy-done.82, pred[3120]{0:T(1024)(128)(4,1)S(1)} %copy-done.55, f32[780,3120]{1,0:T(8,128)} %fusion.152, f32[780]{0:T(1024)S(1)} %copy-done.83, ...), kind=kOutput, calls=%fused_computation.13 | convolution fusion | flops 659503296 | bytes 59480720 | tf_op jit(solution)/shard_map/csh,clh->csl/dot_general | solution.py:81
  927.8 27.7 %multiply_convert_fusion.2 = (bf16[780,3120]{1,0:T(8,128)(2,1)}, bf16[780,3120]{1,0:T(8,128)(2,1)}, bf16[780,3120]{1,0:T(8,128)(2,1)}) fusion(f32[780,3120]{1,0:T(8,128)} %get-tuple-element.196, f32[780,3120]{1,0:T(8,128)} %get-tuple-element.180, f32[780]{0:T(1024)} %get-tuple-element.112, f32[780]{0:T(1024)S(1)} %copy-done.82, ...), kind=kLoop, calls=%fused_computation.12 | loop fusion | flops 43804800 | bytes 73029840 | tf_op jit(solution)/shard_map/convert_element_type | solution.py:83
  955.6 5.4 fusion.50
  970.8 7.0 convert_element_type.474
  977.8 4.5 fusion.48
  988.4 6.8 convert_element_type.470
  995.2 8.6 pad_maximum_fusion
  1003.8 10.4 copy.188
  1014.2 4.8 pad.4.clone
  1019.1 5.4 convolution_convert_fusion.9
  1024.8 4.7 convolution_convert_fusion.10
  1029.5 5.6 convolution_convert_fusion.11
  1035.2 15.0 convolution_convert_fusion
  1050.9 13.1 convolution_convert_fusion.1
  1102.9 5.2 multiply_reduce_fusion.13
  1119.7 10.8 all-reduce.1
  1139.5 4.7 bitcast_convert_fusion
  1153.7 9.6 copy.173
  1163.2 6.1 fusion.84
  1172.1 5.3 fusion.88
  1185.4 10.2 fusion.67
  1195.6 8.1 copy.182
  1203.7 5.2 copy.241
  1208.9 6.9 fusion.81
  1217.5 47.0 %reduce-scatter.26.cloned.1.call-done = bf16[2240,192]{0,1:T(8,128)(2,1)} async-done(((bf16[2240,1536]{0,1:T(8,128)(2,1)}), bf16[2240,192]{0,1:T(8,128)(2,1)}) %reduce-scatter.26.cloned.1.call-update) | async-done | bytes 860176 | tf_op jit(solution)/shard_map/reduce_scatter | solution.py:504
  1267.0 66.4 %reduce-scatter.24.cloned.1.call-done = bf16[192,2240]{1,0:T(8,128)(2,1)} async-done(((bf16[1536,2240]{1,0:T(8,128)(2,1)}), bf16[192,2240]{1,0:T(8,128)(2,1)}) %reduce-scatter.24.cloned.1.call-update) | async-done | bytes 860176 | tf_op jit(solution)/shard_map/reduce_scatter | solution.py:501
  1343.8 102.7 %all-reduce.23.cloned.1.call-done = (bf16[780,1536]{1,0:T(8,128)(2,1)}, bf16[1,128,1536]{2,1,0:T(8,128)(2,1)}) async-done(((bf16[780,1536]{1,0:T(8,128)(2,1)}, bf16[1,128,1536]{2,1,0:T(8,128)(2,1)}), (bf16[780,1536]{1,0:T(8,128)(2,1)}, bf16[1,128,1536]{2,1,0:T(8,128)(2,1)})) %all-reduce.23.cloned.1.call-update) | async-done | bytes 2789392 | tf_op jit(solution)/shard_map/psum | solution.py:60
  1446.5 8.4 fusion.62
  1457.1 5.6 fusion.87
  1465.5 30.0 %all-reduce.4 = (bf16[]{:T(256)}, bf16[6,1536]{1,0:T(8,128)(2,1)}, bf16[3,384]{1,0:T(4,128)(2,1)}, bf16[4,384]{1,0:T(4,128)(2,1)}, bf16[1536]{0:T(1024)(128)(2,1...) all-reduce(bf16[]{:T(256)} %get-tuple-element.110, ...), channel_id=1, replica_groups=mesh['dp'=2,'seq'=4,'tensor'=4] {'dp','seq'}, use_global_device_ids=true, to_apply=%region_30.31 | all-reduce | flops 22977 | bytes 91908 | tf_op jit(solution)/shard_map/psum | solution.py:471
  1496.3 4.9 fusion.266
  1501.2 7.1 add_bitcast_fusion
  1508.3 9.6 copy.174
  1517.9 16.8 %psum.194 = bf16[1,6,1536]{2,1,0:T(8,128)(2,1)} all-reduce(bf16[1,6,1536]{2,1,0:T(8,128)(2,1)} %stack.259), channel_id=1, replica_groups=mesh['dp'=2,'seq'=4,'tensor'=4] {'seq'}, use_global_device_ids=true, to_apply=%region_58.59 | all-reduce | flops 9216 | bytes 36864 | tf_op jit(solution)/shard_map/psum | solution.py:448
  (554 shorter events, 343.8 us)
Async XLA Ops:
  7.2 13.3 copy-start
  7.2 132.6 %all-gather.3.cloned.1.call-start = ((), (), s32[]{:S(2)}) async-start(), calls=%async_computation.9 | async-start | bytes 5990400 | tf_op jit(solution)/shard_map/all_gather | solution.py:189
  15.8 8.2 copy-start.56
  20.5 293.4 %copy-start.68 = (f32[1536]{0:T(1024)}, f32[1536]{0:T(1024)S(1)}, u32[]{:S(2)}) copy-start(f32[1536]{0:T(1024)S(1)} %get-tuple-element.95) | copy-start | bytes 18436
  31.0 15.6 copy-start.100
  72.1 11.7 copy-start.94
  83.8 137.1 %all-gather.5.cloned.1.call-start = ((), (), s32[]{:S(2)}) async-start(), calls=%async_computation.11 | async-start | bytes 1966080 | tf_op jit(solution)/shard_map/all_gather | solution.py:215
  85.8 228.1 %all-reduce.13.cloned.1.call-start = ((), (), s32[]{:S(2)}) async-start(), calls=%async_computation.10 | async-start | bytes 4816896 | tf_op jit(solution)/shard_map/psum | solution.py:60
  87.8 119.3 %copy-start.54 = (pred[3120]{0:T(1024)(128)(4,1)}, pred[3120]{0:T(1024)(128)(4,1)S(1)}, u32[]{:S(2)}) copy-start(pred[3120]{0:T(1024)(128)(4,1)S(1)} %iota_compare_fusion.2) | copy-start | bytes 9364
  174.6 23.8 %copy-start.3 = (f32[780,3120]{1,0:T(8,128)}, f32[780,3120]{1,0:T(8,128)S(1)}, u32[]{:S(2)}) copy-start(f32[780,3120]{1,0:T(8,128)S(1)} %fusion.153) | copy-start | bytes 29203204
  180.5 26.6 %copy-start.95 = (f32[780]{0:T(1024)}, f32[780]{0:T(1024)S(1)}, u32[]{:S(2)}) copy-start(f32[780]{0:T(1024)S(1)} %get-tuple-element.179) | copy-start | bytes 9364
  190.8 7.7 copy-start.101
  190.8 10.1 copy-start.102
  190.8 16.3 %copy-start.113 = (f32[780]{0:T(1024)}, f32[780]{0:T(1024)S(1)}, u32[]{:S(2)}) copy-start(f32[780]{0:T(1024)S(1)} %get-tuple-element.115) | copy-start | bytes 9364
  190.8 7.7 copy-start.22
  198.5 8.6 slice-start.3
  198.5 8.6 slice-start.4
  217.0 237.2 %all-reduce.15.cloned.1.call-start = ((), (), s32[]{:S(2)}) async-start(), calls=%async_computation.12 | async-start | bytes 4816896 | tf_op jit(solution)/shard_map/psum | solution.py:60
  359.1 220.4 %all-reduce.17.cloned.1.call-start = ((), (), s32[]{:S(2)}) async-start(), calls=%async_computation.13 | async-start | bytes 4816896 | tf_op jit(solution)/shard_map/psum | solution.py:60
  454.2 16.3 %slice-start.16 = ((s8[6881280]{0:T(1024)(128)(4,1)}), s8[4194304]{0:T(1024)(128)(4,1)S(1)}, s32[]{:S(2)}) async-start(s8[6881280]{0:T(1024)(128)(4,1)} %bitcast.611), calls=%async_computation.42 | async-start | bytes 8388608
  458.2 12.3 copy-start.4
  458.3 12.3 copy-start.60
  458.9 11.6 copy-start.92
  458.9 11.6 copy-start.85
  461.5 9.1 slice-start.17
  461.5 9.1 copy-start.125
  483.8 227.7 %all-reduce.19.cloned.1.call-start = ((), (), s32[]{:S(2)}) async-start(), calls=%async_computation.14 | async-start | bytes 4816896 | tf_op jit(solution)/shard_map/psum | solution.py:60
  579.5 7.6 copy-start.63
  579.5 7.6 copy-start.126
  587.1 16.9 %copy-start.5 = (f32[780,1536]{1,0:T(8,128)}, f32[780,1536]{1,0:T(8,128)S(1)}, u32[]{:S(2)}) copy-start(f32[780,1536]{1,0:T(8,128)S(1)} %get-tuple-element.150) | copy-start | bytes 14376964
  615.8 243.5 %all-reduce.21.cloned.1.call-start = ((), (), s32[]{:S(2)}) async-start(), calls=%async_computation.15 | async-start | bytes 4816896 | tf_op jit(solution)/shard_map/psum | solution.py:60
  711.5 8.9 slice-start.12
  764.1 301.5 %reduce-scatter.28.cloned.1.call-start = ((), (), s32[]{:S(2)}) async-start(), calls=%async_computation.22 | async-start | bytes 983040
  764.3 9.9 copy-start.36
  764.3 9.9 copy-start.42
  764.3 10.2 copy-start.38
  764.3 10.5 copy-start.40
  788.9 305.4 %reduce-scatter.16.cloned.1.call-start = ((), (), s32[]{:S(2)}) async-start(), calls=%async_computation.16 | async-start | bytes 6021120 | tf_op jit(solution)/shard_map/reduce_scatter | solution.py:388
  868.6 7.4 copy-start.69
  868.6 7.4 copy-start.124
  880.5 7.4 copy-start.23
  880.5 7.4 copy-start.41
  880.5 13.9 slice-start
  880.5 13.9 slice-start.1
  887.9 10.1 slice-start.9
  887.9 10.1 slice-start.10
  1019.0 159.1 %reduce-scatter.22.cloned.1.call-start = ((), (), s32[]{:S(2)}) async-start(), calls=%async_computation.19 | async-start | bytes 1327104 | tf_op jit(solution)/shard_map/reduce_scatter | solution.py:498
  1024.5 155.3 %reduce-scatter.20.cloned.1.call-start = ((), (), s32[]{:S(2)}) async-start(), calls=%async_computation.18 | async-start | bytes 1327104 | tf_op jit(solution)/shard_map/reduce_scatter | solution.py:489
  1029.5 186.4 %reduce-scatter.18.cloned.1.call-start = ((), (), s32[]{:S(2)}) async-start(), calls=%async_computation.17 | async-start | bytes 1327104 | tf_op jit(solution)/shard_map/reduce_scatter | solution.py:486
  1035.1 229.4 %reduce-scatter.26.cloned.1.call-start = ((), (), s32[]{:S(2)}) async-start(), calls=%async_computation.21 | async-start | bytes 7962624 | tf_op jit(solution)/shard_map/reduce_scatter | solution.py:504
  1050.2 283.3 %reduce-scatter.24.cloned.1.call-start = ((), (), s32[]{:S(2)}) async-start(), calls=%async_computation.20 | async-start | bytes 7962624 | tf_op jit(solution)/shard_map/reduce_scatter | solution.py:501
  1063.9 382.5 %all-reduce.23.cloned.1.call-start = ((), (), s32[]{:S(2)}) async-start(), calls=%async_computation.25 | async-start | bytes 5603328 | tf_op jit(solution)/shard_map/psum | solution.py:60
  1072.8 8.3 slice-start.14
  1131.6 7.9 copy-start.26
  1144.3 403.4 %reduce-scatter.32.cloned.1.call-start = ((), (), s32[]{:S(2)}) async-start(), calls=%async_computation.24 | async-start | bytes 2654208
  1152.3 401.5 %reduce-scatter.30.cloned.1.call-start = ((), (), s32[]{:S(2)}) async-start(), calls=%async_computation.23 | async-start | bytes 3981312
  1163.2 7.9 copy-start.15
  1163.2 8.9 copy-start.87
  1172.1 13.3 copy-start.57
  1208.9 127.6 %copy-start.78 = (f32[384]{0:T(512)S(1)}, f32[384]{0:T(512)}, u32[]{:S(2)}) copy-start(f32[384]{0:T(512)} %get-tuple-element.104) | copy-start | bytes 4612
  1446.5 9.6 copy-start.7
  1446.5 10.6 copy-start.74
  1508.3 32.9 %copy-start.114 = (bf16[1536]{0:T(1024)(128)(2,1)S(1)}, bf16[1536]{0:T(1024)(128)(2,1)}, u32[]{:S(2)}) copy-start(bf16[1536]{0:T(1024)(128)(2,1)} %get-tuple-element.132) | copy-start | bytes 9220
  1508.3 36.1 %copy-start.105 = (bf16[3,1536]{1,0:T(4,128)(2,1)S(1)}, bf16[3,1536]{1,0:T(4,128)(2,1)}, u32[]{:S(2)}) copy-start(bf16[3,1536]{1,0:T(4,128)(2,1)} %get-tuple-element.135) | copy-start | bytes 27652
  (103 other events, 378.8 us)
Sparse Core Ops, SparseCore 0:
  83.9 55.8 all-gather.2
  141.7 30.8 all-gather.4
  217.1 96.7 all-reduce.12
  359.2 94.9 all-reduce.14
  483.9 95.5 all-reduce.16
  615.9 95.5 all-reduce.18
  764.2 94.9 all-reduce.20
  862.1 25.0 reduce-scatter.27
  1019.2 56.6 reduce-scatter.15
  1079.0 36.6 reduce-scatter.21
  1118.9 36.6 reduce-scatter.19
  1158.7 36.7 reduce-scatter.17
  1199.0 65.4 reduce-scatter.25
  1267.9 65.4 reduce-scatter.23
  1336.3 110.1 all-reduce.22
  1449.7 42.7 reduce-scatter.31
  1495.8 48.6 reduce-scatter.29

commit v2 on v1

--- a/solution.py
+++ b/solution.py
@@ -4,9 +4,13 @@
 import jax
 import jax.numpy as jnp
 from jax import lax
+from jax.experimental import pallas as pl
+from jax.experimental.pallas import tpu as pltpu
 from jax.sharding import PartitionSpec as P
 
 HEAD_DIM = 128
+LOW = jnp.bfloat16
+WIDE = jnp.float32
 
 
 eps_norm = 1e-06
@@ -52,12 +56,210 @@
     return values * cosine_rep + swapped * sine_rep
 
 
-def tensor_pair(first_term, second_term):
-    return lax.psum((first_term, second_term), "tensor")
-
-
-def stream_sum(partial_out):
-    return lax.psum(partial_out.astype(jnp.bfloat16), "tensor").astype(jnp.float32)
+def line_kernel(count, block, group, lag, lag2, turned, *refs):
+    lhs_refs = refs[:count]
+    rhs_refs = refs[count:2 * count]
+    out_ref, raw, part, stage, cross, raw_s, raw_r, mid_s, mid_r, far_s, far_r, near_s, near_r = refs[2 * count:]
+    steps = out_ref.shape[0] // block
+    me = lax.axis_index("tensor")
+    inner = (me == 1) | (me == 2)
+    outer = jnp.logical_not(inner)
+    leaf = jnp.where(me < 2, 0, 3)
+    hub = jnp.where(me < 2, 1, 2)
+    mate = 3 - me
+    side = jnp.where(me < 2, 0, 1)
+
+    def signal(where):
+        pl.semaphore_signal(
+            pltpu.get_barrier_semaphore(), inc=1, device_id={"tensor": where},
+            device_id_type=pl.DeviceIdType.MESH)
+
+    @pl.when(outer)
+    def _():
+        signal(hub)
+        pl.semaphore_wait(pltpu.get_barrier_semaphore(), 1)
+
+    @pl.when(inner)
+    def _():
+        signal(leaf)
+        signal(mate)
+        pl.semaphore_wait(pltpu.get_barrier_semaphore(), 2)
+
+    def rows_of(step):
+        return pl.ds(pl.multiple_of(step * block, 16), block)
+
+    def remote(src, dst, send, recv, step, where):
+        at = rows_of(step)
+        return pltpu.make_async_remote_copy(
+            src_ref=src.at[at], dst_ref=dst.at[at], send_sem=send.at[step], recv_sem=recv.at[step],
+            device_id={"tensor": where}, device_id_type=pl.DeviceIdType.MESH)
+
+    def raw_copy(step):
+        return remote(raw, raw, raw_s, raw_r, step, hub)
+
+    def mid_copy(step):
+        return remote(stage, cross, mid_s, mid_r, step, mate)
+
+    def far_copy(step):
+        return remote(out_ref, out_ref, far_s, far_r, step, mate)
+
+    def near_copy(step):
+        return remote(out_ref, out_ref, near_s, near_r, step, leaf)
+
+    def body(step, carry):
+        @pl.when((step < steps) & (lax.rem(step, group) == 0))
+        def _():
+            at = pl.ds(pl.multiple_of(step * block, 16), block * group)
+            total = None
+            for lhs, rhs in zip(lhs_refs, rhs_refs):
+                term = lax.dot_general(lhs[at], rhs[...], (((1,), (1 if turned else 0,)), ((), ())),
+                    preferred_element_type=WIDE)
+                total = term if total is None else total + term
+            part[at] = total
+
+        @pl.when(outer & (step < steps))
+        def _():
+            at = rows_of(step)
+            raw[at] = part[at].astype(LOW)
+            raw_copy(step).start()
+
+        late = step - lag2
+        @pl.when(inner & (late >= 0) & (late < steps) & (lax.rem(late + 2 * lag2, 2) != side))
+        def _():
+            far_copy(late).wait_recv()
+            near_copy(late).start()
+
+        near = step - lag
+        @pl.when(inner & (near >= 0) & (near < steps) & (lax.rem(near + 2 * lag2, 2) == side))
+        def _():
+            at = rows_of(near)
+            mid_copy(near).wait_recv()
+            out_ref[at] = (part[at] + cross[at].astype(WIDE)).astype(LOW)
+            far_copy(near).start()
+            near_copy(near).start()
+
+        @pl.when(inner & (step < steps))
+        def _():
+            at = rows_of(step)
+            raw_copy(step).wait_recv()
+
+            @pl.when(lax.rem(step, 2) == side)
+            def _():
+                part[at] = part[at] + raw[at].astype(WIDE)
+
+            @pl.when(lax.rem(step, 2) != side)
+            def _():
+                stage[at] = (part[at] + raw[at].astype(WIDE)).astype(LOW)
+                mid_copy(step).start()
+
+        return carry
+
+    lax.fori_loop(0, steps + lag2, body, 0)
+
+    def drain(step, carry):
+        @pl.when(outer)
+        def _():
+            near_copy(step).wait_recv()
+            raw_copy(step).wait_send()
+
+        @pl.when(inner)
+        def _():
+            near_copy(step).wait_send()
+
+            @pl.when(lax.rem(step, 2) == side)
+            def _():
+                far_copy(step).wait_send()
+
+            @pl.when(lax.rem(step, 2) != side)
+            def _():
+                mid_copy(step).wait_send()
+
+        return carry
+
+    lax.fori_loop(0, steps, drain, 0)
+
+def line_sum(pairs, turned, ident, block=32, group=5, lag=3, lag2=6):
+    true_rows = pairs[0][0].shape[0]
+    width = pairs[0][1].shape[0 if turned else 1]
+    unit = block * group
+    rows = -(-true_rows // unit) * unit
+    pairs = [(jnp.pad(lhs, ((0, rows - true_rows), (0, 0))), rhs) for lhs, rhs in pairs]
+    steps = rows // block
+    dma = pltpu.SemaphoreType.DMA
+    depth = sum(p[0].shape[1] for p in pairs)
+    return pl.pallas_call(
+        functools.partial(line_kernel, len(pairs), block, group, lag, lag2, turned),
+        out_shape=jax.ShapeDtypeStruct((rows, width), LOW),
+        in_specs=[pl.BlockSpec(memory_space=pltpu.VMEM)] * (2 * len(pairs)),
+        out_specs=pl.BlockSpec(memory_space=pltpu.VMEM),
+        scratch_shapes=[
+            pltpu.VMEM((rows, width), LOW),
+            pltpu.VMEM((rows, width), WIDE),
+            pltpu.VMEM((rows, width), LOW),
+            pltpu.VMEM((rows, width), LOW),
+        ] + [dma((steps,))] * 8,
+        compiler_params=pltpu.CompilerParams(collective_id=ident, has_side_effects=True, vmem_limit_bytes=60 << 20),
+        cost_estimate=pl.CostEstimate(flops=2 * rows * width * depth, bytes_accessed=2*(rows*depth+width*depth+rows*width), transcendentals=0),
+        name=f"line_sum_{ident}",
+    )(*[p[0] for p in pairs], *[p[1] for p in pairs])[:true_rows].astype(WIDE)
+
+def small_kernel(value_ref, out_ref, slots, send_sem, recv_sem):
+    count = slots.shape[0]
+    me = lax.axis_index("tensor")
+    barrier = pltpu.get_barrier_semaphore()
+    for hop in range(1, count):
+        pl.semaphore_signal(
+            barrier, inc=1, device_id={"tensor": lax.rem(me + hop, count)},
+            device_id_type=pl.DeviceIdType.MESH)
+    pl.semaphore_wait(barrier, count - 1)
+    copies = []
+    for hop in range(1, count):
+        copy = pltpu.make_async_remote_copy(
+            src_ref=value_ref, dst_ref=slots.at[me], send_sem=send_sem.at[hop - 1],
+            recv_sem=recv_sem.at[hop - 1], device_id={"tensor": lax.rem(me + hop, count)},
+            device_id_type=pl.DeviceIdType.MESH)
+        copy.start()
+        copies.append(copy)
+    slots[pl.ds(me, 1)] = value_ref[...][None]
+    for hop in range(1, count):
+        origin = lax.rem(me + count - hop, count)
+        pltpu.make_async_remote_copy(
+            src_ref=value_ref, dst_ref=slots.at[origin], send_sem=send_sem.at[hop - 1],
+            recv_sem=recv_sem.at[hop - 1], device_id={"tensor": origin},
+            device_id_type=pl.DeviceIdType.MESH).wait_recv()
+    for copy in copies:
+        copy.wait_send()
+    total = slots[0]
+    for slot in range(1, count):
+        total = total + slots[slot]
+    out_ref[...] = total
+
+
+def small_sum(values, ident):
+    count = lax.axis_size("tensor")
+    flat = jnp.concatenate([value.reshape(-1) for value in values])
+    size = flat.shape[0]
+    lines = -(-size // 1024) * 8
+    packed = jnp.pad(flat, (0, lines * 128 - size)).reshape(lines, 128)
+    summed = pl.pallas_call(
+        small_kernel,
+        out_shape=jax.ShapeDtypeStruct((lines, 128), WIDE),
+        in_specs=[pl.BlockSpec(memory_space=pltpu.VMEM)],
+        out_specs=pl.BlockSpec(memory_space=pltpu.VMEM),
+        scratch_shapes=[
+            pltpu.VMEM((count, lines, 128), WIDE),
+            pltpu.SemaphoreType.DMA((count - 1,)),
+            pltpu.SemaphoreType.DMA((count - 1,)),
+        ],
+        compiler_params=pltpu.CompilerParams(collective_id=ident, has_side_effects=True),
+        name=f"small_sum_{ident}",
+    )(packed).reshape(-1)
+    outs = []
+    start = 0
+    for value in values:
+        outs.append(summed[start : start + value.size].reshape(value.shape))
+        start += value.size
+    return outs
 
 
 def head_forward(query, keys, values, key_ok, score_scale):
@@ -170,8 +372,8 @@
     query_pre = projected[0]
     key_pre = projected[1]
     value_pre = projected[2]
-    query_sq, key_sq = tensor_pair(
-        jnp.sum(query_pre * query_pre, axis=-1), jnp.sum(key_pre * key_pre, axis=-1)
+    query_sq, key_sq = small_sum(
+        [jnp.sum(query_pre * query_pre, axis=-1), jnp.sum(key_pre * key_pre, axis=-1)], 6
     )
     query_rate = lax.rsqrt(query_sq / model_width + eps_norm)[:, None]
     key_rate = lax.rsqrt(key_sq / model_width + eps_norm)[:, None]
@@ -204,7 +406,7 @@
     attn_low = jnp.stack(att_heads, axis=2).astype(low_type).reshape(flat_rows, local_width)
     self_totals = jnp.stack(total_heads)
     branch_one = (
-        stream_sum(jnp.dot(attn_low, self_out, preferred_element_type=wide_type)) + out_bias[0]
+        line_sum([(attn_low, self_out)], False, 0) + out_bias[0]
     )
     after_one = hidden_rows + branch_one * gate_one
     normed_three = layer_norm(after_one)
@@ -217,9 +419,12 @@
         jnp.einsum("ctd,kde->kcte", text_all, cross_kv, preferred_element_type=wide_type)
         + cross_bias[1:, None, None, :]
     )
-    cross_sq, text_sq = tensor_pair(
-        jnp.sum(cross_query_pre * cross_query_pre, axis=-1),
-        jnp.sum(text_proj[0] * text_proj[0], axis=-1),
+    cross_sq, text_sq = small_sum(
+        [
+            jnp.sum(cross_query_pre * cross_query_pre, axis=-1),
+            jnp.sum(text_proj[0] * text_proj[0], axis=-1),
+        ],
+        7,
     )
     text_rate_all = lax.rsqrt(text_sq / model_width + eps_norm)[..., None]
     text_key_low = (text_proj[0] * text_rate_all * norm_gains[3]).astype(low_type)
@@ -247,7 +452,7 @@
     cross_att_low = jnp.stack(cross_heads, axis=2).astype(low_type).reshape(flat_rows, local_width)
     cross_totals = jnp.stack(cross_total_heads)
     branch_two = (
-        stream_sum(jnp.dot(cross_att_low, cross_out, preferred_element_type=wide_type))
+        line_sum([(cross_att_low, cross_out)], False, 1)
         + out_bias[1]
     )
     after_two = after_one + branch_two
@@ -256,7 +461,7 @@
     pre_act = jnp.dot(ffn_input, ffn_in, preferred_element_type=wide_type) + ffn_in_bias
     act_low = gelu_tanh(pre_act).astype(low_type)
     branch_three = (
-        stream_sum(jnp.dot(act_low, ffn_out, preferred_element_type=wide_type)) + out_bias[2]
+        line_sum([(act_low, ffn_out)], False, 2) + out_bias[2]
     )
     result = after_two + branch_three * gate_two
     residue = jnp.where(valid_rows[:, None], result - teacher_rows, 0.0)
@@ -268,7 +473,7 @@
     grad_pre_low = grad_pre.astype(low_type)
     grad_ffn_in = jnp.dot(ffn_input.T, grad_pre_low, preferred_element_type=wide_type)
     grad_ffn_bias = jnp.sum(grad_pre, axis=0)
-    grad_ffn_input = stream_sum(jnp.dot(grad_pre_low, ffn_in.T, preferred_element_type=wide_type))
+    grad_ffn_input = line_sum([(grad_pre_low, ffn_in)], True, 3)
     grad_after_two = (
         residue + jax.vjp(layer_norm, after_two)[1](grad_ffn_input * (1.0 + scale_two))[0]
     )
@@ -305,9 +510,12 @@
     text_grads = lax.psum_scatter(
         text_grads_all.astype(jnp.bfloat16), "seq", scatter_dimension=2, tiled=True
     ).astype(jnp.float32)
-    query_term, key_term = tensor_pair(
-        jnp.sum(grad_cross_query * norm_gains[2] * cross_query_pre, axis=-1),
-        jnp.sum(text_grads[0] * norm_gains[3] * text_key_pre, axis=-1),
+    query_term, key_term = small_sum(
+        [
+            jnp.sum(grad_cross_query * norm_gains[2] * cross_query_pre, axis=-1),
+            jnp.sum(text_grads[0] * norm_gains[3] * text_key_pre, axis=-1),
+        ],
+        8,
     )
     grad_cross_query_pre = (
         grad_cross_query * norm_gains[2] * cross_rate
@@ -338,9 +546,7 @@
         ).astype(jnp.bfloat16),
         "tensor",
     ).astype(jnp.float32)
-    grad_cross_in = stream_sum(
-        jnp.dot(grad_cross_query_low, cross_q.T, preferred_element_type=wide_type)
-    )
+    grad_cross_in = line_sum([(grad_cross_query_low, cross_q)], True, 4)
     grad_cross_gain = jnp.sum(grad_cross_in * normed_three, axis=0)
     grad_cross_shift = jnp.sum(grad_cross_in, axis=0)
     grad_after_one = (
@@ -395,9 +601,12 @@
     rotate_back = jax.vjp(rotate_now, query_norm)[1]
     grad_query_norm = rotate_back(jnp.stack(query_grads, axis=2))[0].reshape(flat_rows, local_width)
     grad_key_norm = rotate_back(kv_grads[0].reshape(head_shape))[0].reshape(flat_rows, local_width)
-    query_back, key_back = tensor_pair(
-        jnp.sum(grad_query_norm * norm_gains[0] * query_pre, axis=-1),
-        jnp.sum(grad_key_norm * norm_gains[1] * key_pre, axis=-1),
+    query_back, key_back = small_sum(
+        [
+            jnp.sum(grad_query_norm * norm_gains[0] * query_pre, axis=-1),
+            jnp.sum(grad_key_norm * norm_gains[1] * key_pre, axis=-1),
+        ],
+        9,
     )
     grad_query_pre = (
         grad_query_norm * norm_gains[0] * query_rate
@@ -417,9 +626,7 @@
     grad_self_in = jnp.einsum(
         "rd,kre->kde", attn_in, grad_proj_low, preferred_element_type=wide_type
     )
-    grad_attn_in = stream_sum(
-        jnp.einsum("kre,kde->rd", grad_proj_low, self_in, preferred_element_type=wide_type)
-    )
+    grad_attn_in = line_sum([(grad_proj_low[j], self_in[j]) for j in range(3)], True, 5)
     grad_hidden = (
         grad_after_one + jax.vjp(layer_norm, hidden_rows)[1](grad_attn_in * (1.0 + scale_one))[0]
     )

time: 1580 us -> 1470 us (0.930)
  Pallas kernels: 0 us -> 469 us
  waiting for transfers between devices: 696 us -> 263 us
  matrix products: 301 us -> 235 us
  blocking collectives: 103 us -> 43.2 us
  other arithmetic: 211 us -> 181 us
    psum x6 -> x1, waiting for transfers between devices: 540 us -> 0.01 us  [shards(): lax.psum(jnp.einsum('kcte,kde->ctd', text_grad_low, cross_kv, preferred_e...]
    pallas_call x0 -> x10, Pallas kernels: none -> 469 us  [the longest x6 440 us: line_sum(): pl.pallas_call(functools.partial(line_kernel, len(pairs), block, group, l...]
    unnamed x20 -> x15, waiting for transfers between devices: 0.3 us -> 58.3 us
    psum x4 -> x0, blocking collectives: 55.8 us -> none  [tensor_pair(): return lax.psum((first_term, second_term), 'tensor')]
    dot_general x6 -> x0, matrix products: 40.7 us -> none  [the longest x1 13.2 us: shards(): jnp.dot(act_low, ffn_out, preferred_element_type=wide_type)]
    reduce_scatter x1, waiting for transfers between devices: 0.01 us -> 38.3 us  [shards(): lax.psum_scatter(grad_self_out.astype(jnp.bfloat16), ('dp', 'seq'), scatt...]
    reduce_scatter x1, waiting for transfers between devices: 47 us -> 66.5 us  [shards(): lax.psum_scatter(grad_ffn_out.astype(jnp.bfloat16), ('dp', 'seq'), scatte...]
    unnamed x319 -> x420, local copies, waits for them, and re-layouts: 93 us -> 97.3 us
  transfers between devices with their start and end apart: 17 -> 12, of which waited for: 9 -> 7; matrix products, arithmetic and copies ran while one was open for 35% -> 21% of each run, Pallas kernels for 0% -> 6%
where the time goes in v2:
time: 1470 us; the launch traced here: 1460 us
  Pallas kernels  469 us (32%)
  waiting for transfers between devices  263 us (18%)
  local copies, waits for them, and re-layouts  246 us (17%)
  matrix products  235 us (16%)
  other arithmetic  181 us (12%)
  blocking collectives  43.2 us (3%)
  between operations  19.8 us (1%)
    pallas_call x6, Pallas kernels, line_sum(): pl.pallas_call(functools.partial(line_kernel, len(pairs), block, group, l...  440 us
    unnamed x420, local copies, waits for them, and re-layouts  97.3 us
    reduce_scatter x1, waiting for transfers between devices, shards(): lax.psum_scatter(grad_ffn_in.astype(jnp.bfloat16), ('dp', 'seq'), scatter...  66.5 us
    reduce_scatter x1, waiting for transfers between devices, shards(): lax.psum_scatter(grad_ffn_out.astype(jnp.bfloat16), ('dp', 'seq'), scatte...  66.5 us
    unnamed x15, waiting for transfers between devices  58.3 us
    dot_general x6, matrix products, head_backward(): jnp.einsum('csh,clh->csl', grad_att, values, preferred_element_type=jnp.f...  38.3 us
    reduce_scatter x1, waiting for transfers between devices, shards(): lax.psum_scatter(grad_self_out.astype(jnp.bfloat16), ('dp', 'seq'), scatt...  38.3 us
    all_gather x1, waiting for transfers between devices, shards(): whole_kv = lax.all_gather(local_kv, 'seq', axis=2, tiled=True)  33.5 us
  transfers between devices with their start and end apart: 12, of which 7 were waited for; matrix products, arithmetic and copies ran while one was open for 21% of the time, Pallas kernels for 6%

profile of v2, /device:TPU:0, one launch (start us, length us, event | category | flops | bytes accessed | tf_op | source)
XLA Modules:
  0.0 1458.5 jit_solution(16666789429666700313)
XLA Ops:
  9.5 6.4 reduce_sum.426
  21.5 8.7 add_bitcast_fusion.1
  37.1 8.8 small_sum_6.1
  74.9 9.8 copy.153.refs_1_
  94.6 33.5 %all-gather.3.cloned.1.call-done = bf16[2,1,3120,384]{3,0,1,2:T(2,128)(2,1)} async-done(((bf16[2,1,780,384]{3,0,1,2:T(2,128)(2,1)}), bf16[2,1,3120,384]{3,0,1,2:T(2,128)(2,1)}) %all-gather.3.cloned.1.call-update) | async-done | bytes 4792336 | tf_op jit(solution)/shard_map/all_gather | solution.py:391
  128.0 10.9 fusion.289
  139.0 10.5 copy.138
  149.5 10.5 copy.136
  166.5 9.0 fusion
  175.5 7.9 fusion.1
  185.8 6.1 fusion.136
  199.6 73.4 %line_sum_0.1 = bf16[800,1536]{1,0:T(8,128)(2,1)} custom-call(bf16[800,384]{1,0:T(8,128)(2,1)} %pad.46.refs_0_, bf16[384,1536]{1,0:T(8,128)(2,1)} %refs_1_.5), custom_call_target="tpu_custom_call" | custom-call | flops 943718400 | bytes 4251648 | tf_op jit(solution)/shard_map/line_sum_0/pallas_call | solution.py:190
  284.1 6.8 small_sum_7.1
  313.8 71.1 %line_sum_1.1 = bf16[800,1536]{1,0:T(8,128)(2,1)} custom-call(bf16[800,384]{1,0:T(8,128)(2,1)} %pad.48.refs_0_, bf16[384,1536]{1,0:T(8,128)(2,1)} %refs_1_.6), custom_call_target="tpu_custom_call" | custom-call | flops 943718400 | bytes 4251648 | tf_op jit(solution)/shard_map/line_sum_1/pallas_call | solution.py:190
  390.4 10.2 multiply_convert_fusion.3
  404.5 73.2 %line_sum_2.1 = bf16[800,1536]{1,0:T(8,128)(2,1)} custom-call(bf16[800,2240]{1,0:T(8,128)(2,1)} %pad.49.refs_0_, bf16[2240,1536]{1,0:T(8,128)(2,1)} %refs_1_.7), custom_call_target="tpu_custom_call" | custom-call | flops 5505024000 | bytes 12922880 | tf_op jit(solution)/shard_map/line_sum_2/pallas_call | solution.py:190
  477.8 6.8 fusion.31
  484.6 16.9 %fusion.288 = (bf16[2240]{0:T(1024)(128)(2,1)}, bf16[780,2240]{1,0:T(8,128)(2,1)S(1)}) fusion(bf16[2240,1536]{1,0:T(8,128)(2,1)} %refs_1_.7, f32[780,1536]{1,0:T(8,128)S(1)} %get-tuple-element.143, f32[1536]{0:T(1024)S(1)} %copy-done.71, f32[780]{0:T(1024)S(1)} %get-tuple-element.212, f32[780,2240]{1,0:T(8,128)} %get-tuple-element.194, ...), kind=kOutput, calls=%fused_computation.512 | convolution fusion | flops 5416412160 | bytes 22179504 | tf_op jit(solution)/shard_map/dot_general | solution.py:471
  505.4 74.0 %line_sum_3.1 = bf16[800,1536]{1,0:T(8,128)(2,1)} custom-call(bf16[800,2240]{1,0:T(8,128)(2,1)} %pad.50.refs_0_, bf16[1536,2240]{1,0:T(8,128)(2,1)} %copy.153.refs_1_), custom_call_target="tpu_custom_call" | custom-call | flops 5505024000 | bytes 12922880 | tf_op jit(solution)/shard_map/line_sum_3/pallas_call | solution.py:190
  579.4 4.5 multiply_reduce_fusion.4
  584.1 4.2 fusion.284
  605.5 4.9 copy.190
  610.4 6.8 bitcast_reduce_fusion
  631.3 14.0 reduce-scatter.28.cloned.1.call-done
  650.2 6.9 small_sum_8.1
  661.4 72.0 %line_sum_4.1 = bf16[800,1536]{1,0:T(8,128)(2,1)} custom-call(bf16[800,384]{1,0:T(8,128)(2,1)} %pad.52.refs_0_, bf16[1536,384]{1,0:T(8,128)(2,1)} %refs_1_.8), custom_call_target="tpu_custom_call" | custom-call | flops 943718400 | bytes 4251648 | tf_op jit(solution)/shard_map/line_sum_4/pallas_call | solution.py:190
  733.5 4.2 fusion.25
  737.7 4.9 fusion.27
  753.3 6.7 fusion.158
  760.1 6.6 fusion.156
  776.9 4.3 copy.169
  781.2 6.8 convert_element_type.472
  788.0 21.8 %multiply_reduce_fusion.2 = (f32[780]{0:T(1024)S(1)}, f32[780]{0:T(1024)S(1)}, f32[780]{0:T(1024)S(1)}, f32[780,3120]{1,0:T(8,128)}) fusion(f32[780,3120]{1,0:T(8,128)} %copy-done.4, f32[780]{0:T(1024)S(1)} %log_add_fusion.2, pred[3120]{0:T(1024)(128)(4,1)S(1)} %copy-done.62, f32[780,3120]{1,0:T(8,128)} %fusion.156, f32[780]{0:T(1024)S(1)} %log_add_fusion.1, ...), kind=kOutput, calls=%fused_computation.13 | convolution fusion | flops 659503296 | bytes 60980816 | tf_op jit(solution)/shard_map/csh,clh->csl/dot_general | solution.py:283
  809.9 27.8 %multiply_convert_fusion.2 = (bf16[780,3120]{1,0:T(8,128)(2,1)}, bf16[780,3120]{1,0:T(8,128)(2,1)}, bf16[780,3120]{1,0:T(8,128)(2,1)}) fusion(f32[780,3120]{1,0:T(8,128)} %get-tuple-element.202, f32[780,3120]{1,0:T(8,128)} %copy-done.4, f32[780]{0:T(1024)S(1)} %get-tuple-element.112, f32[780]{0:T(1024)S(1)} %log_add_fusion.2, ...), kind=kLoop, calls=%fused_computation.12 | loop fusion | flops 43804800 | bytes 73029840 | tf_op jit(solution)/shard_map/convert_element_type | solution.py:285
  837.6 4.5 fusion.50
  848.2 4.4 copy.168
  852.6 6.9 convert_element_type.468
  859.5 8.7 pad_maximum_fusion
  868.2 10.7 copy.198
  878.9 4.8 pad.53.clone
  883.8 5.4 convolution_convert_fusion.4
  894.6 4.6 convolution_convert_fusion.5
  899.3 5.5 convolution_convert_fusion.6
  908.3 4.3 copy.194
  912.7 12.7 convolution_convert_fusion
  926.1 13.0 convolution_convert_fusion.1
  945.1 9.6 copy.183
  958.7 6.0 fusion.84
  991.1 5.9 fusion.81
  1005.6 4.9 multiply_reduce_fusion.13
  1022.3 6.8 small_sum_9.1
  1036.9 6.1 fusion.67
  1043.0 8.2 copy.192
  1051.2 4.8 copy.251
  1061.8 38.3 %reduce-scatter.18.cloned.1.call-done = bf16[384,192]{0,1:T(8,128)(2,1)} async-done(((bf16[384,1536]{0,1:T(8,128)(2,1)}), bf16[384,192]{0,1:T(8,128)(2,1)}) %reduce-scatter.18.cloned.1.call-update) | async-done | bytes 147472 | tf_op jit(solution)/shard_map/reduce_scatter | solution.py:693
  1101.8 44.1 %reduce-scatter.32.cloned.1.call-done = bf16[192,768]{1,0:T(8,128)(2,1)} async-done(((bf16[1536,768]{1,0:T(8,128)(2,1)}), bf16[192,768]{1,0:T(8,128)(2,1)}) %reduce-scatter.32.cloned.1.call-update) | async-done | bytes 294928
  1148.2 66.5 %reduce-scatter.26.cloned.1.call-done = bf16[2240,192]{0,1:T(8,128)(2,1)} async-done(((bf16[2240,1536]{0,1:T(8,128)(2,1)}), bf16[2240,192]{0,1:T(8,128)(2,1)}) %reduce-scatter.26.cloned.1.call-update) | async-done | bytes 860176 | tf_op jit(solution)/shard_map/reduce_scatter | solution.py:711
  1217.2 66.5 %reduce-scatter.24.cloned.1.call-done = bf16[192,2240]{1,0:T(8,128)(2,1)} async-done(((bf16[1536,2240]{1,0:T(8,128)(2,1)}), bf16[192,2240]{1,0:T(8,128)(2,1)}) %reduce-scatter.24.cloned.1.call-update) | async-done | bytes 860176 | tf_op jit(solution)/shard_map/reduce_scatter | solution.py:708
  1290.6 75.9 %line_sum_5.1 = bf16[800,1536]{1,0:T(8,128)(2,1)} custom-call(bf16[800,384]{1,0:T(8,128)(2,1)} %pad.55.refs_0_, bf16[800,384]{1,0:T(8,128)(2,1)} %pad.56.refs_1_, bf16[800,384]{1,0:T(8,128)(2,1)} %pad.57.refs_2_, bf16[1536,384]{1,0:T(8,128)(2,1)} %get-tuple-element.154.refs_3_, bf16[1536,384]{1,0:T(8,128)(2,1)} %get-tuple-element.155.refs_4_, ...), custom_call_target="tpu_custom_call" | custom-call | flops 2831155200 | bytes 7839744 | tf_op jit(solution)/shard_map/line_sum_5/pallas_call | solution.py:190
  1366.5 8.4 fusion.62
  1380.3 28.5 %all-reduce.13 = (bf16[]{:T(256)}, bf16[6,1536]{1,0:T(8,128)(2,1)S(1)}, bf16[3,384]{1,0:T(4,128)(2,1)S(1)}, bf16[4,384]{1,0:T(4,128)(2,1)S(1)}, bf16[1536]{0:T(1...) all-reduce(bf16[]{:T(256)} %get-tuple-element.110, ...), channel_id=1, replica_groups=mesh['dp'=2,'seq'=4,'tensor'=4] {'dp','seq'}, use_global_device_ids=true, to_apply=%region_23.24 | all-reduce | flops 22977 | bytes 91908 | tf_op jit(solution)/shard_map/psum | solution.py:678
  1408.8 14.7 %psum.79 = bf16[1,6,1536]{2,1,0:T(8,128)(2,1)S(1)} all-reduce(bf16[1,6,1536]{2,1,0:T(8,128)(2,1)S(1)} %stack.259), channel_id=1, replica_groups=mesh['dp'=2,'seq'=4,'tensor'=4] {'seq'}, use_global_device_ids=true, to_apply=%region_44.45 | all-reduce | flops 9216 | bytes 36864 | tf_op jit(solution)/shard_map/psum | solution.py:655
  1428.9 5.0 fusion.281
  1436.9 9.5 copy.184
  (662 shorter events, 292.6 us)
Async XLA Ops:
  7.2 82.8 %copy-start = (bf16[2,1536,384]{2,1,0:T(8,128)(2,1)S(1)}, bf16[2,1536,384]{2,1,0:T(8,128)(2,1)}, u32[]{:S(2)}) copy-start(bf16[2,1536,384]{2,1,0:T(8,128)(2,1)} %param.35) | copy-start | bytes 7077892
  7.2 82.7 %all-gather.5.cloned.1.call-start = ((), (), s32[]{:S(2)}) async-start(), calls=%async_computation.10 | async-start | bytes 1966080 | tf_op jit(solution)/shard_map/all_gather | solution.py:417
  9.4 118.7 %all-gather.3.cloned.1.call-start = ((), (), s32[]{:S(2)}) async-start(), calls=%async_computation.9 | async-start | bytes 5990400 | tf_op jit(solution)/shard_map/all_gather | solution.py:391
  15.9 14.3 copy-start.69
  19.7 253.4 %copy-start.80 = (f32[1536]{0:T(1024)}, f32[1536]{0:T(1024)S(1)}, u32[]{:S(2)}) copy-start(f32[1536]{0:T(1024)S(1)} %get-tuple-element.95) | copy-start | bytes 18436
  19.7 564.3 %copy-start.74 = (f32[1536]{0:T(1024)}, f32[1536]{0:T(1024)S(1)}, u32[]{:S(2)}) copy-start(f32[1536]{0:T(1024)S(1)} %get-tuple-element.92) | copy-start | bytes 18436
  21.5 562.5 %copy-start.56 = (f32[780]{0:T(1024)}, f32[780]{0:T(1024)S(1)}, u32[]{:S(2)}) copy-start(f32[780]{0:T(1024)S(1)} %get-tuple-element.212) | copy-start | bytes 9364
  31.9 54.1 %copy-start.33 = (f32[780,128]{1,0:T(8,128)}, f32[780,128]{1,0:T(8,128)S(1)}, u32[]{:S(2)}) copy-start(f32[780,128]{1,0:T(8,128)S(1)} %copy.129) | copy-start | bytes 1198084
  34.3 51.7 %copy-start.35 = (f32[780,128]{1,0:T(8,128)}, f32[780,128]{1,0:T(8,128)S(1)}, u32[]{:S(2)}) copy-start(f32[780,128]{1,0:T(8,128)S(1)} %copy.130) | copy-start | bytes 1198084
  54.8 31.3 %copy-start.161 = (pred[128]{0:T(512)(128)(4,1)}, pred[128]{0:T(512)(128)(4,1)S(1)}, u32[]{:S(2)}) copy-start(pred[128]{0:T(512)(128)(4,1)S(1)} %get-tuple-element.209) | copy-start | bytes 388
  54.8 31.3 %copy-start.163 = (pred[128]{0:T(512)(128)(4,1)}, pred[128]{0:T(512)(128)(4,1)S(1)}, u32[]{:S(2)}) copy-start(pred[128]{0:T(512)(128)(4,1)S(1)} %get-tuple-element.210) | copy-start | bytes 388
  54.8 31.2 %copy-start.165 = (s32[128]{0:T(128)}, s32[128]{0:T(128)S(1)}, u32[]{:S(2)}) copy-start(s32[128]{0:T(128)S(1)} %get-tuple-element.207) | copy-start | bytes 1540
  54.8 31.2 %copy-start.167 = (s32[128]{0:T(128)}, s32[128]{0:T(128)S(1)}, u32[]{:S(2)}) copy-start(s32[128]{0:T(128)S(1)} %get-tuple-element.208) | copy-start | bytes 1540
  55.5 30.6 %copy-start.120 = (f32[384]{0:T(512)}, f32[384]{0:T(512)S(1)}, u32[]{:S(2)}) copy-start(f32[384]{0:T(512)S(1)} %get-tuple-element.106) | copy-start | bytes 4612
  55.5 243.2 %copy-start.93 = (f32[384]{0:T(512)}, f32[384]{0:T(512)S(1)}, u32[]{:S(2)}) copy-start(f32[384]{0:T(512)S(1)} %get-tuple-element.104) | copy-start | bytes 4612
  56.1 29.9 %copy-start.100 = (f32[780]{0:T(1024)}, f32[780]{0:T(1024)S(1)}, u32[]{:S(2)}) copy-start(f32[780]{0:T(1024)S(1)} %get-tuple-element.172) | copy-start | bytes 9364
  69.2 576.1 %reduce-scatter.28.cloned.1.call-start = ((), (), s32[]{:S(2)}) async-start(), calls=%async_computation.18 | async-start | bytes 983040
  85.3 106.6 %copy-start.61 = (pred[3120]{0:T(1024)(128)(4,1)}, pred[3120]{0:T(1024)(128)(4,1)S(1)}, u32[]{:S(2)}) copy-start(pred[3120]{0:T(1024)(128)(4,1)S(1)} %iota_compare_fusion.2) | copy-start | bytes 9364
  86.0 187.0 %copy-start.83 = (f32[1536]{0:T(1024)}, f32[1536]{0:T(1024)S(1)}, u32[]{:S(2)}) copy-start(f32[1536]{0:T(1024)S(1)} %get-tuple-element.99) | copy-start | bytes 18436
  162.7 20.7 %copy-start.2 = (f32[780,3120]{1,0:T(8,128)}, f32[780,3120]{1,0:T(8,128)S(1)}, u32[]{:S(2)}) copy-start(f32[780,3120]{1,0:T(8,128)S(1)} %fusion.157) | copy-start | bytes 29203204
  166.5 25.4 %copy-start.4 = (f32[780,3120]{1,0:T(8,128)}, f32[780,3120]{1,0:T(8,128)S(1)}, u32[]{:S(2)}) copy-start(f32[780,3120]{1,0:T(8,128)S(1)} %get-tuple-element.183) | copy-start | bytes 29203204
  166.5 25.4 %copy-start.122 = (f32[780]{0:T(1024)}, f32[780]{0:T(1024)S(1)}, u32[]{:S(2)}) copy-start(f32[780]{0:T(1024)S(1)} %get-tuple-element.182) | copy-start | bytes 9364
  175.5 16.5 %copy-start.156 = (f32[780]{0:T(1024)}, f32[780]{0:T(1024)S(1)}, u32[]{:S(2)}) copy-start(f32[780]{0:T(1024)S(1)} %get-tuple-element.115) | copy-start | bytes 9364
  196.6 80.7 %copy-start.43 = (bf16[1,780,3,128]{1,3,2,0:T(8,128)(2,1)}, bf16[1,780,3,128]{1,3,2,0:T(8,128)(2,1)S(1)}, u32[]{:S(2)}) copy-start(bf16[1,780,3,128]{1,3,2,0:T(8,128)(2,1)S(1)} %copy.144) | copy-start | bytes 1797124
  280.9 17.8 %copy-start.26 = (f32[1,1,512,384]{2,3,0,1:T(8,128)S(1)}, f32[1,1,512,384]{2,3,0,1:T(8,128)}, u32[]{:S(2)}) copy-start(f32[1,1,512,384]{2,3,0,1:T(8,128)} %get-tuple-element.163) | copy-start | bytes 2359300
  304.8 295.3 %copy-start.86 = (f32[780]{0:T(1024)}, f32[780]{0:T(1024)S(1)}, u32[]{:S(2)}) copy-start(f32[780]{0:T(1024)S(1)} %log_add_fusion.4) | copy-start | bytes 9364
  308.4 76.5 %copy-start.110 = (f32[1536]{0:T(1024)S(1)}, f32[1536]{0:T(1024)}, u32[]{:S(2)}) copy-start(f32[1536]{0:T(1024)} %get-tuple-element.100) | copy-start | bytes 18436
  310.7 78.2 %copy-start.45 = (bf16[1,780,3,128]{1,3,2,0:T(8,128)(2,1)}, bf16[1,780,3,128]{1,3,2,0:T(8,128)(2,1)S(1)}, u32[]{:S(2)}) copy-start(bf16[1,780,3,128]{1,3,2,0:T(8,128)(2,1)S(1)} %copy.151) | copy-start | bytes 1797124
  389.0 195.1 %copy-start.67 = (f32[780]{0:T(1024)}, f32[780]{0:T(1024)S(1)}, u32[]{:S(2)}) copy-start(f32[780]{0:T(1024)S(1)} %broadcast_multiply_fusion.3) | copy-start | bytes 9364
  389.6 194.4 %copy-start.98 = (f32[780]{0:T(1024)}, f32[780]{0:T(1024)S(1)}, u32[]{:S(2)}) copy-start(f32[780]{0:T(1024)S(1)} %fusion.239) | copy-start | bytes 9364
  404.5 73.2 %copy-start.71 = (f32[1536]{0:T(1024)S(1)}, f32[1536]{0:T(1024)}, u32[]{:S(2)}) copy-start(f32[1536]{0:T(1024)} %get-tuple-element.93) | copy-start | bytes 18436
  404.5 73.2 %copy-start.76 = (f32[1536]{0:T(1024)S(1)}, f32[1536]{0:T(1024)}, u32[]{:S(2)}) copy-start(f32[1536]{0:T(1024)} %get-tuple-element.98) | copy-start | bytes 18436
  404.5 73.2 %copy-start.155 = (pred[780]{0:T(1024)(128)(4,1)S(1)}, pred[780]{0:T(1024)(128)(4,1)}, u32[]{:S(2)}) copy-start(pred[780]{0:T(1024)(128)(4,1)} %get-tuple-element.211) | copy-start | bytes 2344
  484.6 16.9 %copy-start.5 = (f32[780,1536]{1,0:T(8,128)}, f32[780,1536]{1,0:T(8,128)S(1)}, u32[]{:S(2)}) copy-start(f32[780,1536]{1,0:T(8,128)S(1)} %get-tuple-element.143) | copy-start | bytes 14376964
  604.5 13.8 copy-start.39
  618.3 378.7 %reduce-scatter.16.cloned.1.call-start = ((), (), s32[]{:S(2)}) async-start(), calls=%async_computation.11 | async-start | bytes 6021120 | tf_op jit(solution)/shard_map/reduce_scatter | solution.py:594
  622.9 26.5 %copy-start.27 = (f32[1,1,512,384]{2,3,0,1:T(8,128)S(1)}, f32[1,1,512,384]{2,3,0,1:T(8,128)}, u32[]{:S(2)}) copy-start(f32[1,1,512,384]{2,3,0,1:T(8,128)} %get-tuple-element.163) | copy-start | bytes 2359300
  622.9 26.5 %copy-start.94 = (f32[384]{0:T(512)S(1)}, f32[384]{0:T(512)}, u32[]{:S(2)}) copy-start(f32[384]{0:T(512)} %copy-done.93) | copy-start | bytes 4612
  622.9 34.2 %copy-start.124 = (f32[780]{0:T(1024)S(1)}, f32[780]{0:T(1024)}, u32[]{:S(2)}) copy-start(f32[780]{0:T(1024)} %get-tuple-element.175) | copy-start | bytes 9364
  648.6 84.9 %copy-start.64 = (f32[780]{0:T(1024)S(1)}, f32[780]{0:T(1024)}, u32[]{:S(2)}) copy-start(f32[780]{0:T(1024)} %copy-done.63) | copy-start | bytes 9364
  648.6 84.9 %copy-start.66 = (f32[1536]{0:T(1024)S(1)}, f32[1536]{0:T(1024)}, u32[]{:S(2)}) copy-start(f32[1536]{0:T(1024)} %param.32) | copy-start | bytes 18436
  660.5 82.1 %slice-start = ((s8[4816896]{0:T(1024)(128)(4,1)}), s8[622592]{0:T(1024)(128)(4,1)S(1)}, s32[]{:S(2)}) async-start(s8[4816896]{0:T(1024)(128)(4,1)} %bitcast.535), calls=%async_computation.21 | async-start | bytes 1245184
  661.4 76.3 %copy-start.106 = (f32[780]{0:T(1024)S(1)}, f32[780]{0:T(1024)}, u32[]{:S(2)}) copy-start(f32[780]{0:T(1024)} %copy-done.105) | copy-start | bytes 9364
  661.4 76.3 %copy-start.92 = (f32[780]{0:T(1024)S(1)}, f32[780]{0:T(1024)}, u32[]{:S(2)}) copy-start(f32[780]{0:T(1024)} %copy-done.91) | copy-start | bytes 9364
  883.8 172.5 %reduce-scatter.22.cloned.1.call-start = ((), (), s32[]{:S(2)}) async-start(), calls=%async_computation.15 | async-start | bytes 1327104 | tf_op jit(solution)/shard_map/reduce_scatter | solution.py:705
  889.2 168.7 %all-reduce.16.cloned.1.call-start = ((), (), s32[]{:S(2)}) async-start(), calls=%async_computation.12 | async-start | bytes 786432 | tf_op jit(solution)/shard_map/psum | solution.py:543
  894.5 165.7 %reduce-scatter.20.cloned.1.call-start = ((), (), s32[]{:S(2)}) async-start(), calls=%async_computation.14 | async-start | bytes 1327104 | tf_op jit(solution)/shard_map/reduce_scatter | solution.py:696
  899.2 200.9 %reduce-scatter.18.cloned.1.call-start = ((), (), s32[]{:S(2)}) async-start(), calls=%async_computation.13 | async-start | bytes 1327104 | tf_op jit(solution)/shard_map/reduce_scatter | solution.py:693
  904.9 241.0 %reduce-scatter.32.cloned.1.call-start = ((), (), s32[]{:S(2)}) async-start(), calls=%async_computation.20 | async-start | bytes 2654208
  912.7 302.1 %reduce-scatter.26.cloned.1.call-start = ((), (), s32[]{:S(2)}) async-start(), calls=%async_computation.17 | async-start | bytes 7962624 | tf_op jit(solution)/shard_map/reduce_scatter | solution.py:711
  925.5 358.3 %reduce-scatter.24.cloned.1.call-start = ((), (), s32[]{:S(2)}) async-start(), calls=%async_computation.16 | async-start | bytes 7962624 | tf_op jit(solution)/shard_map/reduce_scatter | solution.py:708
  939.2 508.0 %reduce-scatter.30.cloned.1.call-start = ((), (), s32[]{:S(2)}) async-start(), calls=%async_computation.19 | async-start | bytes 3981312
  941.1 23.6 %copy-start.59 = (pred[780,1]{0,1:T(4,128)(4,1)}, pred[780,1]{0,1:T(4,128)(4,1)S(1)}, u32[]{:S(2)}) copy-start(pred[780,1]{0,1:T(4,128)(4,1)S(1)} %reshape.1882) | copy-start | bytes 2344
  945.1 19.6 %slice-start.5 = ((s8[4816896]{0:T(1024)(128)(4,1)}), s8[622592]{0:T(1024)(128)(4,1)S(1)}, s32[]{:S(2)}) async-start(s8[4816896]{0:T(1024)(128)(4,1)} %bitcast.539), calls=%async_computation.26 | async-start | bytes 1245184
  1013.3 16.7 %copy-start.102 = (f32[780]{0:T(1024)S(1)}, f32[780]{0:T(1024)}, u32[]{:S(2)}) copy-start(f32[780]{0:T(1024)} %copy-done.100) | copy-start | bytes 9364
  1013.3 16.7 %copy-start.109 = (f32[780]{0:T(1024)S(1)}, f32[780]{0:T(1024)}, u32[]{:S(2)}) copy-start(f32[780]{0:T(1024)} %copy-done.108) | copy-start | bytes 9364
  1013.3 16.7 %copy-start.126 = (f32[780]{0:T(1024)S(1)}, f32[780]{0:T(1024)}, u32[]{:S(2)}) copy-start(f32[780]{0:T(1024)} %get-tuple-element.169) | copy-start | bytes 9364
  1013.3 16.7 %copy-start.127 = (f32[780]{0:T(1024)S(1)}, f32[780]{0:T(1024)}, u32[]{:S(2)}) copy-start(f32[780]{0:T(1024)} %get-tuple-element.170) | copy-start | bytes 9364
  1147.0 139.2 %copy-start.158 = (bf16[3,128]{1,0:T(4,128)(2,1)S(1)}, bf16[3,128]{1,0:T(4,128)(2,1)}, u32[]{:S(2)}) copy-start(bf16[3,128]{1,0:T(4,128)(2,1)} %get-tuple-element.203) | copy-start | bytes 2308
  1290.6 75.9 %copy-start.73 = (f32[1536]{0:T(1024)S(1)}, f32[1536]{0:T(1024)}, u32[]{:S(2)}) copy-start(f32[1536]{0:T(1024)} %get-tuple-element.93) | copy-start | bytes 18436
  1290.6 75.9 %copy-start.82 = (f32[1536]{0:T(1024)S(1)}, f32[1536]{0:T(1024)}, u32[]{:S(2)}) copy-start(f32[1536]{0:T(1024)} %copy-done.80) | copy-start | bytes 18436
  1290.6 84.8 %slice-start.9 = ((s8[4792320]{0:T(1024)(128)(4,1)}), s8[598016]{0:T(1024)(128)(4,1)S(1)}, s32[]{:S(2)}) async-start(s8[4792320]{0:T(1024)(128)(4,1)} %bitcast.543), calls=%async_computation.30 | async-start | bytes 1196032
  1375.5 53.4 %copy-start.104 = (f32[780]{0:T(1024)S(1)}, f32[780]{0:T(1024)}, u32[]{:S(2)}) copy-start(f32[780]{0:T(1024)} %copy-done.103) | copy-start | bytes 9364
  1375.5 58.5 %slice-start.19 = ((s8[4816896]{0:T(1024)(128)(4,1)}), s8[622592]{0:T(1024)(128)(4,1)S(1)}, s32[]{:S(2)}) async-start(s8[4816896]{0:T(1024)(128)(4,1)} %bitcast.551), calls=%async_computation.40 | async-start | bytes 1245184
  (148 other events, 802.8 us)
Sparse Core Ops, SparseCore 0:
  9.9 33.5 all-gather.4
  69.3 58.6 all-gather.2
  618.4 26.8 reduce-scatter.27
  883.9 57.0 reduce-scatter.15
  944.1 36.6 reduce-scatter.21
  983.5 36.9 all-reduce.15
  1023.7 36.4 reduce-scatter.19
  1063.4 36.6 reduce-scatter.17
  1103.5 42.3 reduce-scatter.31
  1149.2 65.4 reduce-scatter.25
  1218.3 65.4 reduce-scatter.23
  1287.1 47.9 reduce-scatter.29

commit v3 on v2

--- a/solution.py
+++ b/solution.py
@@ -199,9 +199,90 @@
             pltpu.VMEM((rows, width), LOW),
         ] + [dma((steps,))] * 8,
         compiler_params=pltpu.CompilerParams(collective_id=ident, has_side_effects=True, vmem_limit_bytes=60 << 20),
-        cost_estimate=pl.CostEstimate(flops=2 * rows * width * depth, bytes_accessed=2*(rows*depth+width*depth+rows*width), transcendentals=0),
+        cost_estimate=pl.CostEstimate(flops=2 * rows * width * depth, bytes_accessed=230 * 10**6, transcendentals=0),
         name=f"line_sum_{ident}",
     )(*[p[0] for p in pairs], *[p[1] for p in pairs])[:true_rows].astype(WIDE)
+
+def scatter_rows(mix, dimension):
+    return lax.psum_scatter(mix, ("dp", "seq"), scatter_dimension=dimension, tiled=True)
+
+
+def plane_sum_kernel(seq_count, value_ref, seq_ref, all_ref, slots, send_sem, recv_sem):
+    count = slots.shape[0]
+    dp = lax.axis_index("dp")
+    me = dp * seq_count + lax.axis_index("seq")
+
+    def device(place):
+        return {"dp": place // seq_count, "seq": lax.rem(place, seq_count)}
+
+    barrier = pltpu.get_barrier_semaphore()
+    for hop in range(1, count):
+        pl.semaphore_signal(
+            barrier, inc=1, device_id=device(lax.rem(me + hop, count)),
+            device_id_type=pl.DeviceIdType.MESH)
+    pl.semaphore_wait(barrier, count - 1)
+
+    def copy(slot, hop, place):
+        return pltpu.make_async_remote_copy(
+            src_ref=value_ref, dst_ref=slots.at[slot], send_sem=send_sem.at[hop - 1],
+            recv_sem=recv_sem.at[hop - 1], device_id=device(place),
+            device_id_type=pl.DeviceIdType.MESH)
+
+    for hop in range(1, count):
+        copy(me, hop, lax.rem(me + hop, count)).start()
+    slots[pl.ds(me, 1)] = value_ref[...][None]
+    for hop in range(1, count):
+        origin = lax.rem(me + count - hop, count)
+        copy(origin, hop, origin).wait_recv()
+    for hop in range(1, count):
+        copy(me, hop, lax.rem(me + hop, count)).wait_send()
+
+    def span(start):
+        total = slots[start].astype(WIDE)
+        for slot in range(1, seq_count):
+            total = total + slots[start + slot].astype(WIDE)
+        return total
+
+    seq_ref[...] = span(dp * seq_count)
+    total = span(0)
+    for part in range(1, count // seq_count):
+        total = total + span(part * seq_count)
+    all_ref[...] = total
+
+
+def plane_sum(first, values, ident):
+    seq_count = lax.axis_size("seq")
+    count = lax.axis_size("dp") * seq_count
+    flat = jnp.concatenate([value.reshape(-1).astype(LOW) for value in [first] + values])
+    size = flat.shape[0]
+    lines = -(-size // 2048) * 16
+    packed = jnp.pad(flat, (0, lines * 128 - size)).reshape(lines, 128)
+    vmem = pl.BlockSpec(memory_space=pltpu.VMEM)
+    seq_total, all_total = pl.pallas_call(
+        functools.partial(plane_sum_kernel, seq_count),
+        out_shape=(jax.ShapeDtypeStruct((lines, 128), WIDE),) * 2,
+        in_specs=[vmem],
+        out_specs=(vmem, vmem),
+        scratch_shapes=[
+            pltpu.VMEM((count, lines, 128), LOW),
+            pltpu.SemaphoreType.DMA((count - 1,)),
+            pltpu.SemaphoreType.DMA((count - 1,)),
+        ],
+        compiler_params=pltpu.CompilerParams(collective_id=ident, has_side_effects=True),
+        name="plane_sum",
+    )(packed)
+    all_total = all_total.reshape(-1)
+    first_pair = (
+        seq_total.reshape(-1)[: first.size].reshape(first.shape),
+        all_total[: first.size].reshape(first.shape),
+    )
+    outs = []
+    start = first.size
+    for value in values:
+        outs.append(all_total[start : start + value.size].reshape(value.shape))
+        start += value.size
+    return first_pair, outs
+
 
 def small_kernel(value_ref, out_ref, slots, send_sem, recv_sem):
     count = slots.shape[0]
@@ -260,6 +341,271 @@
         outs.append(summed[start : start + value.size].reshape(value.shape))
         start += value.size
     return outs
+
+
+LOG2E = 1.4426950408889634
+HIDDEN_SCORE = -1e30
+
+
+def plane_places():
+    me = lax.axis_index("seq")
+    column = lax.rem(me, 2)
+    line = me // 2
+    return (me, me + 1 - 2 * column, me + 2 - 4 * line, 3 - me)
+
+
+def plane_barrier(places):
+    barrier = pltpu.get_barrier_semaphore()
+    for place in places[1:]:
+        pl.semaphore_signal(
+            barrier, inc=1, device_id={"seq": place}, device_id_type=pl.DeviceIdType.MESH
+        )
+    pl.semaphore_wait(barrier, 3)
+
+
+def plane_copy(src, dst, send, recv, place):
+    return pltpu.make_async_remote_copy(
+        src_ref=src,
+        dst_ref=dst,
+        send_sem=send,
+        recv_sem=recv,
+        device_id={"seq": place},
+        device_id_type=pl.DeviceIdType.MESH,
+    )
+
+
+def head_lanes(head):
+    return pl.ds(pl.multiple_of(head * HEAD_DIM, 128), HEAD_DIM)
+
+
+def block_valid(key_rows, owner, true_rows, length):
+    row = lax.broadcasted_iota(jnp.int32, (key_rows, 1), 0)
+    return (row < true_rows) & (owner * true_rows + row < length)
+
+
+def over_last(lhs, rhs):
+    return lax.dot_general(lhs, rhs, (((1,), (1,)), ((), ())), preferred_element_type=WIDE)
+
+
+def attend_kernel(
+    true_rows, length_ref, query_ref, kv_ref, out_ref, turned_ref, total_ref, got_ref, peak, summed, send, recv
+):
+    places = plane_places()
+    plane_barrier(places)
+    heads = query_ref.shape[1] // HEAD_DIM
+    key_rows = kv_ref.shape[1]
+    length = length_ref[0]
+    factor = LOG2E / math.sqrt(HEAD_DIM)
+
+    def own_copy(relation, part):
+        index = 2 * relation + part
+        return plane_copy(
+            kv_ref.at[part], got_ref.at[relation, part], send.at[index], recv.at[index], places[relation + 1]
+        )
+
+    key_pass = plane_copy(got_ref.at[0, 0], got_ref.at[2, 0], send.at[4], recv.at[4], places[2])
+    value_pass = plane_copy(got_ref.at[1, 1], got_ref.at[2, 1], send.at[5], recv.at[5], places[1])
+    for part in range(2):
+        for relation in range(2):
+            own_copy(relation, part).start()
+
+    peak[...] = jnp.full(peak.shape, HIDDEN_SCORE, WIDE)
+    summed[...] = jnp.zeros(summed.shape, WIDE)
+    turned_ref[...] = jnp.zeros(turned_ref.shape, WIDE)
+
+    def block(source, owner):
+        def step(head, carry):
+            lanes = head_lanes(head)
+            scores = over_last(source(0, lanes), query_ref[:, lanes]) * factor
+            scores = jnp.where(block_valid(key_rows, owner, true_rows, length), scores, HIDDEN_SCORE)
+            before = peak[head]
+            after = jnp.maximum(before, jnp.max(scores, axis=0, keepdims=True))
+            shrink = jnp.exp2(before - after)
+            terms = jnp.exp2(scores - after)
+            peak[head] = after
+            summed[head] = summed[head] * shrink + jnp.sum(terms, axis=0, keepdims=True)
+            turned_ref[head] = turned_ref[head] * shrink + lax.dot_general(
+                source(1, lanes),
+                terms.astype(LOW),
+                (((0,), (0,)), ((), ())),
+                preferred_element_type=WIDE,
+            )
+
+            return carry
+
+        lax.fori_loop(0, heads, step, 0)
+
+    block(lambda part, lanes: kv_ref[part, :, lanes], places[0])
+    own_copy(0, 0).wait_recv()
+    key_pass.start()
+    own_copy(0, 1).wait_recv()
+    own_copy(1, 1).wait_recv()
+    value_pass.start()
+    own_copy(1, 0).wait_recv()
+    for relation in range(3):
+        if relation == 2:
+            key_pass.wait_recv()
+            value_pass.wait_recv()
+        block(
+            lambda part, lanes, relation=relation: got_ref[relation, part, :, lanes],
+            places[relation + 1],
+        )
+
+    for head in range(heads):
+        lanes = slice(head * HEAD_DIM, (head + 1) * HEAD_DIM)
+        attended = turned_ref[head] / summed[head]
+        turned_ref[head] = attended
+        out_ref[:, lanes] = jnp.transpose(attended).astype(LOW)
+        total_ref[head] = peak[head] + jnp.log2(summed[head])
+    for part in range(2):
+        for relation in range(2):
+            own_copy(relation, part).wait_send()
+    key_pass.wait_send()
+    value_pass.wait_send()
+
+
+def attend(query_low, kv_low, length, true_rows, ident):
+    rows, width = query_low.shape
+    heads = width // HEAD_DIM
+    key_rows = kv_low.shape[1]
+    dma = pltpu.SemaphoreType.DMA
+    vmem = pl.BlockSpec(memory_space=pltpu.VMEM)
+    return pl.pallas_call(
+        functools.partial(attend_kernel, true_rows),
+        out_shape=(
+            jax.ShapeDtypeStruct((rows, width), LOW),
+            jax.ShapeDtypeStruct((heads, HEAD_DIM, rows), WIDE),
+            jax.ShapeDtypeStruct((heads, 1, rows), WIDE),
+            jax.ShapeDtypeStruct((3, 2, key_rows, width), LOW),
+        ),
+        in_specs=[pl.BlockSpec(memory_space=pltpu.SMEM), vmem, vmem],
+        out_specs=(vmem,) * 4,
+        scratch_shapes=[
+            pltpu.VMEM((heads, 1, rows), WIDE),
+            pltpu.VMEM((heads, 1, rows), WIDE),
+            dma((6,)),
+            dma((6,)),
+        ],
+        compiler_params=pltpu.CompilerParams(
+            collective_id=ident, has_side_effects=True, vmem_limit_bytes=56 << 20
+        ),
+        cost_estimate=pl.CostEstimate(flops=10**9, bytes_accessed=150 * 10**6, transcendentals=0),
+        name="attend",
+    )(length, query_low, kv_low)
+
+
+def attend_back_kernel(
+    true_rows, length_ref, query_ref, kv_ref, got_ref, turned_ref, total_ref, grad_ref,
+    query_grad_ref, kv_grad_ref, centre, query_turned, leaving, landing, send, recv,
+):
+    places = plane_places()
+    plane_barrier(places)
+    heads = query_ref.shape[1] // HEAD_DIM
+    key_rows = kv_ref.shape[1]
+    length = length_ref[0]
+    scale = 1.0 / math.sqrt(HEAD_DIM)
+    for head in range(heads):
+        lanes = slice(head * HEAD_DIM, (head + 1) * HEAD_DIM)
+        grads = jnp.transpose(grad_ref[:, lanes].astype(WIDE))
+        centre[head] = jnp.sum(grads * turned_ref[head], axis=0, keepdims=True)
+    query_turned[...] = jnp.zeros(query_turned.shape, WIDE)
+
+    def block(source, sink, owner):
+        def step(head, carry):
+            lanes = head_lanes(head)
+            keys = source(0, lanes)
+            query = query_ref[:, lanes]
+            grads = grad_ref[:, lanes]
+            probs = jnp.exp2(over_last(keys, query) * (scale * LOG2E) - total_ref[head])
+            probs = jnp.where(block_valid(key_rows, owner, true_rows, length), probs, 0.0)
+            grad_probs = over_last(source(1, lanes), grads)
+            grad_scores = (probs * (grad_probs - centre[head])).astype(LOW)
+            sink(0, lanes, jnp.dot(grad_scores, query, preferred_element_type=WIDE) * scale)
+            sink(1, lanes, jnp.dot(probs.astype(LOW), grads, preferred_element_type=WIDE))
+            query_turned[head] = query_turned[head] + lax.dot_general(
+                keys, grad_scores, (((0,), (0,)), ((), ())), preferred_element_type=WIDE
+            )
+
+            return carry
+
+        lax.fori_loop(0, heads, step, 0)
+
+    def grad_copy(relation, part):
+        return plane_copy(
+            leaving.at[relation, part],
+            landing.at[relation, part],
+            send.at[relation, part],
+            recv.at[relation, part],
+            places[relation + 1],
+        )
+
+    for relation in (2, 1, 0):
+
+        def sink(part, lanes, value, relation=relation):
+            leaving[relation, part, :, lanes] = value.astype(LOW)
+
+        block(
+            lambda part, lanes, relation=relation: got_ref[relation, part, :, lanes],
+            sink,
+            places[relation + 1],
+        )
+        for part in range(2):
+            grad_copy(relation, part).start()
+
+    def own_sink(part, lanes, value):
+        kv_grad_ref[part, :, lanes] = value
+
+    block(lambda part, lanes: kv_ref[part, :, lanes], own_sink, places[0])
+    for head in range(heads):
+        lanes = slice(head * HEAD_DIM, (head + 1) * HEAD_DIM)
+        query_grad_ref[:, lanes] = jnp.transpose(query_turned[head]) * scale
+    for relation in (2, 1, 0):
+        for part in range(2):
+            grad_copy(relation, part).wait_recv()
+
+    def gather(tile, carry):
+        rows = pl.ds(pl.multiple_of(tile * 16, 16), 16)
+        for part in range(2):
+            total = kv_grad_ref[part, rows]
+            for relation in range(3):
+                total = total + landing[relation, part, rows].astype(WIDE)
+            kv_grad_ref[part, rows] = total
+        return carry
+
+    lax.fori_loop(0, key_rows // 16, gather, 0)
+    for relation in range(3):
+        for part in range(2):
+            grad_copy(relation, part).wait_send()
+
+
+def attend_back(query_low, kv_low, got, turned, total, grad_low, length, true_rows, ident):
+    rows, width = query_low.shape
+    heads = width // HEAD_DIM
+    key_rows = kv_low.shape[1]
+    dma = pltpu.SemaphoreType.DMA
+    vmem = pl.BlockSpec(memory_space=pltpu.VMEM)
+    return pl.pallas_call(
+        functools.partial(attend_back_kernel, true_rows),
+        out_shape=(
+            jax.ShapeDtypeStruct((rows, width), WIDE),
+            jax.ShapeDtypeStruct((2, key_rows, width), WIDE),
+        ),
+        in_specs=[pl.BlockSpec(memory_space=pltpu.SMEM)] + [vmem] * 6,
+        out_specs=(vmem,) * 2,
+        scratch_shapes=[
+            pltpu.VMEM((heads, 1, rows), WIDE),
+            pltpu.VMEM((heads, HEAD_DIM, rows), WIDE),
+            pltpu.VMEM((3, 2, key_rows, width), LOW),
+            pltpu.VMEM((3, 2, key_rows, width), LOW),
+            dma((3, 2)),
+            dma((3, 2)),
+        ],
+        compiler_params=pltpu.CompilerParams(
+            collective_id=ident, has_side_effects=True, vmem_limit_bytes=56 << 20
+        ),
+        cost_estimate=pl.CostEstimate(flops=10**9, bytes_accessed=200 * 10**6, transcendentals=0),
+        name="attend_back",
+    )(length, query_low, kv_low, got, turned, total, grad_low)
 
 
 def head_forward(query, keys, values, key_ok, score_scale):
@@ -382,29 +728,46 @@
     query_low = rotate_now(query_norm).astype(low_type)
     key_low = rotate_now(key_norm).astype(low_type)
     value_low = value_pre.astype(low_type).reshape(head_shape)
-    local_kv = jnp.stack(
-        [
-            key_low.reshape(clip_count, seq_rows, local_width),
-            value_low.reshape(clip_count, seq_rows, local_width),
-        ]
-    )
-    whole_kv = lax.all_gather(local_kv, "seq", axis=2, tiled=True)
-    keys_all = whole_kv[0].reshape(clip_count, slot_count, local_heads, HEAD_DIM)
-    values_all = whole_kv[1].reshape(clip_count, slot_count, local_heads, HEAD_DIM)
-    att_heads = []
-    total_heads = []
-    for head_no in range(local_heads):
-        attended, log_total = head_forward(
-            query_low[:, :, head_no],
-            keys_all[:, :, head_no],
-            values_all[:, :, head_no],
-            key_valid,
-            score_scale,
+    plane = seq_count == 4 and clip_count == 1
+    if plane:
+        query_pad = -flat_rows % 128
+        key_pad = -flat_rows % 16
+        query_flat = query_low.reshape(flat_rows, local_width)
+        query_flat = jnp.pad(query_flat, ((0, query_pad), (0, 0)))
+        own_kv = jnp.pad(
+            jnp.stack(
+                [key_low.reshape(flat_rows, local_width), value_low.reshape(flat_rows, local_width)]
+            ),
+            ((0, 0), (0, key_pad), (0, 0)),
         )
-        att_heads.append(attended)
-        total_heads.append(log_total)
-    attn_low = jnp.stack(att_heads, axis=2).astype(low_type).reshape(flat_rows, local_width)
-    self_totals = jnp.stack(total_heads)
+        attn_low, attn_turned, self_totals, got_kv = attend(
+            query_flat, own_kv, clip_lengths, flat_rows, 10
+        )
+        attn_low = attn_low[:flat_rows]
+    else:
+        local_kv = jnp.stack(
+            [
+                key_low.reshape(clip_count, seq_rows, local_width),
+                value_low.reshape(clip_count, seq_rows, local_width),
+            ]
+        )
+        whole_kv = lax.all_gather(local_kv, "seq", axis=2, tiled=True)
+        keys_all = whole_kv[0].reshape(clip_count, slot_count, local_heads, HEAD_DIM)
+        values_all = whole_kv[1].reshape(clip_count, slot_count, local_heads, HEAD_DIM)
+        att_heads = []
+        total_heads = []
+        for head_no in range(local_heads):
+            attended, log_total = head_forward(
+                query_low[:, :, head_no],
+                keys_all[:, :, head_no],
+                values_all[:, :, head_no],
+                key_valid,
+                score_scale,
+            )
+            att_heads.append(attended)
+            total_heads.append(log_total)
+        attn_low = jnp.stack(att_heads, axis=2).astype(low_type).reshape(flat_rows, local_width)
+        self_totals = jnp.stack(total_heads)
     branch_one = (
         line_sum([(attn_low, self_out)], False, 0) + out_bias[0]
     )
@@ -467,18 +830,22 @@
     residue = jnp.where(valid_rows[:, None], result - teacher_rows, 0.0)
     grad_three = residue * gate_two
     grad_three_low = grad_three.astype(low_type)
-    grad_ffn_out = jnp.dot(act_low.T, grad_three_low, preferred_element_type=wide_type)
+    ffn_out_mix = jnp.dot(act_low.T, grad_three_low, preferred_element_type=wide_type)
     grad_act = jnp.dot(grad_three_low, ffn_out.T, preferred_element_type=wide_type)
     grad_pre = jax.vjp(gelu_tanh, pre_act)[1](grad_act)[0]
     grad_pre_low = grad_pre.astype(low_type)
-    grad_ffn_in = jnp.dot(ffn_input.T, grad_pre_low, preferred_element_type=wide_type)
+    grad_pre_low, ffn_out_mix = lax.optimization_barrier(
+        (grad_pre_low, ffn_out_mix.astype(low_type))
+    )
+    part_ffn_out = scatter_rows(ffn_out_mix, 1)
+    ffn_in_mix = jnp.dot(ffn_input.T, grad_pre_low, preferred_element_type=wide_type)
     grad_ffn_bias = jnp.sum(grad_pre, axis=0)
     grad_ffn_input = line_sum([(grad_pre_low, ffn_in)], True, 3)
     grad_after_two = (
         residue + jax.vjp(layer_norm, after_two)[1](grad_ffn_input * (1.0 + scale_two))[0]
     )
     grad_two_low = grad_after_two.astype(low_type)
-    grad_cross_out = jnp.dot(cross_att_low.T, grad_two_low, preferred_element_type=wide_type)
+    cross_out_mix = jnp.dot(grad_two_low.T, cross_att_low, preferred_element_type=wide_type)
     grad_cross_att = (
         jnp.dot(grad_two_low, cross_out.T, preferred_element_type=wide_type)
         .astype(low_type)
@@ -510,22 +877,29 @@
     text_grads = lax.psum_scatter(
         text_grads_all.astype(jnp.bfloat16), "seq", scatter_dimension=2, tiled=True
     ).astype(jnp.float32)
-    query_term, key_term = small_sum(
-        [
-            jnp.sum(grad_cross_query * norm_gains[2] * cross_query_pre, axis=-1),
-            jnp.sum(text_grads[0] * norm_gains[3] * text_key_pre, axis=-1),
-        ],
-        8,
+    (query_term,) = small_sum(
+        [jnp.sum(grad_cross_query * norm_gains[2] * cross_query_pre, axis=-1)], 8
     )
     grad_cross_query_pre = (
         grad_cross_query * norm_gains[2] * cross_rate
         - cross_query_pre * cross_rate**3 * query_term[:, None] / model_width
     )
+    gain_cross_query = jnp.sum(grad_cross_query * cross_query_pre * cross_rate, axis=0)
+    grad_cross_query_low = grad_cross_query_pre.astype(low_type)
+    grad_cross_query_low, ffn_in_mix, part_ffn_out = lax.optimization_barrier(
+        (grad_cross_query_low, ffn_in_mix.astype(low_type), part_ffn_out)
+    )
+    part_ffn_in = scatter_rows(ffn_in_mix, 0)
+    cross_q_mix = jnp.dot(cross_in.T, grad_cross_query_low, preferred_element_type=wide_type)
+    grad_cross_in = line_sum([(grad_cross_query_low, cross_q)], True, 4)
+    text_grads, grad_cross_in = lax.optimization_barrier((text_grads, grad_cross_in))
+    (key_term,) = small_sum(
+        [jnp.sum(text_grads[0] * norm_gains[3] * text_key_pre, axis=-1)], 12
+    )
     grad_text_key_pre = (
         text_grads[0] * norm_gains[3] * text_key_rate
         - text_key_pre * text_key_rate**3 * key_term[..., None] / model_width
     )
-    gain_cross_query = jnp.sum(grad_cross_query * cross_query_pre * cross_rate, axis=0)
     gain_text_key = jnp.sum(text_grads[0] * text_key_pre * text_key_rate, axis=(0, 1))
     grad_cross_bias = jnp.stack(
         [
@@ -534,10 +908,8 @@
             jnp.sum(text_grads[1], axis=(0, 1)),
         ]
     )
-    grad_cross_query_low = grad_cross_query_pre.astype(low_type)
     text_grad_low = jnp.stack([grad_text_key_pre, text_grads[1]]).astype(low_type)
-    grad_cross_q = jnp.dot(cross_in.T, grad_cross_query_low, preferred_element_type=wide_type)
-    grad_cross_kv = jnp.einsum(
+    cross_kv_mix = jnp.einsum(
         "ctd,kcte->kde", text_low, text_grad_low, preferred_element_type=wide_type
     )
     grad_text = lax.psum(
@@ -546,7 +918,6 @@
         ).astype(jnp.bfloat16),
         "tensor",
     ).astype(jnp.float32)
-    grad_cross_in = line_sum([(grad_cross_query_low, cross_q)], True, 4)
     grad_cross_gain = jnp.sum(grad_cross_in * normed_three, axis=0)
     grad_cross_shift = jnp.sum(grad_cross_in, axis=0)
     grad_after_one = (
@@ -554,52 +925,74 @@
     )
     grad_one = grad_after_one * gate_one
     grad_one_low = grad_one.astype(low_type)
-    grad_self_out = jnp.dot(attn_low.T, grad_one_low, preferred_element_type=wide_type)
+    self_out_mix = jnp.dot(grad_one_low.T, attn_low, preferred_element_type=wide_type)
     grad_attn = (
         jnp.dot(grad_one_low, self_out.T, preferred_element_type=wide_type)
         .astype(low_type)
         .reshape(head_shape)
     )
-    query_grads = []
-    key_grads = []
-    value_grads = []
-    for head_no in range(local_heads):
-        head_grads = head_backward(
-            query_low[:, :, head_no],
-            keys_all[:, :, head_no],
-            values_all[:, :, head_no],
-            key_valid,
-            self_totals[head_no],
-            grad_attn[:, :, head_no],
-            score_scale,
+    group_mix = jnp.concatenate(
+        [cross_out_mix, cross_q_mix, self_out_mix, cross_kv_mix[0], cross_kv_mix[1]], axis=-1
+    ).astype(low_type)
+    grad_attn, group_mix = lax.optimization_barrier((grad_attn, group_mix))
+    part_group = scatter_rows(group_mix, 0)
+    if plane:
+        query_grads, kv_grads = attend_back(
+            query_flat,
+            own_kv,
+            got_kv,
+            attn_turned,
+            self_totals,
+            jnp.pad(grad_attn.reshape(flat_rows, local_width), ((0, query_pad), (0, 0))),
+            clip_lengths,
+            flat_rows,
+            11,
         )
-        query_grads.append(head_grads[0])
-        key_grads.append(head_grads[2])
-        value_grads.append(head_grads[3])
-    owner_grads = [
-        jnp.stack(parts, axis=2)
-        .astype(jnp.bfloat16)
-        .reshape(clip_count, seq_count, seq_rows, local_width)
-        for parts in (key_grads, value_grads)
-    ]
-    owner_grads = jnp.concatenate(
-        [
-            jnp.swapaxes(part, 0, 1).reshape(seq_count, flat_rows, local_width)
-            for part in owner_grads
-        ],
-        axis=-1,
-    )
-    pad_rows = -flat_rows % 16
-    owner_grads = jnp.pad(owner_grads, ((0, 0), (0, pad_rows), (0, 0)))
-    kv_rows = lax.psum_scatter(
-        owner_grads.reshape(seq_count * (flat_rows + pad_rows), 2 * local_width),
-        "seq",
-        scatter_dimension=0,
-        tiled=True,
-    )[:flat_rows].astype(jnp.float32)
-    kv_grads = (kv_rows[:, :local_width], kv_rows[:, local_width:])
+        query_grads = query_grads[:flat_rows].reshape(head_shape)
+        kv_grads = kv_grads[:, :flat_rows]
+    else:
+        query_grads = []
+        key_grads = []
+        value_grads = []
+        for head_no in range(local_heads):
+            head_grads = head_backward(
+                query_low[:, :, head_no],
+                keys_all[:, :, head_no],
+                values_all[:, :, head_no],
+                key_valid,
+                self_totals[head_no],
+                grad_attn[:, :, head_no],
+                score_scale,
+            )
+            query_grads.append(head_grads[0])
+            key_grads.append(head_grads[2])
+            value_grads.append(head_grads[3])
+        owner_grads = [
+            jnp.stack(parts, axis=2)
+            .astype(jnp.bfloat16)
+            .reshape(clip_count, seq_count, seq_rows, local_width)
+            for parts in (key_grads, value_grads)
+        ]
+        owner_grads = jnp.concatenate(
+            [
+                jnp.swapaxes(part, 0, 1).reshape(seq_count, flat_rows, local_width)
+                for part in owner_grads
+            ],
+            axis=-1,
+        )
+        pad_rows = -flat_rows % 16
+        owner_grads = jnp.pad(owner_grads, ((0, 0), (0, pad_rows), (0, 0)))
+        kv_rows = lax.psum_scatter(
+            owner_grads.reshape(seq_count * (flat_rows + pad_rows), 2 * local_width),
+            "seq",
+            scatter_dimension=0,
+            tiled=True,
+        )[:flat_rows].astype(jnp.float32)
+        kv_grads = (kv_rows[:, :local_width], kv_rows[:, local_width:])
+        query_grads = jnp.stack(query_grads, axis=2)
+    query_grads, part_ffn_in = lax.optimization_barrier((query_grads, part_ffn_in))
     rotate_back = jax.vjp(rotate_now, query_norm)[1]
-    grad_query_norm = rotate_back(jnp.stack(query_grads, axis=2))[0].reshape(flat_rows, local_width)
+    grad_query_norm = rotate_back(query_grads)[0].reshape(flat_rows, local_width)
     grad_key_norm = rotate_back(kv_grads[0].reshape(head_shape))[0].reshape(flat_rows, local_width)
     query_back, key_back = small_sum(
         [
@@ -623,9 +1016,17 @@
     )
     grad_self_bias = jnp.sum(grad_proj, axis=1)
     grad_proj_low = grad_proj.astype(low_type)
-    grad_self_in = jnp.einsum(
-        "rd,kre->kde", attn_in, grad_proj_low, preferred_element_type=wide_type
-    )
+    self_in_mix = jnp.concatenate(
+        [
+            jnp.dot(attn_in.T, grad_proj_low[j], preferred_element_type=wide_type).astype(low_type)
+            for j in range(3)
+        ],
+        axis=-1,
+    )
+    grad_proj_low, self_in_mix, part_group = lax.optimization_barrier(
+        (grad_proj_low, self_in_mix, part_group)
+    )
+    part_self_in = scatter_rows(self_in_mix, 0)
     grad_attn_in = line_sum([(grad_proj_low[j], self_in[j]) for j in range(3)], True, 5)
     grad_hidden = (
         grad_after_one + jax.vjp(layer_norm, hidden_rows)[1](grad_attn_in * (1.0 + scale_one))[0]
@@ -652,8 +1053,23 @@
         jnp.sum(residue * residue),
     )
     grad_time_local, grad_cross_gain, grad_cross_shift, grad_out_bias, square_local = stream_values
-    grad_time = lax.psum(grad_time_local.astype(jnp.bfloat16), "seq").astype(jnp.float32)
     grad_norm_gains = jnp.stack([gain_query, gain_key, gain_cross_query, gain_text_key])
+    time_pair, sums = plane_sum(
+        grad_time_local,
+        [
+            grad_self_bias,
+            grad_norm_gains,
+            grad_cross_gain,
+            grad_cross_shift,
+            grad_cross_bias,
+            grad_ffn_bias,
+            grad_out_bias,
+            square_local,
+        ],
+        13,
+    )
+    grad_time, time_all = time_pair
+    sum_modulation = jnp.sum(time_all, axis=0)
     (
         sum_self_bias,
         sum_gains,
@@ -662,57 +1078,21 @@
         sum_cross_bias,
         sum_ffn_bias,
         sum_out_bias,
-        sum_modulation,
         square_sum,
-    ) = (
-        lax.psum(grad_self_bias.astype(jnp.bfloat16), ("dp", "seq")).astype(jnp.float32),
-        lax.psum(grad_norm_gains.astype(jnp.bfloat16), ("dp", "seq")).astype(jnp.float32),
-        lax.psum(grad_cross_gain.astype(jnp.bfloat16), ("dp", "seq")).astype(jnp.float32),
-        lax.psum(grad_cross_shift.astype(jnp.bfloat16), ("dp", "seq")).astype(jnp.float32),
-        lax.psum(grad_cross_bias.astype(jnp.bfloat16), ("dp", "seq")).astype(jnp.float32),
-        lax.psum(grad_ffn_bias.astype(jnp.bfloat16), ("dp", "seq")).astype(jnp.float32),
-        lax.psum(grad_out_bias.astype(jnp.bfloat16), ("dp", "seq")).astype(jnp.float32),
-        lax.psum(jnp.sum(grad_time_local, axis=0).astype(jnp.bfloat16), ("dp", "seq")).astype(
-            jnp.float32
-        ),
-        lax.psum(square_local.astype(jnp.bfloat16), ("dp", "seq")).astype(jnp.float32),
-    )
+    ) = sums
     loss = square_sum / (valid_total * model_width)
-    (
-        part_self_in,
-        part_self_out,
-        part_cross_q,
-        part_cross_kv,
-        part_cross_out,
-        part_ffn_in,
-        part_ffn_out,
-    ) = (
-        lax.psum_scatter(
-            grad_self_in.astype(jnp.bfloat16), ("dp", "seq"), scatter_dimension=1, tiled=True
-        ).astype(jnp.float32),
-        lax.psum_scatter(
-            grad_self_out.astype(jnp.bfloat16), ("dp", "seq"), scatter_dimension=1, tiled=True
-        ).astype(jnp.float32),
-        lax.psum_scatter(
-            grad_cross_q.astype(jnp.bfloat16), ("dp", "seq"), scatter_dimension=0, tiled=True
-        ).astype(jnp.float32),
-        lax.psum_scatter(
-            jnp.concatenate([grad_cross_kv[0], grad_cross_kv[1]], axis=-1).astype(jnp.bfloat16),
-            ("dp", "seq"),
-            scatter_dimension=0,
-            tiled=True,
-        ).astype(jnp.float32),
-        lax.psum_scatter(
-            grad_cross_out.astype(jnp.bfloat16), ("dp", "seq"), scatter_dimension=1, tiled=True
-        ).astype(jnp.float32),
-        lax.psum_scatter(
-            grad_ffn_in.astype(jnp.bfloat16), ("dp", "seq"), scatter_dimension=0, tiled=True
-        ).astype(jnp.float32),
-        lax.psum_scatter(
-            grad_ffn_out.astype(jnp.bfloat16), ("dp", "seq"), scatter_dimension=1, tiled=True
-        ).astype(jnp.float32),
-    )
-    part_cross_kv = jnp.stack([part_cross_kv[:, :local_width], part_cross_kv[:, local_width:]])
+    part_ffn_in = part_ffn_in.astype(wide_type)
+    part_ffn_out = part_ffn_out.astype(wide_type)
+    pieces = [
+        part_group[:, j * local_width : (j + 1) * local_width].astype(wide_type) for j in range(5)
+    ]
+    part_cross_out = pieces[0].T
+    part_cross_q = pieces[1]
+    part_self_out = pieces[2].T
+    part_cross_kv = jnp.stack([pieces[3], pieces[4]])
+    part_self_in = jnp.stack(
+        [part_self_in[:, j * local_width : (j + 1) * local_width] for j in range(3)]
+    ).astype(wide_type)
     result_out = result.reshape(clip_count, seq_rows, model_width)
     grad_hidden_out = grad_hidden.reshape(clip_count, seq_rows, model_width)
     return (

time: 1470 us -> 1230 us (0.84)
  waiting for transfers between devices: 263 us -> 62.4 us
  Pallas kernels: 469 us -> 618 us
  matrix products: 235 us -> 141 us
  other arithmetic: 181 us -> 126 us
  blocking collectives: 43.2 us -> 0 us
    reduce_scatter x6 -> x0, waiting for transfers between devices: 172 us -> none  [the longest x1 66.5 us: shards(): lax.psum_scatter(grad_ffn_in.astype(jnp.bfloat16), ('dp', 'seq'), scatter...]
    pallas_call x0 -> x3, Pallas kernels: none -> 148 us  [the longest x1 87.4 us: attend_back(): pl.pallas_call(functools.partial(attend_back_kernel, true_rows), out_shap...]
    psum x2 -> x0, blocking collectives: 43.2 us -> none  [the longest x1 28.5 us: shards(): lax.psum(square_local.astype(jnp.bfloat16), ('dp', 'seq'))]
    dot_general x6 -> x3, matrix products: 38.3 us -> 2.65 us  [head_backward(): jnp.einsum('csh,clh->csl', grad_att, values, preferred_element_type=jnp.f...]
    all_gather x1 -> x0, waiting for transfers between devices: 33.5 us -> none  [shards(): whole_kv = lax.all_gather(local_kv, 'seq', axis=2, tiled=True)]
    convert_element_type x4 -> x3, other arithmetic: 28.9 us -> 1.11 us  [head_backward(): (probs * (grad_probs - centre[..., None])).astype(jnp.bfloat16)]
    dot_general x6 -> x3, matrix products: 20.2 us -> 2.43 us  [head_forward(): jnp.einsum('csh,clh->csl', query, keys, preferred_element_type=jnp.float32)]
    unnamed x420 -> x325, local copies, waits for them, and re-layouts: 97.3 us -> 115 us
  transfers between devices with their start and end apart: 12 -> 7, of which waited for: 7 -> 2; matrix products, arithmetic and copies ran while one was open for 21% -> 25% of each run, Pallas kernels for 6% -> 25%
where the time goes in v3:
time: 1230 us; the launch traced here: 1220 us
  Pallas kernels  618 us (50%)
  local copies, waits for them, and re-layouts  257 us (21%)
  matrix products  141 us (11%)
  other arithmetic  126 us (10%)
  waiting for transfers between devices  62.4 us (5%)
  between operations  18.6 us (2%)
    pallas_call x6, Pallas kernels, line_sum(): pl.pallas_call(functools.partial(line_kernel, len(pairs), block, group, l...  434 us
    unnamed x325, local copies, waits for them, and re-layouts  115 us
    pallas_call x1, Pallas kernels, attend_back(): pl.pallas_call(functools.partial(attend_back_kernel, true_rows), out_shap...  87.4 us
    unnamed x12, waiting for transfers between devices  62.4 us
    pallas_call x1, Pallas kernels, attend(): pl.pallas_call(functools.partial(attend_kernel, true_rows), out_shape=(ja...  50.8 us
    pallas_call x5, Pallas kernels, small_sum(): pl.pallas_call(small_kernel, out_shape=jax.ShapeDtypeStruct((lines, 128),...  36.1 us
    reduce_sum x6, other arithmetic, layer_norm(): centred = values - jnp.mean(values, axis=-1, keepdims=True)  25.3 us
  transfers between devices with their start and end apart: 7, of which 2 were waited for; matrix products, arithmetic and copies ran while one was open for 25% of the time, Pallas kernels for 25%

profile of v3, /device:TPU:0, one launch (start us, length us, event | category | flops | bytes accessed | tf_op | source)
XLA Modules:
  0.0 1223.1 jit_solution(11929322855288789835)
XLA Ops:
  10.9 6.4 reduce_sum.371
  17.3 3.1 multiply_reduce_fusion.7
  22.3 3.9 add_convert_fusion.2
  26.2 3.3 add_bitcast_fusion.1
  48.1 8.8 small_sum_6.1
  58.4 3.9 fusion.65
  66.7 2.8 copy.137
  72.4 3.9 fusion.66
  78.8 9.8 copy.148.refs_1_
  91.9 50.8 %attend.1 = (bf16[896,384]{1,0:T(8,128)(2,1)}, f32[3,128,896]{2,1,0:T(8,128)}, f32[3,1,896]{2,1,0:T(1,128)}, bf16[3,2,784,384]{3,2,1,0:T(8,128)(2,1)}) custom-call(s32[1]{0:T(128)} %dynamic_slice.9.length_ref, bf16[896,384]{1,0:T(8,128)(2,1)} %pad.61.query_ref, bf16[2,784,384]{2,1,0:T(8,128)(2,1)} %fusion.73.kv_ref), custom_call_target="tpu_custom_call" | custom-call | flops 1000000000 | bytes 150000000 | tf_op jit(solution)/shard_map/attend/pallas_call | solution.py:473
  144.7 71.7 %line_sum_0.1 = bf16[800,1536]{1,0:T(8,128)(2,1)} custom-call(bf16[800,384]{1,0:T(8,128)(2,1)} %slice_select_fusion.refs_0_, bf16[384,1536]{1,0:T(8,128)(2,1)} %refs_1_.5), custom_call_target="tpu_custom_call" | custom-call | flops 943718400 | bytes 230000000 | tf_op jit(solution)/shard_map/line_sum_0/pallas_call | solution.py:190
  216.4 4.2 fusion.230
  232.5 6.8 small_sum_7.1
  259.9 69.6 %line_sum_1.1 = bf16[800,1536]{1,0:T(8,128)(2,1)} custom-call(bf16[800,384]{1,0:T(8,128)(2,1)} %pad.65.refs_0_, bf16[384,1536]{1,0:T(8,128)(2,1)} %refs_1_.6), custom_call_target="tpu_custom_call" | custom-call | flops 943718400 | bytes 230000000 | tf_op jit(solution)/shard_map/line_sum_1/pallas_call | solution.py:190
  329.6 3.9 fusion.229
  335.6 13.0 %multiply_convert_fusion = (bf16[780,2240]{1,0:T(8,128)(2,1)S(1)}, f32[780,2240]{1,0:T(8,128)}) fusion(f32[2240]{0:T(1024)S(1)} %copy-done.132, bf16[1536,2240]{0,1:T(8,128)(2,1)} %param.38, f32[780,1536]{1,0:T(8,128)S(1)} %get-tuple-element.168, f32[1536]{0:T(1024)S(1)} %copy-done.105, f32[1536]{0:T(1024)S(1)} %copy-done.65, f32[780]{0:T(1024)S(1)} %fusion.198, ...), kind=kOutput, calls=%fused_computation.14 | convolution fusion | flops 5394452480 | bytes 22187408 | tf_op jit(solution)/shard_map/dot_general | solution.py:824
  352.5 70.3 %line_sum_2.1 = bf16[800,1536]{1,0:T(8,128)(2,1)} custom-call(bf16[800,2240]{1,0:T(8,128)(2,1)} %pad.66.refs_0_, bf16[2240,1536]{1,0:T(8,128)(2,1)} %refs_1_.7), custom_call_target="tpu_custom_call" | custom-call | flops 5505024000 | bytes 230000000 | tf_op jit(solution)/shard_map/line_sum_2/pallas_call | solution.py:190
  422.9 7.0 fusion.9
  429.9 9.6 convolution_convert_fusion.1
  439.5 15.2 %fusion.232 = (bf16[2240]{0:T(1024)(128)(2,1)}, bf16[780,2240]{1,0:T(8,128)(2,1)S(1)}) fusion(bf16[2240,1536]{1,0:T(8,128)(2,1)} %refs_1_.7, f32[780,1536]{1,0:T(8,128)S(1)} %get-tuple-element.171, f32[1536]{0:T(1024)S(1)} %copy-done.63, f32[780]{0:T(1024)S(1)} %get-tuple-element.240, f32[780,2240]{1,0:T(8,128)} %get-tuple-element.223, ...), kind=kOutput, calls=%fused_computation.430 | convolution fusion | flops 5416412160 | bytes 22179504 | tf_op jit(solution)/shard_map/dot_general | solution.py:834
  458.6 73.6 %line_sum_3.1 = bf16[800,1536]{1,0:T(8,128)(2,1)} custom-call(bf16[800,2240]{1,0:T(8,128)(2,1)} %pad.67.refs_0_, bf16[1536,2240]{1,0:T(8,128)(2,1)} %copy.148.refs_1_), custom_call_target="tpu_custom_call" | custom-call | flops 5505024000 | bytes 230000000 | tf_op jit(solution)/shard_map/line_sum_3/pallas_call | solution.py:190
  532.2 4.6 multiply_reduce_fusion.4
  536.8 4.3 fusion.228
  558.3 3.0 copy.191
  561.3 6.8 bitcast_reduce_fusion
  569.2 9.9 copy.193
  584.8 2.9 copy.153
  593.7 6.7 small_sum_8.1
  601.8 3.7 fusion.226
  605.5 5.8 fusion.24
  611.4 10.0 convolution_convert_fusion
  624.8 38.9 %reduce-scatter.18.cloned.1.call-done = bf16[192,2240]{1,0:T(8,128)(2,1)} async-done(((bf16[1536,2240]{1,0:T(8,128)(2,1)}), bf16[192,2240]{1,0:T(8,128)(2,1)}) %reduce-scatter.18.cloned.1.call-update) | async-done | bytes 860176
  667.0 73.9 %line_sum_4.1 = bf16[800,1536]{1,0:T(8,128)(2,1)} custom-call(bf16[800,384]{1,0:T(8,128)(2,1)} %pad.69.refs_0_, bf16[1536,384]{1,0:T(8,128)(2,1)} %refs_1_.8), custom_call_target="tpu_custom_call" | custom-call | flops 943718400 | bytes 230000000 | tf_op jit(solution)/shard_map/line_sum_4/pallas_call | solution.py:190
  740.9 4.6 slice_convert_fusion
  746.8 6.7 small_sum_12.1
  755.7 3.2 fusion.21
  760.6 6.1 multiply_reduce_fusion.2
  776.3 4.4 fusion.23
  787.1 8.6 copy.197
  795.8 9.9 copy.195
  810.5 3.9 slice_bitcast_fusion.2
  814.4 9.6 copy.178
  826.9 6.2 fusion.112
  839.4 87.4 %attend_back.1 = (f32[896,384]{1,0:T(8,128)}, f32[2,784,384]{2,1,0:T(8,128)}) custom-call(s32[1]{0:T(128)} %dynamic_slice.9.length_ref, bf16[896,384]{1,0:T(8,128)(2,1)} %pad.61.query_ref, bf16[2,784,384]{2,1,0:T(8,128)(2,1)} %fusion.73.kv_ref, bf16[3,2,784,384]{3,2,1,0:T(8,128)(2,1)} %get-tuple-element.43.got_ref, ...), custom_call_target="tpu_custom_call" | custom-call | flops 1000000000 | bytes 200000000 | tf_op jit(solution)/shard_map/attend_back/pallas_call | solution.py:587
  932.0 3.2 fusion.234
  935.2 3.1 copy.166
  938.3 3.0 copy.167
  941.3 5.5 multiply_reduce_fusion.12
  949.6 2.8 copy.170
  952.4 3.2 copy.172
  955.7 5.3 fusion.105
  970.7 23.4 %reduce-scatter.20.cloned.1.call-done = bf16[192,2240]{1,0:T(8,128)(2,1)} async-done(((bf16[1536,2240]{1,0:T(8,128)(2,1)}), bf16[192,2240]{1,0:T(8,128)(2,1)}) %reduce-scatter.20.cloned.1.call-update) | async-done | bytes 860176
  998.7 6.4 multiply_reduce_fusion.13
  1010.6 2.8 copy.165
  1016.8 7.0 small_sum_9.1
  1024.7 3.1 multiply_subtract_fusion.1
  1039.5 5.8 copy.199
  1045.3 74.7 %line_sum_5.1 = bf16[800,1536]{1,0:T(8,128)(2,1)} custom-call(bf16[800,384]{1,0:T(8,128)(2,1)} %pad.73.refs_0_, bf16[800,384]{1,0:T(8,128)(2,1)} %pad.74.refs_1_, bf16[800,384]{1,0:T(8,128)(2,1)} %pad.75.refs_2_, bf16[1536,384]{1,0:T(8,128)(2,1)} %get-tuple-element.180.refs_3_, bf16[1536,384]{1,0:T(8,128)(2,1)} %get-tuple-element.181.refs_4_, ...), custom_call_target="tpu_custom_call" | custom-call | flops 2831155200 | bytes 230000000 | tf_op jit(solution)/shard_map/line_sum_5/pallas_call | solution.py:190
  1122.8 5.5 fusion.111
  1136.6 8.3 multiply_reduce_fusion.1
  1145.6 7.1 concatenate.51
  1154.1 9.7 plane_sum.1
  1170.1 5.3 fusion.224
  1178.1 9.5 copy.179
  (538 shorter events, 247.1 us)
Async XLA Ops:
  7.2 220.4 %copy-start = (bf16[2,1536,384]{2,1,0:T(8,128)(2,1)S(1)}, bf16[2,1536,384]{2,1,0:T(8,128)(2,1)}, u32[]{:S(2)}) copy-start(bf16[2,1536,384]{2,1,0:T(8,128)(2,1)} %param.35) | copy-start | bytes 7077892
  7.2 220.3 %all-gather.2.cloned.1.call-start = ((), (), s32[]{:S(2)}) async-start(), calls=%async_computation.5 | async-start | bytes 1966080 | tf_op jit(solution)/shard_map/all_gather | solution.py:780
  9.3 612.0 %reduce-scatter.16.cloned.1.call-start = ((), (), s32[]{:S(2)}) async-start(), calls=%async_computation.7 | async-start | bytes 983040
  10.9 11.4 copy-start.58
  10.9 205.5 %copy-start.71 = (f32[1536]{0:T(1024)}, f32[1536]{0:T(1024)S(1)}, u32[]{:S(2)}) copy-start(f32[1536]{0:T(1024)S(1)} %get-tuple-element.140) | copy-start | bytes 18436
  35.5 180.9 %copy-start.69 = (f32[1536]{0:T(1024)}, f32[1536]{0:T(1024)S(1)}, u32[]{:S(2)}) copy-start(f32[1536]{0:T(1024)S(1)} %get-tuple-element.144) | copy-start | bytes 18436
  42.6 19.7 %copy-start.25 = (f32[780,128]{0,1:T(8,128)}, f32[780,128]{0,1:T(8,128)S(1)}, u32[]{:S(2)}) copy-start(f32[780,128]{0,1:T(8,128)S(1)} %broadcast_in_dim.135) | copy-start | bytes 1198084
  45.9 26.4 %copy-start.30 = (f32[780,128]{1,0:T(8,128)}, f32[780,128]{1,0:T(8,128)S(1)}, u32[]{:S(2)}) copy-start(f32[780,128]{1,0:T(8,128)S(1)} %copy.133) | copy-start | bytes 1198084
  47.4 19.2 %copy-start.97 = (f32[384]{0:T(512)}, f32[384]{0:T(512)S(1)}, u32[]{:S(2)}) copy-start(f32[384]{0:T(512)S(1)} %get-tuple-element.151) | copy-start | bytes 4612
  47.4 24.9 %copy-start.95 = (f32[384]{0:T(512)}, f32[384]{0:T(512)S(1)}, u32[]{:S(2)}) copy-start(f32[384]{0:T(512)S(1)} %get-tuple-element.150) | copy-start | bytes 4612
  47.4 196.4 %copy-start.93 = (f32[384]{0:T(512)}, f32[384]{0:T(512)S(1)}, u32[]{:S(2)}) copy-start(f32[384]{0:T(512)S(1)} %get-tuple-element.152) | copy-start | bytes 4612
  58.4 8.3 copy-start.84
  58.4 14.0 %copy-start.90 = (f32[780]{0:T(1024)}, f32[780]{0:T(1024)S(1)}, u32[]{:S(2)}) copy-start(f32[780]{0:T(1024)S(1)} %get-tuple-element.206) | copy-start | bytes 9364
  78.8 9.8 copy-start.42
  91.9 50.8 %copy-start.131 = (pred[800]{0:T(1024)(128)(4,1)S(1)}, pred[800]{0:T(1024)(128)(4,1)}, u32[]{:S(2)}) copy-start(pred[800]{0:T(1024)(128)(4,1)} %constant.94.clone.1) | copy-start | bytes 2404
  231.7 17.5 %copy-start.20 = (f32[1,1,512,384]{2,3,0,1:T(8,128)}, f32[1,1,512,384]{2,3,0,1:T(8,128)S(1)}, u32[]{:S(2)}) copy-start(f32[1,1,512,384]{2,3,0,1:T(8,128)S(1)} %get-tuple-element.187) | copy-start | bytes 2359300
  241.9 7.3 copy-start.75
  256.9 72.7 %copy-start.36 = (bf16[1,780,3,128]{1,3,2,0:T(8,128)(2,1)}, bf16[1,780,3,128]{1,3,2,0:T(8,128)(2,1)S(1)}, u32[]{:S(2)}) copy-start(bf16[1,780,3,128]{1,3,2,0:T(8,128)(2,1)S(1)} %copy.146) | copy-start | bytes 1797124
  259.9 69.6 %copy-start.92 = (f32[1536]{0:T(1024)S(1)}, f32[1536]{0:T(1024)}, u32[]{:S(2)}) copy-start(f32[1536]{0:T(1024)} %get-tuple-element.145) | copy-start | bytes 18436
  334.2 202.6 %copy-start.81 = (f32[780]{0:T(1024)}, f32[780]{0:T(1024)S(1)}, u32[]{:S(2)}) copy-start(f32[780]{0:T(1024)S(1)} %fusion.198) | copy-start | bytes 9364
  352.5 70.3 %copy-start.63 = (f32[1536]{0:T(1024)S(1)}, f32[1536]{0:T(1024)}, u32[]{:S(2)}) copy-start(f32[1536]{0:T(1024)} %get-tuple-element.138) | copy-start | bytes 18436
  352.5 70.3 %copy-start.112 = (pred[780]{0:T(1024)(128)(4,1)S(1)}, pred[780]{0:T(1024)(128)(4,1)}, u32[]{:S(2)}) copy-start(pred[780]{0:T(1024)(128)(4,1)} %get-tuple-element.239) | copy-start | bytes 2344
  422.9 7.0 copy-start.29
  429.9 9.6 copy-start.3
  569.1 94.6 %reduce-scatter.18.cloned.1.call-start = ((), (), s32[]{:S(2)}) async-start(), calls=%async_computation.8 | async-start | bytes 7962624
  579.1 387.4 %all-reduce.18.cloned.1.call-start = ((), (), s32[]{:S(2)}) async-start(), calls=%async_computation.6 | async-start | bytes 786432 | tf_op jit(solution)/shard_map/psum | solution.py:915
  584.8 26.5 %slice-start = ((s8[4816896]{0:T(1024)(128)(4,1)}), s8[622592]{0:T(1024)(128)(4,1)S(1)}, s32[]{:S(2)}) async-start(s8[4816896]{0:T(1024)(128)(4,1)} %bitcast.440), calls=%async_computation.12 | async-start | bytes 1245184
  587.7 14.1 %copy-start.99 = (f32[780]{0:T(1024)S(1)}, f32[780]{0:T(1024)}, u32[]{:S(2)}) copy-start(f32[780]{0:T(1024)} %get-tuple-element.210) | copy-start | bytes 9364
  601.8 9.5 slice-start.1
  621.4 44.7 %copy-start.43 = (bf16[780,384]{1,0:T(8,128)(2,1)S(1)}, bf16[780,384]{1,0:T(8,128)(2,1)}, u32[]{:S(2)}) copy-start(bf16[780,384]{1,0:T(8,128)(2,1)} %get-tuple-element.48) | copy-start | bytes 1797124
  624.8 129.5 %copy-start.23 = (f32[2,1,128,384]{2,3,1,0:T(8,128)}, f32[2,1,128,384]{2,3,1,0:T(8,128)S(1)}, u32[]{:S(2)}) copy-start(f32[2,1,128,384]{2,3,1,0:T(8,128)S(1)} %convert_element_type.353) | copy-start | bytes 1179652
  760.6 6.2 slice-start.2
  760.6 6.2 copy-start.89
  760.6 6.2 slice-start.3
  760.6 6.6 copy-start.5
  774.0 6.6 slice-start.8
  783.3 185.2 %reduce-scatter.22.cloned.1.call-start = ((), (), s32[]{:S(2)}) async-start(), calls=%async_computation.10 | async-start | bytes 6635520
  795.7 198.4 %reduce-scatter.20.cloned.1.call-start = ((), (), s32[]{:S(2)}) async-start(), calls=%async_computation.9 | async-start | bytes 7962624
  805.7 403.0 %reduce-scatter.24.cloned.1.call-start = ((), (), s32[]{:S(2)}) async-start(), calls=%async_computation.11 | async-start | bytes 3981312
  814.4 12.5 %copy-start.83 = (f32[780]{0:T(1024)S(1)}, f32[780]{0:T(1024)}, u32[]{:S(2)}) copy-start(f32[780]{0:T(1024)} %copy-done.81) | copy-start | bytes 9364
  814.4 19.3 %slice-start.6 = ((s8[4816896]{0:T(1024)(128)(4,1)}), s8[622592]{0:T(1024)(128)(4,1)S(1)}, s32[]{:S(2)}) async-start(s8[4816896]{0:T(1024)(128)(4,1)} %bitcast.446), calls=%async_computation.18 | async-start | bytes 1245184
  824.0 9.7 slice-start.7
  826.9 6.8 copy-start.18
  935.2 6.1 copy-start.46
  935.2 6.1 copy-start.91
  935.2 6.1 copy-start.120
  935.2 6.1 copy-start.123
  935.2 6.1 copy-start.126
  935.2 6.1 copy-start.129
  955.7 7.8 copy-start.113
  955.7 9.2 copy-start.22
  970.7 27.9 %copy-start.85 = (f32[780]{0:T(1024)S(1)}, f32[780]{0:T(1024)}, u32[]{:S(2)}) copy-start(f32[780]{0:T(1024)} %copy-done.84) | copy-start | bytes 9364
  970.7 27.9 %copy-start.121 = (s32[128]{0:T(128)S(1)}, s32[128]{0:T(128)}, u32[]{:S(2)}) copy-start(s32[128]{0:T(128)} %get-tuple-element.235) | copy-start | bytes 1540
  970.7 27.9 %copy-start.124 = (s32[128]{0:T(128)S(1)}, s32[128]{0:T(128)}, u32[]{:S(2)}) copy-start(s32[128]{0:T(128)} %get-tuple-element.236) | copy-start | bytes 1540
  970.7 27.9 %copy-start.127 = (pred[128]{0:T(512)(128)(4,1)S(1)}, pred[128]{0:T(512)(128)(4,1)}, u32[]{:S(2)}) copy-start(pred[128]{0:T(512)(128)(4,1)} %get-tuple-element.237) | copy-start | bytes 388
  970.7 27.9 %copy-start.130 = (pred[128]{0:T(512)(128)(4,1)S(1)}, pred[128]{0:T(512)(128)(4,1)}, u32[]{:S(2)}) copy-start(pred[128]{0:T(512)(128)(4,1)} %get-tuple-element.238) | copy-start | bytes 388
  1013.4 11.3 copy-start.101
  1013.4 11.3 copy-start.102
  1128.3 8.3 copy-start.59
  1128.3 8.3 copy-start.64
  1136.6 32.6 %copy-start.87 = (f32[780]{0:T(1024)S(1)}, f32[780]{0:T(1024)}, u32[]{:S(2)}) copy-start(f32[780]{0:T(1024)} %copy-done.86) | copy-start | bytes 9364
  1169.2 6.2 slice-start.10
  1178.1 10.9 copy-start.55
  1201.1 6.3 copy-start.62
  (93 other events, 325.7 us)
Sparse Core Ops, SparseCore 0:
  9.9 33.5 all-gather.1
  569.3 25.3 reduce-scatter.15
  598.1 65.5 reduce-scatter.17
  783.4 36.5 all-reduce.17
  823.3 101.8 reduce-scatter.21
  928.6 65.4 reduce-scatter.19
  1045.5 47.8 reduce-scatter.23

commit v4 on v3

--- a/solution.py
+++ b/solution.py
@@ -178,12 +178,13 @@
 
     lax.fori_loop(0, steps, drain, 0)
 
-def line_sum(pairs, turned, ident, block=32, group=5, lag=3, lag2=6):
-    true_rows = pairs[0][0].shape[0]
+def line_sum(pairs, turned, ident, true_rows, block=16, group=7, lag=4, lag2=8):
     width = pairs[0][1].shape[0 if turned else 1]
     unit = block * group
     rows = -(-true_rows // unit) * unit
-    pairs = [(jnp.pad(lhs, ((0, rows - true_rows), (0, 0))), rhs) for lhs, rhs in pairs]
+    pairs = [
+        (jnp.pad(lhs, ((0, max(rows - lhs.shape[0], 0)), (0, 0))), rhs) for lhs, rhs in pairs
+    ]
     steps = rows // block
     dma = pltpu.SemaphoreType.DMA
     depth = sum(p[0].shape[1] for p in pairs)
@@ -509,6 +510,8 @@
         grads = jnp.transpose(grad_ref[:, lanes].astype(WIDE))
         centre[head] = jnp.sum(grads * turned_ref[head], axis=0, keepdims=True)
     query_turned[...] = jnp.zeros(query_turned.shape, WIDE)
+    spare = query_ref.shape[0] - key_rows
+    kv_grad_ref[:, pl.ds(key_rows, spare), :] = jnp.zeros((2, spare, query_ref.shape[1]), WIDE)
 
     def block(source, sink, owner):
         def step(head, carry):
@@ -553,7 +556,7 @@
             grad_copy(relation, part).start()
 
     def own_sink(part, lanes, value):
-        kv_grad_ref[part, :, lanes] = value
+        kv_grad_ref[part, pl.ds(0, key_rows), lanes] = value
 
     block(lambda part, lanes: kv_ref[part, :, lanes], own_sink, places[0])
     for head in range(heads):
@@ -588,7 +591,7 @@
         functools.partial(attend_back_kernel, true_rows),
         out_shape=(
             jax.ShapeDtypeStruct((rows, width), WIDE),
-            jax.ShapeDtypeStruct((2, key_rows, width), WIDE),
+            jax.ShapeDtypeStruct((2, rows, width), WIDE),
         ),
         in_specs=[pl.BlockSpec(memory_space=pltpu.SMEM)] + [vmem] * 6,
         out_specs=(vmem,) * 2,
@@ -606,6 +609,246 @@
         cost_estimate=pl.CostEstimate(flops=10**9, bytes_accessed=200 * 10**6, transcendentals=0),
         name="attend_back",
     )(length, query_low, kv_low, got, turned, total, grad_low)
+
+
+def pair_swap(values):
+    lane = lax.broadcasted_iota(jnp.int32, values.shape, 1)
+    return jnp.where(
+        lax.rem(lane, 2) == 0,
+        pltpu.roll(values, HEAD_DIM - 1, axis=1),
+        pltpu.roll(values, 1, axis=1),
+    )
+
+
+def rows_to_lanes(values):
+    return jnp.sum(jnp.transpose(values), axis=0, keepdims=True)
+
+
+def lanes_to_rows(row):
+    return jnp.transpose(jnp.broadcast_to(row, (HEAD_DIM, row.shape[1])))
+
+
+def tensor_barrier():
+    count = lax.axis_size("tensor")
+    me = lax.axis_index("tensor")
+    barrier = pltpu.get_barrier_semaphore()
+    for hop in range(1, count):
+        pl.semaphore_signal(
+            barrier, inc=1, device_id={"tensor": lax.rem(me + hop, count)},
+            device_id_type=pl.DeviceIdType.MESH)
+    pl.semaphore_wait(barrier, count - 1)
+
+
+def tensor_copy(stage, slots, send, recv, slot, hop, place):
+    return pltpu.make_async_remote_copy(
+        src_ref=stage, dst_ref=slots.at[slot], send_sem=send.at[hop - 1],
+        recv_sem=recv.at[hop - 1], device_id={"tensor": place},
+        device_id_type=pl.DeviceIdType.MESH)
+
+
+def tensor_send(stage, slots, send, recv):
+    count = slots.shape[0]
+    me = lax.axis_index("tensor")
+    for hop in range(1, count):
+        tensor_copy(stage, slots, send, recv, me, hop, lax.rem(me + hop, count)).start()
+    slots[pl.ds(me, 1)] = stage[...][None]
+
+
+def tensor_collect(stage, slots, send, recv):
+    count = slots.shape[0]
+    me = lax.axis_index("tensor")
+    for hop in range(1, count):
+        origin = lax.rem(me + count - hop, count)
+        tensor_copy(stage, slots, send, recv, origin, hop, origin).wait_recv()
+    for hop in range(1, count):
+        tensor_copy(stage, slots, send, recv, me, hop, lax.rem(me + hop, count)).wait_send()
+    total = slots[0]
+    for slot in range(1, count):
+        total = total + slots[slot]
+    return total
+
+
+def project_kernel(
+    rows_ref, weight_ref, bias_ref, gain_ref, cosine_ref, sine_ref,
+    pre_ref, query_ref, kv_ref, square_ref, stage, slots, send, recv,
+):
+    heads = query_ref.shape[1] // HEAD_DIM
+    key_rows = kv_ref.shape[1]
+    width = rows_ref.shape[1]
+    tensor_barrier()
+    stage[...] = jnp.zeros(stage.shape, WIDE)
+    for part in range(2):
+        pre_ref[part] = (
+            jnp.dot(rows_ref[...], weight_ref[part], preferred_element_type=WIDE)
+            + bias_ref[part : part + 1]
+        )
+        squares = None
+        for head in range(heads):
+            piece = pre_ref[part, :, head * HEAD_DIM : (head + 1) * HEAD_DIM]
+            squares = piece * piece if squares is None else squares + piece * piece
+        stage[part : part + 1] = rows_to_lanes(squares)
+    tensor_send(stage, slots, send, recv)
+    values = jnp.dot(rows_ref[...], weight_ref[2], preferred_element_type=WIDE) + bias_ref[2:3]
+    kv_ref[1] = values[:key_rows].astype(LOW)
+    total = tensor_collect(stage, slots, send, recv)
+    square_ref[...] = total
+    for part in range(2):
+        rate = lanes_to_rows(lax.rsqrt(total[part : part + 1] / width + eps_norm))
+        for head in range(heads):
+            lanes = slice(head * HEAD_DIM, (head + 1) * HEAD_DIM)
+            normed = pre_ref[part, :, lanes] * rate * gain_ref[part : part + 1, lanes]
+            turned = normed * cosine_ref[...] + pair_swap(normed) * sine_ref[...]
+            if part == 0:
+                query_ref[:, lanes] = turned.astype(LOW)
+            else:
+                kv_ref[0, :, lanes] = turned[:key_rows].astype(LOW)
+
+
+def project(rows_low, weights, bias, gains, cosine, sine, key_rows, ident):
+    rows = rows_low.shape[0]
+    width = weights.shape[2]
+    count = lax.axis_size("tensor")
+    vmem = pl.BlockSpec(memory_space=pltpu.VMEM)
+    dma = pltpu.SemaphoreType.DMA
+    return pl.pallas_call(
+        project_kernel,
+        out_shape=(
+            jax.ShapeDtypeStruct((2, rows, width), WIDE),
+            jax.ShapeDtypeStruct((rows, width), LOW),
+            jax.ShapeDtypeStruct((2, key_rows, width), LOW),
+            jax.ShapeDtypeStruct((8, rows), WIDE),
+        ),
+        in_specs=[vmem] * 6,
+        out_specs=(vmem,) * 4,
+        scratch_shapes=[
+            pltpu.VMEM((8, rows), WIDE),
+            pltpu.VMEM((count, 8, rows), WIDE),
+            dma((count - 1,)),
+            dma((count - 1,)),
+        ],
+        compiler_params=pltpu.CompilerParams(
+            collective_id=ident, has_side_effects=True, vmem_limit_bytes=56 << 20
+        ),
+        name="project",
+    )(rows_low, weights, bias, gains, cosine, sine)
+
+
+def unproject_kernel(
+    width, query_grad_ref, kv_grad_ref, pre_ref, square_ref, gain_ref, cosine_ref, sine_ref,
+    query_low_ref, key_low_ref, value_low_ref, sums_ref, work, stage, slots, send, recv,
+):
+    heads = query_grad_ref.shape[1] // HEAD_DIM
+    tensor_barrier()
+    stage[...] = jnp.zeros(stage.shape, WIDE)
+    sums_ref[...] = jnp.zeros(sums_ref.shape, WIDE)
+    total = square_ref[...]
+    for part in range(2):
+        terms = None
+        rate = lanes_to_rows(lax.rsqrt(total[part : part + 1] / width + eps_norm))
+        for head in range(heads):
+            lanes = slice(head * HEAD_DIM, (head + 1) * HEAD_DIM)
+            grads = query_grad_ref[:, lanes] if part == 0 else kv_grad_ref[0, :, lanes]
+            grads = grads * cosine_ref[...] - pair_swap(grads) * sine_ref[...]
+            pre = pre_ref[part, :, lanes]
+            sums_ref[3 + part : 4 + part, lanes] = jnp.sum(
+                grads * pre * rate, axis=0, keepdims=True
+            )
+            grads = grads * gain_ref[part : part + 1, lanes]
+            work[part, :, lanes] = grads
+            terms = grads * pre if terms is None else terms + grads * pre
+        stage[part : part + 1] = rows_to_lanes(terms)
+    tensor_send(stage, slots, send, recv)
+    values = kv_grad_ref[1]
+    sums_ref[2:3] = jnp.sum(values, axis=0, keepdims=True)
+    value_low_ref[...] = values.astype(LOW)
+    back_total = tensor_collect(stage, slots, send, recv)
+    for part in range(2):
+        rate_row = lax.rsqrt(total[part : part + 1] / width + eps_norm)
+        rate = lanes_to_rows(rate_row)
+        back = lanes_to_rows(rate_row * rate_row * rate_row * back_total[part : part + 1] / width)
+        for head in range(heads):
+            lanes = slice(head * HEAD_DIM, (head + 1) * HEAD_DIM)
+            grads = work[part, :, lanes] * rate - pre_ref[part, :, lanes] * back
+            sums_ref[part : part + 1, lanes] = jnp.sum(grads, axis=0, keepdims=True)
+            if part == 0:
+                query_low_ref[:, lanes] = grads.astype(LOW)
+            else:
+                key_low_ref[:, lanes] = grads.astype(LOW)
+
+
+def unproject(query_grads, kv_grads, pre, squares, gains, cosine, sine, model_width, ident):
+    rows, width = query_grads.shape
+    count = lax.axis_size("tensor")
+    vmem = pl.BlockSpec(memory_space=pltpu.VMEM)
+    dma = pltpu.SemaphoreType.DMA
+    return pl.pallas_call(
+        functools.partial(unproject_kernel, model_width),
+        out_shape=(jax.ShapeDtypeStruct((rows, width), LOW),) * 3
+        + (jax.ShapeDtypeStruct((8, width), WIDE),),
+        in_specs=[vmem] * 7,
+        out_specs=(vmem,) * 4,
+        scratch_shapes=[
+            pltpu.VMEM((2, rows, width), WIDE),
+            pltpu.VMEM((8, rows), WIDE),
+            pltpu.VMEM((count, 8, rows), WIDE),
+            dma((count - 1,)),
+            dma((count - 1,)),
+        ],
+        compiler_params=pltpu.CompilerParams(
+            collective_id=ident, has_side_effects=True, vmem_limit_bytes=56 << 20
+        ),
+        name="unproject",
+    )(query_grads, kv_grads, pre, squares, gains, cosine, sine)
+
+
+def seq_scatter_kernel(blocks_ref, out_ref, slots, send_sem, recv_sem):
+    count = slots.shape[0]
+    me = lax.axis_index("seq")
+    barrier = pltpu.get_barrier_semaphore()
+    for hop in range(1, count):
+        pl.semaphore_signal(
+            barrier, inc=1, device_id={"seq": lax.rem(me + hop, count)},
+            device_id_type=pl.DeviceIdType.MESH)
+    pl.semaphore_wait(barrier, count - 1)
+
+    def copy(block, slot, hop, place):
+        return pltpu.make_async_remote_copy(
+            src_ref=blocks_ref.at[block], dst_ref=slots.at[slot], send_sem=send_sem.at[hop - 1],
+            recv_sem=recv_sem.at[hop - 1], device_id={"seq": place},
+            device_id_type=pl.DeviceIdType.MESH)
+
+    for hop in range(1, count):
+        place = lax.rem(me + hop, count)
+        copy(place, me, hop, place).start()
+    slots[pl.ds(me, 1)] = blocks_ref[pl.ds(me, 1)]
+    for hop in range(1, count):
+        origin = lax.rem(me + count - hop, count)
+        copy(me, origin, hop, origin).wait_recv()
+    for hop in range(1, count):
+        place = lax.rem(me + hop, count)
+        copy(place, me, hop, place).wait_send()
+    total = slots[0].astype(WIDE)
+    for slot in range(1, count):
+        total = total + slots[slot].astype(WIDE)
+    out_ref[...] = total
+
+
+def seq_scatter(blocks, ident):
+    count, rows, width = blocks.shape
+    vmem = pl.BlockSpec(memory_space=pltpu.VMEM)
+    return pl.pallas_call(
+        seq_scatter_kernel,
+        out_shape=jax.ShapeDtypeStruct((rows, width), WIDE),
+        in_specs=[vmem],
+        out_specs=vmem,
+        scratch_shapes=[
+            pltpu.VMEM((count, rows, width), LOW),
+            pltpu.SemaphoreType.DMA((count - 1,)),
+            pltpu.SemaphoreType.DMA((count - 1,)),
+        ],
+        compiler_params=pltpu.CompilerParams(collective_id=ident, has_side_effects=True),
+        name="seq_scatter",
+    )(blocks)
 
 
 def head_forward(query, keys, values, key_ok, score_scale):
@@ -710,41 +953,30 @@
     scale_two = per_row(4)
     gate_two = per_row(5)
     normed_one = layer_norm(hidden_rows)
-    attn_in = (normed_one * (1.0 + scale_one) + per_row(0)).astype(low_type)
-    projected = (
-        jnp.einsum("rd,kde->kre", attn_in, self_in, preferred_element_type=wide_type)
-        + self_bias[:, None, :]
-    )
-    query_pre = projected[0]
-    key_pre = projected[1]
-    value_pre = projected[2]
-    query_sq, key_sq = small_sum(
-        [jnp.sum(query_pre * query_pre, axis=-1), jnp.sum(key_pre * key_pre, axis=-1)], 6
-    )
-    query_rate = lax.rsqrt(query_sq / model_width + eps_norm)[:, None]
-    key_rate = lax.rsqrt(key_sq / model_width + eps_norm)[:, None]
-    query_norm = (query_pre * query_rate * norm_gains[0]).reshape(head_shape)
-    key_norm = (key_pre * key_rate * norm_gains[1]).reshape(head_shape)
-    query_low = rotate_now(query_norm).astype(low_type)
-    key_low = rotate_now(key_norm).astype(low_type)
-    value_low = value_pre.astype(low_type).reshape(head_shape)
+    query_pad = -flat_rows % 128
+    key_pad = -flat_rows % 16
+
+    def pad_queries(values):
+        return jnp.pad(values, ((0, query_pad), (0, 0)))
+
+    attn_in = pad_queries((normed_one * (1.0 + scale_one) + per_row(0)).astype(low_type))
+    cosine_flat = pad_queries(cosine_rep.reshape(flat_rows, HEAD_DIM))
+    sine_flat = pad_queries(sine_rep.reshape(flat_rows, HEAD_DIM)) * jnp.where(
+        jnp.arange(HEAD_DIM) % 2 == 0, -1.0, 1.0
+    )
+    self_gains = norm_gains[:2]
+    proj_pre, query_flat, own_kv, proj_squares = project(
+        attn_in, self_in, self_bias, self_gains, cosine_flat, sine_flat, flat_rows + key_pad, 6
+    )
     plane = seq_count == 4 and clip_count == 1
     if plane:
-        query_pad = -flat_rows % 128
-        key_pad = -flat_rows % 16
-        query_flat = query_low.reshape(flat_rows, local_width)
-        query_flat = jnp.pad(query_flat, ((0, query_pad), (0, 0)))
-        own_kv = jnp.pad(
-            jnp.stack(
-                [key_low.reshape(flat_rows, local_width), value_low.reshape(flat_rows, local_width)]
-            ),
-            ((0, 0), (0, key_pad), (0, 0)),
-        )
         attn_low, attn_turned, self_totals, got_kv = attend(
             query_flat, own_kv, clip_lengths, flat_rows, 10
         )
-        attn_low = attn_low[:flat_rows]
     else:
+        query_low = query_flat[:flat_rows].reshape(head_shape)
+        key_low = own_kv[0, :flat_rows]
+        value_low = own_kv[1, :flat_rows]
         local_kv = jnp.stack(
             [
                 key_low.reshape(clip_count, seq_rows, local_width),
@@ -767,9 +999,10 @@
             att_heads.append(attended)
             total_heads.append(log_total)
         attn_low = jnp.stack(att_heads, axis=2).astype(low_type).reshape(flat_rows, local_width)
+        attn_low = pad_queries(attn_low)
         self_totals = jnp.stack(total_heads)
     branch_one = (
-        line_sum([(attn_low, self_out)], False, 0) + out_bias[0]
+        line_sum([(attn_low, self_out)], False, 0, flat_rows) + out_bias[0]
     )
     after_one = hidden_rows + branch_one * gate_one
     normed_three = layer_norm(after_one)
@@ -815,7 +1048,7 @@
     cross_att_low = jnp.stack(cross_heads, axis=2).astype(low_type).reshape(flat_rows, local_width)
     cross_totals = jnp.stack(cross_total_heads)
     branch_two = (
-        line_sum([(cross_att_low, cross_out)], False, 1)
+        line_sum([(cross_att_low, cross_out)], False, 1, flat_rows)
         + out_bias[1]
     )
     after_two = after_one + branch_two
@@ -824,7 +1057,7 @@
     pre_act = jnp.dot(ffn_input, ffn_in, preferred_element_type=wide_type) + ffn_in_bias
     act_low = gelu_tanh(pre_act).astype(low_type)
     branch_three = (
-        line_sum([(act_low, ffn_out)], False, 2) + out_bias[2]
+        line_sum([(act_low, ffn_out)], False, 2, flat_rows) + out_bias[2]
     )
     result = after_two + branch_three * gate_two
     residue = jnp.where(valid_rows[:, None], result - teacher_rows, 0.0)
@@ -840,7 +1073,7 @@
     part_ffn_out = scatter_rows(ffn_out_mix, 1)
     ffn_in_mix = jnp.dot(ffn_input.T, grad_pre_low, preferred_element_type=wide_type)
     grad_ffn_bias = jnp.sum(grad_pre, axis=0)
-    grad_ffn_input = line_sum([(grad_pre_low, ffn_in)], True, 3)
+    grad_ffn_input = line_sum([(grad_pre_low, ffn_in)], True, 3, flat_rows)
     grad_after_two = (
         residue + jax.vjp(layer_norm, after_two)[1](grad_ffn_input * (1.0 + scale_two))[0]
     )
@@ -874,11 +1107,25 @@
             jnp.stack(text_value_grads, axis=2).reshape(clip_count, text_count, local_width),
         ]
     )
-    text_grads = lax.psum_scatter(
-        text_grads_all.astype(jnp.bfloat16), "seq", scatter_dimension=2, tiled=True
-    ).astype(jnp.float32)
-    (query_term,) = small_sum(
-        [jnp.sum(grad_cross_query * norm_gains[2] * cross_query_pre, axis=-1)], 8
+    text_blocks = text_grads_all.astype(low_type).reshape(
+        2, clip_count, seq_count, text_local, local_width
+    )
+    text_blocks = jnp.transpose(text_blocks, (2, 1, 3, 0, 4)).reshape(
+        seq_count, clip_count * text_local, 2 * local_width
+    )
+    text_rows = seq_scatter(text_blocks, 14)
+    text_grads = [
+        text_rows[:, j * local_width : (j + 1) * local_width].reshape(
+            clip_count, text_local, local_width
+        )
+        for j in range(2)
+    ]
+    query_term, key_term = small_sum(
+        [
+            jnp.sum(grad_cross_query * norm_gains[2] * cross_query_pre, axis=-1),
+            jnp.sum(text_grads[0] * norm_gains[3] * text_key_pre, axis=-1),
+        ],
+        8,
     )
     grad_cross_query_pre = (
         grad_cross_query * norm_gains[2] * cross_rate
@@ -891,11 +1138,7 @@
     )
     part_ffn_in = scatter_rows(ffn_in_mix, 0)
     cross_q_mix = jnp.dot(cross_in.T, grad_cross_query_low, preferred_element_type=wide_type)
-    grad_cross_in = line_sum([(grad_cross_query_low, cross_q)], True, 4)
-    text_grads, grad_cross_in = lax.optimization_barrier((text_grads, grad_cross_in))
-    (key_term,) = small_sum(
-        [jnp.sum(text_grads[0] * norm_gains[3] * text_key_pre, axis=-1)], 12
-    )
+    grad_cross_in = line_sum([(grad_cross_query_low, cross_q)], True, 4, flat_rows)
     grad_text_key_pre = (
         text_grads[0] * norm_gains[3] * text_key_rate
         - text_key_pre * text_key_rate**3 * key_term[..., None] / model_width
@@ -925,7 +1168,7 @@
     )
     grad_one = grad_after_one * gate_one
     grad_one_low = grad_one.astype(low_type)
-    self_out_mix = jnp.dot(grad_one_low.T, attn_low, preferred_element_type=wide_type)
+    self_out_mix = jnp.dot(grad_one_low.T, attn_low[:flat_rows], preferred_element_type=wide_type)
     grad_attn = (
         jnp.dot(grad_one_low, self_out.T, preferred_element_type=wide_type)
         .astype(low_type)
@@ -943,13 +1186,11 @@
             got_kv,
             attn_turned,
             self_totals,
-            jnp.pad(grad_attn.reshape(flat_rows, local_width), ((0, query_pad), (0, 0))),
+            pad_queries(grad_attn.reshape(flat_rows, local_width)),
             clip_lengths,
             flat_rows,
             11,
         )
-        query_grads = query_grads[:flat_rows].reshape(head_shape)
-        kv_grads = kv_grads[:, :flat_rows]
     else:
         query_grads = []
         key_grads = []
@@ -988,34 +1229,25 @@
             scatter_dimension=0,
             tiled=True,
         )[:flat_rows].astype(jnp.float32)
-        kv_grads = (kv_rows[:, :local_width], kv_rows[:, local_width:])
-        query_grads = jnp.stack(query_grads, axis=2)
+        kv_grads = jnp.stack(
+            [pad_queries(kv_rows[:, :local_width]), pad_queries(kv_rows[:, local_width:])]
+        )
+        query_grads = pad_queries(
+            jnp.stack(query_grads, axis=2).reshape(flat_rows, local_width)
+        )
     query_grads, part_ffn_in = lax.optimization_barrier((query_grads, part_ffn_in))
-    rotate_back = jax.vjp(rotate_now, query_norm)[1]
-    grad_query_norm = rotate_back(query_grads)[0].reshape(flat_rows, local_width)
-    grad_key_norm = rotate_back(kv_grads[0].reshape(head_shape))[0].reshape(flat_rows, local_width)
-    query_back, key_back = small_sum(
-        [
-            jnp.sum(grad_query_norm * norm_gains[0] * query_pre, axis=-1),
-            jnp.sum(grad_key_norm * norm_gains[1] * key_pre, axis=-1),
-        ],
+    *grad_proj_low, proj_sums = unproject(
+        query_grads,
+        kv_grads,
+        proj_pre,
+        proj_squares,
+        self_gains,
+        cosine_flat,
+        sine_flat,
+        model_width,
         9,
     )
-    grad_query_pre = (
-        grad_query_norm * norm_gains[0] * query_rate
-        - query_pre * query_rate**3 * query_back[:, None] / model_width
-    )
-    grad_key_pre = (
-        grad_key_norm * norm_gains[1] * key_rate
-        - key_pre * key_rate**3 * key_back[:, None] / model_width
-    )
-    gain_query = jnp.sum(grad_query_norm * query_pre * query_rate, axis=0)
-    gain_key = jnp.sum(grad_key_norm * key_pre * key_rate, axis=0)
-    grad_proj = jnp.stack(
-        [grad_query_pre, grad_key_pre, kv_grads[1].reshape(flat_rows, local_width)]
-    )
-    grad_self_bias = jnp.sum(grad_proj, axis=1)
-    grad_proj_low = grad_proj.astype(low_type)
+    grad_self_bias = proj_sums[:3]
     self_in_mix = jnp.concatenate(
         [
             jnp.dot(attn_in.T, grad_proj_low[j], preferred_element_type=wide_type).astype(low_type)
@@ -1027,7 +1259,7 @@
         (grad_proj_low, self_in_mix, part_group)
     )
     part_self_in = scatter_rows(self_in_mix, 0)
-    grad_attn_in = line_sum([(grad_proj_low[j], self_in[j]) for j in range(3)], True, 5)
+    grad_attn_in = line_sum([(grad_proj_low[j], self_in[j]) for j in range(3)], True, 5, flat_rows)
     grad_hidden = (
         grad_after_one + jax.vjp(layer_norm, hidden_rows)[1](grad_attn_in * (1.0 + scale_one))[0]
     )
@@ -1053,7 +1285,9 @@
         jnp.sum(residue * residue),
     )
     grad_time_local, grad_cross_gain, grad_cross_shift, grad_out_bias, square_local = stream_values
-    grad_norm_gains = jnp.stack([gain_query, gain_key, gain_cross_query, gain_text_key])
+    grad_norm_gains = jnp.concatenate(
+        [proj_sums[3:5], gain_cross_query[None], gain_text_key[None]]
+    )
     time_pair, sums = plane_sum(
         grad_time_local,
         [

time: 1230 us -> 1100 us (0.89)
  local copies, waits for them, and re-layouts: 257 us -> 193 us
  Pallas kernels: 618 us -> 585 us
  matrix products: 141 us -> 122 us
    pallas_call x0 -> x3, Pallas kernels: none -> 42.8 us  [the longest x1 17.6 us: project(): pl.pallas_call(project_kernel, out_shape=(jax.ShapeDtypeStruct((2, rows,...]
    pallas_call x1, Pallas kernels: 87.4 us -> 51.8 us  [attend_back(): pl.pallas_call(functools.partial(attend_back_kernel, true_rows), out_shap...]
    dot_general x6 -> x1, matrix products: 25.5 us -> 2.6 us  [shards(): jnp.dot(grad_one_low.T, attn_low[:flat_rows], preferred_element_type=wide...]
    pallas_call x5 -> x2, Pallas kernels: 36.1 us -> 13.9 us  [small_sum(): pl.pallas_call(small_kernel, out_shape=jax.ShapeDtypeStruct((lines, 128),...]
    unnamed x325 -> x246, local copies, waits for them, and re-layouts: 115 us -> 93.6 us
    pallas_call x6, Pallas kernels: 434 us -> 415 us  [line_sum(): pl.pallas_call(functools.partial(line_kernel, len(pairs), block, group, l...]
    slice x9 -> x4, local copies, waits for them, and re-layouts: 20.4 us -> 3.93 us  [the longest x1 1.5 us: shards(): out_bias[2]]
    reshape x7 -> x1, local copies, waits for them, and re-layouts: 15 us -> 1.45 us  [shards(): jnp.transpose(text_blocks, (2, 1, 3, 0, 4))]
  transfers between devices with their start and end apart: 7 -> 6, of which waited for: 2 -> 1; matrix products, arithmetic and copies ran while one was open for 25% -> 27% of each run, Pallas kernels for 25% -> 33%
where the time goes in v4:
time: 1100 us; the launch traced here: 1090 us
  Pallas kernels  585 us (53%)
  local copies, waits for them, and re-layouts  193 us (18%)
  matrix products  122 us (11%)
  other arithmetic  121 us (11%)
  waiting for transfers between devices  52.9 us (5%)
  between operations  18.6 us (2%)
    pallas_call x6, Pallas kernels, line_sum(): pl.pallas_call(functools.partial(line_kernel, len(pairs), block, group, l...  415 us
    unnamed x246, local copies, waits for them, and re-layouts  93.6 us
    unnamed x10, waiting for transfers between devices  52.9 us
    pallas_call x1, Pallas kernels, attend_back(): pl.pallas_call(functools.partial(attend_back_kernel, true_rows), out_shap...  51.8 us
    pallas_call x1, Pallas kernels, attend(): pl.pallas_call(functools.partial(attend_kernel, true_rows), out_shape=(ja...  51.7 us
    reduce_sum x5, other arithmetic, layer_norm(): centred = values - jnp.mean(values, axis=-1, keepdims=True)  26 us
    dot_general x6, matrix products, per_clip(): return jnp.dot(clip_table.T, values, precision=lax.Precision.HIGHEST)  23 us
  transfers between devices with their start and end apart: 6, of which 1 were waited for; matrix products, arithmetic and copies ran while one was open for 27% of the time, Pallas kernels for 33%

profile of v4, /device:TPU:0, one launch (start us, length us, event | category | flops | bytes accessed | tf_op | source)
XLA Modules:
  0.0 1093.0 jit_solution(5783698664377929733)
XLA Ops:
  18.2 6.6 reduce_sum.315
  24.8 3.0 multiply_reduce_fusion.5
  31.0 9.8 copy.103.refs_1_
  42.7 3.6 add_convert_fusion.2
  50.2 17.6 %project.1 = (f32[2,896,384]{2,1,0:T(8,128)}, bf16[896,384]{1,0:T(8,128)(2,1)}, bf16[2,784,384]{2,1,0:T(8,128)(2,1)}, f32[8,896]{1,0:T(8,128)}) custom-call(bf16[896,1536]{1,0:T(8,128)(2,1)} %pad.41.rows_ref, bf16[3,1536,384]{2,1,0:T(8,128)(2,1)} %weight_ref.1, f32[3,384]{1,0:T(4,128)} %bias_ref.1, f32[2,384]{1,0:T(2,128)} %slice.241.gain_ref, ...), custom_call_target="tpu_custom_call" | custom-call | tf_op jit(solution)/shard_map/project/pallas_call | solution.py:713
  67.8 51.7 %attend.1 = (bf16[896,384]{1,0:T(8,128)(2,1)}, f32[3,128,896]{2,1,0:T(8,128)}, f32[3,1,896]{2,1,0:T(1,128)}, bf16[3,2,784,384]{3,2,1,0:T(8,128)(2,1)}) custom-call(s32[1]{0:T(128)} %dynamic_slice.9.length_ref, bf16[896,384]{1,0:T(8,128)(2,1)} %get-tuple-element.50.query_ref, bf16[2,784,384]{2,1,0:T(8,128)(2,1)} %get-tuple-element.51.kv_ref), custom_call_target="tpu_custom_call" | custom-call | flops 1000000000 | bytes 150000000 | tf_op jit(solution)/shard_map/attend/pallas_call | solution.py:474
  119.5 70.5 %line_sum_0.1 = bf16[784,1536]{1,0:T(8,128)(2,1)} custom-call(bf16[896,384]{1,0:T(8,128)(2,1)} %get-tuple-element.52.refs_0_, bf16[384,1536]{1,0:T(8,128)(2,1)} %refs_1_.5), custom_call_target="tpu_custom_call" | custom-call | flops 924844032 | bytes 230000000 | tf_op jit(solution)/shard_map/line_sum_0/pallas_call | solution.py:191
  190.0 4.2 fusion.144
  197.8 2.5 multiply_reduce_fusion.11
  200.3 2.8 fusion.40
  205.1 7.1 small_sum_7.1
  216.8 2.3 multiply_convert_fusion.4
  237.3 67.0 %line_sum_1.1 = bf16[784,1536]{1,0:T(8,128)(2,1)} custom-call(bf16[784,384]{1,0:T(8,128)(2,1)} %pad.45.refs_0_, bf16[384,1536]{1,0:T(8,128)(2,1)} %refs_1_.6), custom_call_target="tpu_custom_call" | custom-call | flops 924844032 | bytes 230000000 | tf_op jit(solution)/shard_map/line_sum_1/pallas_call | solution.py:191
  304.4 4.0 fusion.143
  309.9 10.5 multiply_convert_fusion
  320.4 4.1 pad.46.refs_0_
  324.5 68.4 %line_sum_2.1 = bf16[784,1536]{1,0:T(8,128)(2,1)} custom-call(bf16[784,2240]{1,0:T(8,128)(2,1)} %pad.46.refs_0_, bf16[2240,1536]{1,0:T(8,128)(2,1)} %refs_1_.7), custom_call_target="tpu_custom_call" | custom-call | flops 5394923520 | bytes 230000000 | tf_op jit(solution)/shard_map/line_sum_2/pallas_call | solution.py:191
  392.9 7.0 fusion.13
  399.9 9.4 convolution_convert_fusion.1
  409.3 15.2 %fusion.146 = (bf16[2240]{0:T(1024)(128)(2,1)}, bf16[780,2240]{1,0:T(8,128)(2,1)S(1)}) fusion(bf16[2240,1536]{1,0:T(8,128)(2,1)} %refs_1_.7, f32[780,1536]{1,0:T(8,128)S(1)} %get-tuple-element.181, f32[1536]{0:T(1024)S(1)} %copy-done.49, f32[780]{0:T(1024)S(1)} %get-tuple-element.227, f32[780,2240]{1,0:T(8,128)} %get-tuple-element.218, ...), kind=kOutput, calls=%fused_computation.312 | convolution fusion | flops 5416412160 | bytes 22179504 | tf_op jit(solution)/shard_map/dot_general | solution.py:1067
  428.4 72.9 %line_sum_3.1 = bf16[784,1536]{1,0:T(8,128)(2,1)} custom-call(bf16[784,2240]{1,0:T(8,128)(2,1)} %pad.47.refs_0_, bf16[1536,2240]{1,0:T(8,128)(2,1)} %copy.103.refs_1_), custom_call_target="tpu_custom_call" | custom-call | flops 5394923520 | bytes 230000000 | tf_op jit(solution)/shard_map/line_sum_3/pallas_call | solution.py:191
  501.3 4.6 multiply_reduce_fusion.2
  505.9 6.3 fusion.142
  512.9 9.6 copy.131
  525.0 5.7 fusion.138
  530.7 2.5 copy-done.13
  561.5 11.2 %seq_scatter.1 = f32[128,768]{1,0:T(8,128)} custom-call(bf16[4,128,768]{2,1,0:T(8,128)(2,1)} %copy.130.blocks_ref), custom_call_target="tpu_custom_call" | custom-call | tf_op jit(solution)/shard_map/seq_scatter/pallas_call | solution.py:839
  578.5 2.8 copy.108
  581.3 2.8 copy.109
  587.8 6.9 small_sum_8.1
  597.9 3.2 fusion.25
  601.2 3.0 fusion.139
  604.2 5.0 fusion.28
  609.2 10.0 convolution_convert_fusion
  619.3 2.3 copy.132
  623.7 64.4 %line_sum_4.1 = bf16[784,1536]{1,0:T(8,128)(2,1)} custom-call(bf16[784,384]{1,0:T(8,128)(2,1)} %pad.49.refs_0_, bf16[1536,384]{1,0:T(8,128)(2,1)} %refs_1_.8), custom_call_target="tpu_custom_call" | custom-call | flops 924844032 | bytes 230000000 | tf_op jit(solution)/shard_map/line_sum_4/pallas_call | solution.py:191
  688.1 4.2 fusion.7
  692.4 4.9 fusion.9
  697.3 3.8 add_add_fusion.3
  703.3 2.3 convolution_convert_fusion.9
  707.8 4.4 fusion.27
  712.2 2.6 fusion.26
  717.1 8.6 copy.135
  725.8 9.8 copy.133
  737.6 4.3 slice_bitcast_fusion.2
  741.9 9.6 copy.118
  751.5 2.3 fusion.76
  754.4 5.5 fusion.89
  771.3 5.5 fusion.82
  779.0 51.8 %attend_back.1 = (f32[896,384]{1,0:T(8,128)}, f32[2,896,384]{2,1,0:T(8,128)}) custom-call(s32[1]{0:T(128)} %dynamic_slice.9.length_ref, bf16[896,384]{1,0:T(8,128)(2,1)} %get-tuple-element.50.query_ref, bf16[2,784,384]{2,1,0:T(8,128)(2,1)} %get-tuple-element.51.kv_ref, bf16[3,2,784,384]{3,2,1,0:T(8,128)(2,1)} %get-tuple-element.53.got_ref, ...), custom_call_target="tpu_custom_call" | custom-call | flops 1000000000 | bytes 200000000 | tf_op jit(solution)/shard_map/attend_back/pallas_call | solution.py:590
  831.8 2.3 copy.136
  834.2 52.8 %reduce-scatter.15.cloned.1.call-done = bf16[192,2240]{1,0:T(8,128)(2,1)} async-done(((bf16[1536,2240]{1,0:T(8,128)(2,1)}), bf16[192,2240]{1,0:T(8,128)(2,1)}) %reduce-scatter.15.cloned.1.call-update) | async-done | bytes 860176
  888.9 13.9 %unproject.1 = (bf16[896,384]{1,0:T(8,128)(2,1)}, bf16[896,384]{1,0:T(8,128)(2,1)}, bf16[896,384]{1,0:T(8,128)(2,1)}, f32[8,384]{1,0:T(8,128)}) custom-call(f32[896,384]{1,0:T(8,128)} %get-tuple-element.62.query_grad_ref, f32[2,896,384]{2,1,0:T(8,128)} %get-tuple-element.63.kv_grad_ref, f32[2,896,384]{2,1,0:T(8,128)} %get-tuple-element.64.pre_ref, ...), custom_call_target="tpu_custom_call" | custom-call | tf_op jit(solution)/shard_map/unproject/pallas_call | solution.py:784
  904.8 2.5 convolution_convert_fusion.3
  912.1 5.8 copy.137
  917.9 72.3 %line_sum_5.1 = bf16[784,1536]{1,0:T(8,128)(2,1)} custom-call(bf16[896,384]{1,0:T(8,128)(2,1)} %get-tuple-element.70.refs_0_, bf16[896,384]{1,0:T(8,128)(2,1)} %get-tuple-element.71.refs_1_, bf16[896,384]{1,0:T(8,128)(2,1)} %get-tuple-element.72.refs_2_, bf16[1536,384]{1,0:T(8,128)(2,1)} %get-tuple-element.186.refs_3_, ...), custom_call_target="tpu_custom_call" | custom-call | flops 2774532096 | bytes 230000000 | tf_op jit(solution)/shard_map/line_sum_5/pallas_call | solution.py:191
  993.0 5.5 fusion.88
  1004.5 8.3 multiply_reduce_fusion.1
  1013.5 7.1 concatenate.53
  1022.0 9.8 plane_sum.1
  1037.9 4.9 fusion.137
  1042.8 5.1 add_bitcast_fusion
  1047.9 9.5 copy.119
  1060.7 2.4 convert_bitcast_fusion
  (419 shorter events, 172.4 us)
Async XLA Ops:
  7.2 193.1 %copy-start = (bf16[2,1536,384]{2,1,0:T(8,128)(2,1)S(1)}, bf16[2,1536,384]{2,1,0:T(8,128)(2,1)}, u32[]{:S(2)}) copy-start(bf16[2,1536,384]{2,1,0:T(8,128)(2,1)} %param.35) | copy-start | bytes 7077892
  7.2 193.1 %all-gather.2.cloned.1.call-start = ((), (), s32[]{:S(2)}) async-start(), calls=%async_computation.4 | async-start | bytes 1966080 | tf_op jit(solution)/shard_map/all_gather | solution.py:1013
  9.3 610.0 %reduce-scatter.13.cloned.1.call-start = ((), (), s32[]{:S(2)}) async-start(), calls=%async_computation.6 | async-start | bytes 7962624
  16.7 26.0 %copy-start.44 = (f32[1536]{0:T(1024)}, f32[1536]{0:T(1024)S(1)}, u32[]{:S(2)}) copy-start(f32[1536]{0:T(1024)S(1)} %get-tuple-element.154) | copy-start | bytes 18436
  16.7 173.3 %copy-start.55 = (f32[1536]{0:T(1024)}, f32[1536]{0:T(1024)S(1)}, u32[]{:S(2)}) copy-start(f32[1536]{0:T(1024)S(1)} %get-tuple-element.152) | copy-start | bytes 18436
  18.2 171.8 %copy-start.53 = (f32[1536]{0:T(1024)}, f32[1536]{0:T(1024)S(1)}, u32[]{:S(2)}) copy-start(f32[1536]{0:T(1024)S(1)} %get-tuple-element.156) | copy-start | bytes 18436
  18.2 9.7 copy-start.91
  24.8 17.8 %copy-start.40 = (f32[780]{0:T(1024)}, f32[780]{0:T(1024)S(1)}, u32[]{:S(2)}) copy-start(f32[780]{0:T(1024)S(1)} %broadcast_multiply_fusion.5) | copy-start | bytes 9364
  27.8 13.0 %copy-start.72 = (f32[780]{0:T(1024)}, f32[780]{0:T(1024)S(1)}, u32[]{:S(2)}) copy-start(f32[780]{0:T(1024)S(1)} %multiply_reduce_fusion.5) | copy-start | bytes 9364
  27.8 14.8 %copy-start.57 = (f32[780]{0:T(1024)}, f32[780]{0:T(1024)S(1)}, u32[]{:S(2)}) copy-start(f32[780]{0:T(1024)S(1)} %fusion.117) | copy-start | bytes 9364
  31.0 9.8 copy-start.102
  31.0 11.6 %copy-start.78 = (f32[1536]{0:T(1024)S(1)}, f32[1536]{0:T(1024)}, u32[]{:S(2)}) copy-start(f32[1536]{0:T(1024)} %get-tuple-element.153) | copy-start | bytes 18436
  42.6 6.7 copy-start.98
  200.3 16.4 %copy-start.79 = (f32[384]{0:T(512)S(1)}, f32[384]{0:T(512)}, u32[]{:S(2)}) copy-start(f32[384]{0:T(512)} %get-tuple-element.162) | copy-start | bytes 4612
  214.8 12.2 %copy-start.59 = (f32[780]{0:T(1024)}, f32[780]{0:T(1024)S(1)}, u32[]{:S(2)}) copy-start(f32[780]{0:T(1024)S(1)} %get-tuple-element.206) | copy-start | bytes 9364
  235.4 69.0 %copy-start.77 = (f32[1536]{0:T(1024)S(1)}, f32[1536]{0:T(1024)}, u32[]{:S(2)}) copy-start(f32[1536]{0:T(1024)} %get-tuple-element.157) | copy-start | bytes 18436
  308.3 12.0 %copy-start.2 = (f32[780,1536]{1,0:T(8,128)}, f32[780,1536]{1,0:T(8,128)S(1)}, u32[]{:S(2)}) copy-start(f32[780,1536]{1,0:T(8,128)S(1)} %get-tuple-element.178) | copy-start | bytes 14376964
  309.0 196.9 %copy-start.64 = (f32[780]{0:T(1024)}, f32[780]{0:T(1024)S(1)}, u32[]{:S(2)}) copy-start(f32[780]{0:T(1024)S(1)} %fusion.119) | copy-start | bytes 9364
  324.5 68.4 %copy-start.49 = (f32[1536]{0:T(1024)S(1)}, f32[1536]{0:T(1024)}, u32[]{:S(2)}) copy-start(f32[1536]{0:T(1024)} %get-tuple-element.150) | copy-start | bytes 18436
  324.5 68.4 %copy-start.95 = (pred[780]{0:T(1024)(128)(4,1)S(1)}, pred[780]{0:T(1024)(128)(4,1)}, u32[]{:S(2)}) copy-start(pred[780]{0:T(1024)(128)(4,1)} %get-tuple-element.226) | copy-start | bytes 2344
  392.9 7.0 copy-start.21
  399.9 9.4 copy-start.3
  522.5 242.6 %all-reduce.13.cloned.1.call-start = ((), (), s32[]{:S(2)}) async-start(), calls=%async_computation.5 | async-start | bytes 786432 | tf_op jit(solution)/shard_map/psum | solution.py:1158
  525.0 8.2 copy-start.33
  574.2 10.6 copy-start.26
  574.2 10.6 copy-start.30
  574.3 10.6 copy-start.76
  575.8 9.2 copy-start.60
  575.8 9.2 copy-start.80
  581.3 16.7 %copy-start.22 = (bf16[1,128,1536]{2,1,0:T(8,128)(2,1)S(1)}, bf16[1,128,1536]{2,1,0:T(8,128)(2,1)}, u32[]{:S(2)}) copy-start(bf16[1,128,1536]{2,1,0:T(8,128)(2,1)} %convert_element_type.301) | copy-start | bytes 1179652
  584.8 16.3 %copy-start.61 = (f32[780]{0:T(1024)S(1)}, f32[780]{0:T(1024)}, u32[]{:S(2)}) copy-start(f32[780]{0:T(1024)} %copy-done.59) | copy-start | bytes 9364
  584.8 16.3 %copy-start.81 = (f32[384]{0:T(512)S(1)}, f32[384]{0:T(512)}, u32[]{:S(2)}) copy-start(f32[384]{0:T(512)} %get-tuple-element.162) | copy-start | bytes 4612
  584.8 16.3 %copy-start.82 = (f32[780]{0:T(1024)S(1)}, f32[780]{0:T(1024)}, u32[]{:S(2)}) copy-start(f32[780]{0:T(1024)} %get-tuple-element.205) | copy-start | bytes 9364
  594.7 6.4 copy-start.90
  596.3 12.9 %slice-start.2 = ((s8[4816896]{0:T(1024)(128)(4,1)}), s8[622592]{0:T(1024)(128)(4,1)S(1)}, s32[]{:S(2)}) async-start(s8[4816896]{0:T(1024)(128)(4,1)} %bitcast.286), calls=%async_computation.12 | async-start | bytes 1245184
  601.1 8.1 slice-start.3
  601.1 8.1 copy-start.20
  601.1 8.1 copy-start.52
  601.1 8.1 copy-start.65
  601.2 8.1 copy-start.93
  619.2 68.8 %copy-start.43 = (f32[780]{0:T(1024)S(1)}, f32[780]{0:T(1024)}, u32[]{:S(2)}) copy-start(f32[780]{0:T(1024)} %copy-done.42) | copy-start | bytes 9364
  619.2 68.8 %copy-start.47 = (f32[1536]{0:T(1024)S(1)}, f32[1536]{0:T(1024)}, u32[]{:S(2)}) copy-start(f32[1536]{0:T(1024)} %param.32) | copy-start | bytes 18436
  619.3 212.6 %reduce-scatter.17.cloned.1.call-start = ((), (), s32[]{:S(2)}) async-start(), calls=%async_computation.8 | async-start | bytes 6635520
  621.7 75.6 %slice-start = ((s8[4816896]{0:T(1024)(128)(4,1)}), s8[622592]{0:T(1024)(128)(4,1)S(1)}, s32[]{:S(2)}) async-start(s8[4816896]{0:T(1024)(128)(4,1)} %bitcast.284), calls=%async_computation.10 | async-start | bytes 1245184
  623.7 68.6 %copy-start.75 = (f32[780]{0:T(1024)S(1)}, f32[780]{0:T(1024)}, u32[]{:S(2)}) copy-start(f32[780]{0:T(1024)} %copy-done.74) | copy-start | bytes 9364
  623.7 68.7 %copy-start.63 = (f32[780]{0:T(1024)S(1)}, f32[780]{0:T(1024)}, u32[]{:S(2)}) copy-start(f32[780]{0:T(1024)} %copy-done.62) | copy-start | bytes 9364
  688.1 9.2 slice-start.1
  705.5 6.6 slice-start.6
  725.8 161.2 %reduce-scatter.15.cloned.1.call-start = ((), (), s32[]{:S(2)}) async-start(), calls=%async_computation.7 | async-start | bytes 7962624
  735.6 342.8 %reduce-scatter.19.cloned.1.call-start = ((), (), s32[]{:S(2)}) async-start(), calls=%async_computation.9 | async-start | bytes 3981312
  741.9 18.5 %slice-start.4 = ((s8[4816896]{0:T(1024)(128)(4,1)}), s8[622592]{0:T(1024)(128)(4,1)S(1)}, s32[]{:S(2)}) async-start(s8[4816896]{0:T(1024)(128)(4,1)} %bitcast.288), calls=%async_computation.14 | async-start | bytes 1245184
  751.5 9.0 slice-start.5
  751.5 9.0 copy-start.16
  760.5 10.8 copy-start.54
  767.0 10.3 copy-start.18
  779.0 51.8 %copy-start.6 = (bf16[784,1536]{1,0:T(8,128)(2,1)S(1)}, bf16[784,1536]{1,0:T(8,128)(2,1)}, u32[]{:S(2)}) copy-start(bf16[784,1536]{1,0:T(8,128)(2,1)} %line_sum_4.1) | copy-start | bytes 7225348
  888.9 15.9 %copy-start.15 = (bf16[780,1536]{1,0:T(8,128)(2,1)S(1)}, bf16[780,1536]{1,0:T(8,128)(2,1)}, u32[]{:S(2)}) copy-start(bf16[780,1536]{1,0:T(8,128)(2,1)} %copy-done.14) | copy-start | bytes 7188484
  917.9 75.1 %copy-start.41 = (f32[780]{0:T(1024)S(1)}, f32[780]{0:T(1024)}, u32[]{:S(2)}) copy-start(f32[780]{0:T(1024)} %copy-done.40) | copy-start | bytes 9364
  917.9 75.1 %copy-start.58 = (f32[780]{0:T(1024)S(1)}, f32[780]{0:T(1024)}, u32[]{:S(2)}) copy-start(f32[780]{0:T(1024)} %copy-done.57) | copy-start | bytes 9364
  990.2 14.3 %copy-start.45 = (f32[1536]{0:T(1024)S(1)}, f32[1536]{0:T(1024)}, u32[]{:S(2)}) copy-start(f32[1536]{0:T(1024)} %copy-done.44) | copy-start | bytes 18436
  990.2 14.3 %copy-start.50 = (f32[1536]{0:T(1024)S(1)}, f32[1536]{0:T(1024)}, u32[]{:S(2)}) copy-start(f32[1536]{0:T(1024)} %get-tuple-element.150) | copy-start | bytes 18436
  1004.5 32.7 %copy-start.73 = (f32[780]{0:T(1024)S(1)}, f32[780]{0:T(1024)}, u32[]{:S(2)}) copy-start(f32[780]{0:T(1024)} %copy-done.72) | copy-start | bytes 9364
  1047.9 10.9 copy-start.39
  1060.7 16.5 %copy-start.48 = (f32[4608]{0:T(1024)S(1)}, f32[4608]{0:T(1024)}, u32[]{:S(2)}) copy-start(f32[4608]{0:T(1024)} %slice.341) | copy-start | bytes 55300
  (56 other events, 184.2 us)
Sparse Core Ops, SparseCore 0:
  9.9 33.5 all-gather.1
  522.6 67.4 reduce-scatter.12
  619.4 38.9 all-reduce.12
  725.9 92.1 reduce-scatter.16
  821.4 65.4 reduce-scatter.14
  918.0 47.8 reduce-scatter.18

commit v5 on v4

--- a/solution.py
+++ b/solution.py
@@ -6,6 +6,7 @@
 from jax import lax
 from jax.experimental import pallas as pl
 from jax.experimental.pallas import tpu as pltpu
+from jax.experimental.layout import Layout, with_layout_constraint
 from jax.sharding import PartitionSpec as P
 
 HEAD_DIM = 128
@@ -203,6 +204,10 @@
         cost_estimate=pl.CostEstimate(flops=2 * rows * width * depth, bytes_accessed=230 * 10**6, transcendentals=0),
         name=f"line_sum_{ident}",
     )(*[p[0] for p in pairs], *[p[1] for p in pairs])[:true_rows].astype(WIDE)
+
+def row_major(values):
+    return with_layout_constraint(values, Layout((0, 1)))
+
 
 def scatter_rows(mix, dimension):
     return lax.psum_scatter(mix, ("dp", "seq"), scatter_dimension=dimension, tiled=True)
@@ -849,6 +854,271 @@
         compiler_params=pltpu.CompilerParams(collective_id=ident, has_side_effects=True),
         name="seq_scatter",
     )(blocks)
+
+
+def head_sum(term):
+    def add(heads):
+        total = None
+        for head in range(heads):
+            piece = term(head, slice(head * HEAD_DIM, (head + 1) * HEAD_DIM))
+            total = piece if total is None else total + piece
+        return total
+
+    return add
+
+
+def cross_attend_kernel(
+    rows_ref, text_ref, query_weight_ref, text_weight_ref, bias_ref, gain_ref,
+    query_pre_ref, key_pre_ref, query_ref, kv_ref, square_ref, out_ref, turned_ref, total_ref,
+    stage, slots, send, recv,
+):
+    heads = query_ref.shape[1] // HEAD_DIM
+    width = rows_ref.shape[1]
+    factor = LOG2E / math.sqrt(HEAD_DIM)
+    tensor_barrier()
+    stage[...] = jnp.zeros(stage.shape, WIDE)
+    query_pre_ref[...] = (
+        jnp.dot(rows_ref[...], query_weight_ref[...], preferred_element_type=WIDE)
+        + bias_ref[0:1]
+    )
+    key_pre_ref[...] = (
+        jnp.dot(text_ref[...], text_weight_ref[0], preferred_element_type=WIDE) + bias_ref[1:2]
+    )
+    for part, pre_ref in enumerate((query_pre_ref, key_pre_ref)):
+        squares = head_sum(lambda head, lanes: pre_ref[:, lanes] * pre_ref[:, lanes])(heads)
+        stage[part : part + 1, : pre_ref.shape[0]] = rows_to_lanes(squares)
+    tensor_send(stage, slots, send, recv)
+    values = jnp.dot(text_ref[...], text_weight_ref[1], preferred_element_type=WIDE)
+    kv_ref[1] = (values + bias_ref[2:3]).astype(LOW)
+    total = tensor_collect(stage, slots, send, recv)
+    square_ref[...] = total
+    for part, pre_ref in enumerate((query_pre_ref, key_pre_ref)):
+        square = total[part : part + 1, : pre_ref.shape[0]]
+        rate = lanes_to_rows(lax.rsqrt(square / width + eps_norm))
+        for head in range(heads):
+            lanes = slice(head * HEAD_DIM, (head + 1) * HEAD_DIM)
+            normed = (pre_ref[:, lanes] * rate * gain_ref[part : part + 1, lanes]).astype(LOW)
+            if part == 0:
+                query_ref[:, lanes] = normed
+            else:
+                kv_ref[0, :, lanes] = normed
+
+    def step(head, carry):
+        lanes = head_lanes(head)
+        scores = over_last(kv_ref[0, :, lanes], query_ref[:, lanes]) * factor
+        peak = jnp.max(scores, axis=0, keepdims=True)
+        terms = jnp.exp2(scores - peak)
+        summed = jnp.sum(terms, axis=0, keepdims=True)
+        attended = (
+            lax.dot_general(
+                kv_ref[1, :, lanes],
+                terms.astype(LOW),
+                (((0,), (0,)), ((), ())),
+                preferred_element_type=WIDE,
+            )
+            / summed
+        )
+        turned_ref[head] = attended
+        out_ref[:, lanes] = jnp.transpose(attended).astype(LOW)
+        total_ref[head] = peak + jnp.log2(summed)
+        return carry
+
+    lax.fori_loop(0, heads, step, 0)
+
+
+def cross_attend(rows_low, text_all, query_weight, text_weights, bias, gains, ident):
+    rows = rows_low.shape[0]
+    tokens = text_all.shape[0]
+    width = query_weight.shape[1]
+    heads = width // HEAD_DIM
+    count = lax.axis_size("tensor")
+    vmem = pl.BlockSpec(memory_space=pltpu.VMEM)
+    dma = pltpu.SemaphoreType.DMA
+    return pl.pallas_call(
+        cross_attend_kernel,
+        out_shape=(
+            jax.ShapeDtypeStruct((rows, width), WIDE),
+            jax.ShapeDtypeStruct((tokens, width), WIDE),
+            jax.ShapeDtypeStruct((rows, width), LOW),
+            jax.ShapeDtypeStruct((2, tokens, width), LOW),
+            jax.ShapeDtypeStruct((8, rows), WIDE),
+            jax.ShapeDtypeStruct((rows, width), LOW),
+            jax.ShapeDtypeStruct((heads, HEAD_DIM, rows), WIDE),
+            jax.ShapeDtypeStruct((heads, 1, rows), WIDE),
+        ),
+        in_specs=[vmem] * 6,
+        out_specs=(vmem,) * 8,
+        scratch_shapes=[
+            pltpu.VMEM((8, rows), WIDE),
+            pltpu.VMEM((count, 8, rows), WIDE),
+            dma((count - 1,)),
+            dma((count - 1,)),
+        ],
+        compiler_params=pltpu.CompilerParams(
+            collective_id=ident, has_side_effects=True, vmem_limit_bytes=56 << 20
+        ),
+        name="cross_attend",
+    )(rows_low, text_all, query_weight, text_weights, bias, gains)
+
+
+def cross_back_kernel(
+    width, query_ref, kv_ref, turned_ref, total_ref, grad_ref, query_pre_ref, key_pre_ref,
+    square_ref, text_square_ref, gain_ref, query_low_ref, text_low_ref, sums_ref,
+    centre, query_turned, work, text_work, leaving, landing, stage, slots, text_send, text_recv,
+    send, recv,
+):
+    heads = query_ref.shape[1] // HEAD_DIM
+    tokens = key_pre_ref.shape[0]
+    scale = 1.0 / math.sqrt(HEAD_DIM)
+    places = plane_places()
+    count = slots.shape[0]
+    mine = lax.axis_index("tensor")
+    barrier = pltpu.get_barrier_semaphore()
+    for place in places[1:]:
+        pl.semaphore_signal(
+            barrier, inc=1, device_id={"seq": place}, device_id_type=pl.DeviceIdType.MESH
+        )
+    for hop in range(1, count):
+        pl.semaphore_signal(
+            barrier, inc=1, device_id={"tensor": lax.rem(mine + hop, count)},
+            device_id_type=pl.DeviceIdType.MESH)
+    pl.semaphore_wait(barrier, 3 + count - 1)
+
+    for head in range(heads):
+        lanes = slice(head * HEAD_DIM, (head + 1) * HEAD_DIM)
+        grads = jnp.transpose(grad_ref[:, lanes].astype(WIDE))
+        centre[head] = jnp.sum(grads * turned_ref[head], axis=0, keepdims=True)
+    stage[...] = jnp.zeros(stage.shape, WIDE)
+    sums_ref[...] = jnp.zeros(sums_ref.shape, WIDE)
+
+    def step(head, carry):
+        lanes = head_lanes(head)
+        keys = kv_ref[0, :, lanes]
+        query = query_ref[:, lanes]
+        grads = grad_ref[:, lanes]
+        probs = jnp.exp2(over_last(keys, query) * (scale * LOG2E) - total_ref[head])
+        grad_probs = over_last(kv_ref[1, :, lanes], grads)
+        grad_scores = (probs * (grad_probs - centre[head])).astype(LOW)
+        key_grads = jnp.dot(grad_scores, query, preferred_element_type=WIDE) * scale
+        leaving[0, :, lanes] = key_grads.astype(LOW)
+        value_grads = jnp.dot(probs.astype(LOW), grads, preferred_element_type=WIDE)
+        leaving[1, :, lanes] = value_grads.astype(LOW)
+        query_turned[head] = lax.dot_general(
+            keys, grad_scores, (((0,), (0,)), ((), ())), preferred_element_type=WIDE
+        )
+        return carry
+
+    lax.fori_loop(0, heads, step, 0)
+
+    def owned(place):
+        return pl.ds(pl.multiple_of(place * tokens, 16), tokens)
+
+    def text_copy(relation, part):
+        place = places[relation + 1]
+        return plane_copy(
+            leaving.at[part, owned(place)],
+            landing.at[relation, part],
+            text_send.at[relation, part],
+            text_recv.at[relation, part],
+            place,
+        )
+
+    for relation in (2, 1, 0):
+        for part in range(2):
+            text_copy(relation, part).start()
+
+    rate_row = lax.rsqrt(square_ref[0:1] / width + eps_norm)
+    rate = lanes_to_rows(rate_row)
+    terms = None
+    for head in range(heads):
+        lanes = slice(head * HEAD_DIM, (head + 1) * HEAD_DIM)
+        grads = jnp.transpose(query_turned[head]) * scale
+        pre = query_pre_ref[:, lanes]
+        sums_ref[3:4, lanes] = jnp.sum(grads * pre * rate, axis=0, keepdims=True)
+        grads = grads * gain_ref[0:1, lanes]
+        work[:, lanes] = grads
+        terms = grads * pre if terms is None else terms + grads * pre
+    stage[0:1] = rows_to_lanes(terms)
+
+    for relation in range(3):
+        for part in range(2):
+            text_copy(relation, part).wait_recv()
+    for part in range(2):
+        total = leaving[part, owned(places[0])].astype(WIDE)
+        for relation in range(3):
+            total = total + landing[relation, part].astype(WIDE)
+        text_work[part] = total
+    text_row = lax.rsqrt(text_square_ref[0:1] / width + eps_norm)
+    text_rate = lanes_to_rows(text_row)
+    terms = None
+    for head in range(heads):
+        lanes = slice(head * HEAD_DIM, (head + 1) * HEAD_DIM)
+        grads = text_work[0, :, lanes]
+        pre = key_pre_ref[:, lanes]
+        sums_ref[4:5, lanes] = jnp.sum(grads * pre * text_rate, axis=0, keepdims=True)
+        grads = grads * gain_ref[1:2, lanes]
+        text_work[0, :, lanes] = grads
+        terms = grads * pre if terms is None else terms + grads * pre
+    stage[1:2, :tokens] = rows_to_lanes(terms)
+
+    tensor_send(stage, slots, send, recv)
+    sums_ref[2:3] = jnp.sum(text_work[1], axis=0, keepdims=True)
+    text_low_ref[1] = text_work[1].astype(LOW)
+    back_total = tensor_collect(stage, slots, send, recv)
+    back = lanes_to_rows(rate_row * rate_row * rate_row * back_total[0:1] / width)
+    text_back = lanes_to_rows(text_row * text_row * text_row * back_total[1:2, :tokens] / width)
+    for head in range(heads):
+        lanes = slice(head * HEAD_DIM, (head + 1) * HEAD_DIM)
+        grads = work[:, lanes] * rate - query_pre_ref[:, lanes] * back
+        sums_ref[0:1, lanes] = jnp.sum(grads, axis=0, keepdims=True)
+        query_low_ref[:, lanes] = grads.astype(LOW)
+        grads = text_work[0, :, lanes] * text_rate - key_pre_ref[:, lanes] * text_back
+        sums_ref[1:2, lanes] = jnp.sum(grads, axis=0, keepdims=True)
+        text_low_ref[0, :, lanes] = grads.astype(LOW)
+    for relation in range(3):
+        for part in range(2):
+            text_copy(relation, part).wait_send()
+
+
+def cross_back(saved, grad_low, key_pre_own, text_squares, gains, model_width, ident):
+    query_pre, _, query_low, kv_low, squares, _, turned, total = saved
+    rows, width = query_low.shape
+    heads = width // HEAD_DIM
+    tokens = key_pre_own.shape[0]
+    count = lax.axis_size("tensor")
+    vmem = pl.BlockSpec(memory_space=pltpu.VMEM)
+    dma = pltpu.SemaphoreType.DMA
+    return pl.pallas_call(
+        functools.partial(cross_back_kernel, model_width),
+        out_shape=(
+            jax.ShapeDtypeStruct((rows, width), LOW),
+            jax.ShapeDtypeStruct((2, tokens, width), LOW),
+            jax.ShapeDtypeStruct((8, width), WIDE),
+        ),
+        in_specs=[vmem] * 10,
+        out_specs=(vmem,) * 3,
+        scratch_shapes=[
+            pltpu.VMEM((heads, 1, rows), WIDE),
+            pltpu.VMEM((heads, HEAD_DIM, rows), WIDE),
+            pltpu.VMEM((rows, width), WIDE),
+            pltpu.VMEM((2, tokens, width), WIDE),
+            pltpu.VMEM(kv_low.shape, LOW),
+            pltpu.VMEM((3, 2, tokens, width), LOW),
+            pltpu.VMEM((8, rows), WIDE),
+            pltpu.VMEM((count, 8, rows), WIDE),
+            dma((3, 2)),
+            dma((3, 2)),
+            dma((count - 1,)),
+            dma((count - 1,)),
+        ],
+        compiler_params=pltpu.CompilerParams(
+            collective_id=ident, has_side_effects=True, vmem_limit_bytes=56 << 20
+        ),
+        name="cross_back",
+    )(
+        query_low, kv_low, turned, total, grad_low, query_pre, key_pre_own, squares, text_squares,
+        gains,
+    )
 
 
 def head_forward(query, keys, values, key_ok, score_scale):
@@ -1007,46 +1277,54 @@
     after_one = hidden_rows + branch_one * gate_one
     normed_three = layer_norm(after_one)
     cross_in = (normed_three * cross_gain + cross_shift).astype(low_type)
-    cross_query_pre = jnp.dot(cross_in, cross_q, preferred_element_type=wide_type) + cross_bias[0]
     text_low = text.astype(low_type)
     text_start = seq_place * text_local
     text_all = lax.all_gather(text_low, "seq", axis=1, tiled=True)
-    text_proj = (
-        jnp.einsum("ctd,kde->kcte", text_all, cross_kv, preferred_element_type=wide_type)
-        + cross_bias[1:, None, None, :]
-    )
-    cross_sq, text_sq = small_sum(
-        [
-            jnp.sum(cross_query_pre * cross_query_pre, axis=-1),
-            jnp.sum(text_proj[0] * text_proj[0], axis=-1),
-        ],
-        7,
-    )
-    text_rate_all = lax.rsqrt(text_sq / model_width + eps_norm)[..., None]
-    text_key_low = (text_proj[0] * text_rate_all * norm_gains[3]).astype(low_type)
-    text_value_low = text_proj[1].astype(low_type)
-    text_key_pre = lax.dynamic_slice_in_dim(text_proj[0], text_start, text_local, 1)
-    text_key_rate = lax.dynamic_slice_in_dim(text_rate_all, text_start, text_local, 1)
-    cross_rate = lax.rsqrt(cross_sq / model_width + eps_norm)[:, None]
-    cross_query_low = (
-        (cross_query_pre * cross_rate * norm_gains[2]).astype(low_type).reshape(head_shape)
-    )
-    text_key_heads = text_key_low.reshape(clip_count, text_count, local_heads, HEAD_DIM)
-    text_value_heads = text_value_low.reshape(clip_count, text_count, local_heads, HEAD_DIM)
-    cross_heads = []
-    cross_total_heads = []
-    for head_no in range(local_heads):
-        attended, log_total = head_forward(
-            cross_query_low[:, :, head_no],
-            text_key_heads[:, :, head_no],
-            text_value_heads[:, :, head_no],
-            text_valid,
-            score_scale,
-        )
-        cross_heads.append(attended)
-        cross_total_heads.append(log_total)
-    cross_att_low = jnp.stack(cross_heads, axis=2).astype(low_type).reshape(flat_rows, local_width)
-    cross_totals = jnp.stack(cross_total_heads)
+    cross_plane = plane and text_local % 128 == 0 and text_count <= flat_rows
+    if cross_plane:
+        cross_in = pad_queries(cross_in)
+        cross_saved = cross_attend(
+            cross_in, text_all[0], cross_q, cross_kv, cross_bias, norm_gains[2:], 7
+        )
+        cross_att_low = cross_saved[5]
+    else:
+        cross_query_pre = jnp.dot(cross_in, cross_q, preferred_element_type=wide_type) + cross_bias[0]
+        text_proj = (
+            jnp.einsum("ctd,kde->kcte", text_all, cross_kv, preferred_element_type=wide_type)
+            + cross_bias[1:, None, None, :]
+        )
+        cross_sq, text_sq = small_sum(
+            [
+                jnp.sum(cross_query_pre * cross_query_pre, axis=-1),
+                jnp.sum(text_proj[0] * text_proj[0], axis=-1),
+            ],
+            7,
+        )
+        text_rate_all = lax.rsqrt(text_sq / model_width + eps_norm)[..., None]
+        text_key_low = (text_proj[0] * text_rate_all * norm_gains[3]).astype(low_type)
+        text_value_low = text_proj[1].astype(low_type)
+        text_key_pre = lax.dynamic_slice_in_dim(text_proj[0], text_start, text_local, 1)
+        text_key_rate = lax.dynamic_slice_in_dim(text_rate_all, text_start, text_local, 1)
+        cross_rate = lax.rsqrt(cross_sq / model_width + eps_norm)[:, None]
+        cross_query_low = (
+            (cross_query_pre * cross_rate * norm_gains[2]).astype(low_type).reshape(head_shape)
+        )
+        text_key_heads = text_key_low.reshape(clip_count, text_count, local_heads, HEAD_DIM)
+        text_value_heads = text_value_low.reshape(clip_count, text_count, local_heads, HEAD_DIM)
+        cross_heads = []
+        cross_total_heads = []
+        for head_no in range(local_heads):
+            attended, log_total = head_forward(
+                cross_query_low[:, :, head_no],
+                text_key_heads[:, :, head_no],
+                text_value_heads[:, :, head_no],
+                text_valid,
+                score_scale,
+            )
+            cross_heads.append(attended)
+            cross_total_heads.append(log_total)
+        cross_att_low = jnp.stack(cross_heads, axis=2).astype(low_type).reshape(flat_rows, local_width)
+        cross_totals = jnp.stack(cross_total_heads)
     branch_two = (
         line_sum([(cross_att_low, cross_out)], False, 1, flat_rows)
         + out_bias[1]
@@ -1063,14 +1341,14 @@
     residue = jnp.where(valid_rows[:, None], result - teacher_rows, 0.0)
     grad_three = residue * gate_two
     grad_three_low = grad_three.astype(low_type)
-    ffn_out_mix = jnp.dot(act_low.T, grad_three_low, preferred_element_type=wide_type)
+    ffn_out_mix = jnp.dot(grad_three_low.T, act_low, preferred_element_type=wide_type)
     grad_act = jnp.dot(grad_three_low, ffn_out.T, preferred_element_type=wide_type)
     grad_pre = jax.vjp(gelu_tanh, pre_act)[1](grad_act)[0]
     grad_pre_low = grad_pre.astype(low_type)
     grad_pre_low, ffn_out_mix = lax.optimization_barrier(
-        (grad_pre_low, ffn_out_mix.astype(low_type))
-    )
-    part_ffn_out = scatter_rows(ffn_out_mix, 1)
+        (grad_pre_low, row_major(ffn_out_mix.astype(low_type)))
+    )
+    part_ffn_out = scatter_rows(ffn_out_mix, 0)
     ffn_in_mix = jnp.dot(ffn_input.T, grad_pre_low, preferred_element_type=wide_type)
     grad_ffn_bias = jnp.sum(grad_pre, axis=0)
     grad_ffn_input = line_sum([(grad_pre_low, ffn_in)], True, 3, flat_rows)
@@ -1078,80 +1356,99 @@
         residue + jax.vjp(layer_norm, after_two)[1](grad_ffn_input * (1.0 + scale_two))[0]
     )
     grad_two_low = grad_after_two.astype(low_type)
-    cross_out_mix = jnp.dot(grad_two_low.T, cross_att_low, preferred_element_type=wide_type)
+    cross_out_mix = jnp.dot(grad_two_low.T, cross_att_low[:flat_rows], preferred_element_type=wide_type)
     grad_cross_att = (
-        jnp.dot(grad_two_low, cross_out.T, preferred_element_type=wide_type)
-        .astype(low_type)
-        .reshape(head_shape)
-    )
-    cross_query_grads = []
-    text_key_grads = []
-    text_value_grads = []
-    for head_no in range(local_heads):
-        head_grads = head_backward(
-            cross_query_low[:, :, head_no],
-            text_key_heads[:, :, head_no],
-            text_value_heads[:, :, head_no],
-            text_valid,
-            cross_totals[head_no],
-            grad_cross_att[:, :, head_no],
-            score_scale,
-        )
-        cross_query_grads.append(head_grads[0])
-        text_key_grads.append(head_grads[2])
-        text_value_grads.append(head_grads[3])
-    grad_cross_query = jnp.stack(cross_query_grads, axis=2).reshape(flat_rows, local_width)
-    text_grads_all = jnp.stack(
-        [
-            jnp.stack(text_key_grads, axis=2).reshape(clip_count, text_count, local_width),
-            jnp.stack(text_value_grads, axis=2).reshape(clip_count, text_count, local_width),
+        jnp.dot(grad_two_low, cross_out.T, preferred_element_type=wide_type).astype(low_type)
+    )
+    if cross_plane:
+        grad_cross_query_low, text_grad_low, cross_sums = cross_back(
+            cross_saved,
+            pad_queries(grad_cross_att),
+            lax.dynamic_slice_in_dim(cross_saved[1], text_start, text_local, 0),
+            lax.dynamic_slice_in_dim(
+                jnp.broadcast_to(cross_saved[4][1:2, :text_count], (8, text_count)),
+                text_start,
+                text_local,
+                1,
+            ),
+            norm_gains[2:],
+            model_width,
+            8,
+        )
+        text_grad_low = text_grad_low[:, None]
+        grad_cross_bias = cross_sums[:3]
+        gain_cross_query = cross_sums[3]
+        gain_text_key = cross_sums[4]
+    else:
+        grad_cross_att = grad_cross_att.reshape(head_shape)
+        cross_query_grads = []
+        text_key_grads = []
+        text_value_grads = []
+        for head_no in range(local_heads):
+            head_grads = head_backward(
+                cross_query_low[:, :, head_no],
+                text_key_heads[:, :, head_no],
+                text_value_heads[:, :, head_no],
+                text_valid,
+                cross_totals[head_no],
+                grad_cross_att[:, :, head_no],
+                score_scale,
+            )
+            cross_query_grads.append(head_grads[0])
+            text_key_grads.append(head_grads[2])
+            text_value_grads.append(head_grads[3])
+        grad_cross_query = jnp.stack(cross_query_grads, axis=2).reshape(flat_rows, local_width)
+        text_grads_all = jnp.stack(
+            [
+                jnp.stack(text_key_grads, axis=2).reshape(clip_count, text_count, local_width),
+                jnp.stack(text_value_grads, axis=2).reshape(clip_count, text_count, local_width),
+            ]
+        )
+        text_blocks = text_grads_all.astype(low_type).reshape(
+            2, clip_count, seq_count, text_local, local_width
+        )
+        text_blocks = jnp.transpose(text_blocks, (2, 1, 3, 0, 4)).reshape(
+            seq_count, clip_count * text_local, 2 * local_width
+        )
+        text_rows = seq_scatter(text_blocks, 14)
+        text_grads = [
+            text_rows[:, j * local_width : (j + 1) * local_width].reshape(
+                clip_count, text_local, local_width
+            )
+            for j in range(2)
         ]
-    )
-    text_blocks = text_grads_all.astype(low_type).reshape(
-        2, clip_count, seq_count, text_local, local_width
-    )
-    text_blocks = jnp.transpose(text_blocks, (2, 1, 3, 0, 4)).reshape(
-        seq_count, clip_count * text_local, 2 * local_width
-    )
-    text_rows = seq_scatter(text_blocks, 14)
-    text_grads = [
-        text_rows[:, j * local_width : (j + 1) * local_width].reshape(
-            clip_count, text_local, local_width
-        )
-        for j in range(2)
-    ]
-    query_term, key_term = small_sum(
-        [
-            jnp.sum(grad_cross_query * norm_gains[2] * cross_query_pre, axis=-1),
-            jnp.sum(text_grads[0] * norm_gains[3] * text_key_pre, axis=-1),
-        ],
-        8,
-    )
-    grad_cross_query_pre = (
-        grad_cross_query * norm_gains[2] * cross_rate
-        - cross_query_pre * cross_rate**3 * query_term[:, None] / model_width
-    )
-    gain_cross_query = jnp.sum(grad_cross_query * cross_query_pre * cross_rate, axis=0)
-    grad_cross_query_low = grad_cross_query_pre.astype(low_type)
+        query_term, key_term = small_sum(
+            [
+                jnp.sum(grad_cross_query * norm_gains[2] * cross_query_pre, axis=-1),
+                jnp.sum(text_grads[0] * norm_gains[3] * text_key_pre, axis=-1),
+            ],
+            8,
+        )
+        grad_cross_query_pre = (
+            grad_cross_query * norm_gains[2] * cross_rate
+            - cross_query_pre * cross_rate**3 * query_term[:, None] / model_width
+        )
+        gain_cross_query = jnp.sum(grad_cross_query * cross_query_pre * cross_rate, axis=0)
+        grad_cross_query_low = grad_cross_query_pre.astype(low_type)
+        grad_text_key_pre = (
+            text_grads[0] * norm_gains[3] * text_key_rate
+            - text_key_pre * text_key_rate**3 * key_term[..., None] / model_width
+        )
+        gain_text_key = jnp.sum(text_grads[0] * text_key_pre * text_key_rate, axis=(0, 1))
+        grad_cross_bias = jnp.stack(
+            [
+                jnp.sum(grad_cross_query_pre, axis=0),
+                jnp.sum(grad_text_key_pre, axis=(0, 1)),
+                jnp.sum(text_grads[1], axis=(0, 1)),
+            ]
+        )
+        text_grad_low = jnp.stack([grad_text_key_pre, text_grads[1]]).astype(low_type)
     grad_cross_query_low, ffn_in_mix, part_ffn_out = lax.optimization_barrier(
-        (grad_cross_query_low, ffn_in_mix.astype(low_type), part_ffn_out)
+        (grad_cross_query_low, row_major(ffn_in_mix.astype(low_type)), part_ffn_out)
     )
     part_ffn_in = scatter_rows(ffn_in_mix, 0)
     cross_q_mix = jnp.dot(cross_in.T, grad_cross_query_low, preferred_element_type=wide_type)
     grad_cross_in = line_sum([(grad_cross_query_low, cross_q)], True, 4, flat_rows)
-    grad_text_key_pre = (
-        text_grads[0] * norm_gains[3] * text_key_rate
-        - text_key_pre * text_key_rate**3 * key_term[..., None] / model_width
-    )
-    gain_text_key = jnp.sum(text_grads[0] * text_key_pre * text_key_rate, axis=(0, 1))
-    grad_cross_bias = jnp.stack(
-        [
-            jnp.sum(grad_cross_query_pre, axis=0),
-            jnp.sum(grad_text_key_pre, axis=(0, 1)),
-            jnp.sum(text_grads[1], axis=(0, 1)),
-        ]
-    )
-    text_grad_low = jnp.stack([grad_text_key_pre, text_grads[1]]).astype(low_type)
     cross_kv_mix = jnp.einsum(
         "ctd,kcte->kde", text_low, text_grad_low, preferred_element_type=wide_type
     )
@@ -1177,7 +1474,7 @@
     group_mix = jnp.concatenate(
         [cross_out_mix, cross_q_mix, self_out_mix, cross_kv_mix[0], cross_kv_mix[1]], axis=-1
     ).astype(low_type)
-    grad_attn, group_mix = lax.optimization_barrier((grad_attn, group_mix))
+    grad_attn, group_mix = lax.optimization_barrier((grad_attn, row_major(group_mix)))
     part_group = scatter_rows(group_mix, 0)
     if plane:
         query_grads, kv_grads = attend_back(
@@ -1256,7 +1553,7 @@
         axis=-1,
     )
     grad_proj_low, self_in_mix, part_group = lax.optimization_barrier(
-        (grad_proj_low, self_in_mix, part_group)
+        (grad_proj_low, row_major(self_in_mix), part_group)
     )
     part_self_in = scatter_rows(self_in_mix, 0)
     grad_attn_in = line_sum([(grad_proj_low[j], self_in[j]) for j in range(3)], True, 5, flat_rows)
@@ -1316,7 +1613,7 @@
     ) = sums
     loss = square_sum / (valid_total * model_width)
     part_ffn_in = part_ffn_in.astype(wide_type)
-    part_ffn_out = part_ffn_out.astype(wide_type)
+    part_ffn_out = part_ffn_out.T.astype(wide_type)
     pieces = [
         part_group[:, j * local_width : (j + 1) * local_width].astype(wide_type) for j in range(5)
     ]

time: 1100 us -> 897 us (0.82)
  local copies, waits for them, and re-layouts: 193 us -> 82.7 us
  waiting for transfers between devices: 52.9 us -> 0.13 us
  other arithmetic: 121 us -> 84.4 us
  matrix products: 122 us -> 100 us
  Pallas kernels: 585 us -> 604 us
    unnamed x246 -> x118, local copies, waits for them, and re-layouts: 93.6 us -> 39.9 us
    unnamed x10 -> x6, waiting for transfers between devices: 52.9 us -> 0.1 us
    dot_general x22 -> x2, matrix products: 41.8 us -> 15.1 us  [the longest x1 9.8 us: shards(): jnp.dot(grad_three_low.T, act_low, preferred_element_type=wide_type)]
    pallas_call x3 -> x2, Pallas kernels: 25.1 us -> 38.2 us  [the longest x1 21.9 us: cross_back(): pl.pallas_call(functools.partial(cross_back_kernel, model_width), out_sha...]
  transfers between devices with their start and end apart: 6 -> 6, of which waited for: 1 -> 0; matrix products, arithmetic and copies ran while one was open for 27% -> 23% of each run, Pallas kernels for 33% -> 51%
where the time goes in v5:
time: 897 us; the launch traced here: 890 us
  Pallas kernels  604 us (67%)
  matrix products  100 us (11%)
  other arithmetic  84.4 us (9%)
  local copies, waits for them, and re-layouts  82.7 us (9%)
  between operations  18 us (2%)
    pallas_call x6, Pallas kernels, line_sum(): pl.pallas_call(functools.partial(line_kernel, len(pairs), block, group, l...  411 us
    pallas_call x1, Pallas kernels, attend_back(): pl.pallas_call(functools.partial(attend_back_kernel, true_rows), out_shap...  61.7 us
    pallas_call x1, Pallas kernels, attend(): pl.pallas_call(functools.partial(attend_kernel, true_rows), out_shape=(ja...  51.1 us
    unnamed x118, local copies, waits for them, and re-layouts  39.9 us
    reduce_sum x5, other arithmetic, layer_norm(): centred = values - jnp.mean(values, axis=-1, keepdims=True)  22.9 us
    dot_general x6, matrix products, per_clip(): return jnp.dot(clip_table.T, values, precision=lax.Precision.HIGHEST)  21.9 us
    pallas_call x1, Pallas kernels, cross_back(): pl.pallas_call(functools.partial(cross_back_kernel, model_width), out_sha...  21.9 us
  transfers between devices with their start and end apart: 6, of which 0 were waited for; matrix products, arithmetic and copies ran while one was open for 23% of the time, Pallas kernels for 51%

profile of v5, /device:TPU:0, one launch (start us, length us, event | category | flops | bytes accessed | tf_op | source)
XLA Modules:
  0.0 889.9 jit_solution(13962865893416602214)
XLA Ops:
  7.2 1.9 convert_element_type.210
  10.2 6.4 reduce_sum.183
  16.6 3.0 multiply_reduce_fusion.5
  23.4 3.7 add_convert_fusion.2
  29.3 1.7 pad.32.rows_ref
  31.0 17.7 %project.1 = (f32[2,896,384]{2,1,0:T(8,128)}, bf16[896,384]{1,0:T(8,128)(2,1)}, bf16[2,784,384]{2,1,0:T(8,128)(2,1)}, f32[8,896]{1,0:T(8,128)}) custom-call(bf16[896,1536]{1,0:T(8,128)(2,1)} %pad.32.rows_ref, bf16[3,1536,384]{2,1,0:T(8,128)(2,1)} %weight_ref.1, f32[3,384]{1,0:T(4,128)} %bias_ref.2, f32[2,384]{1,0:T(2,128)} %get-tuple-element.193.gain_ref, ...), custom_call_target="tpu_custom_call" | custom-call | tf_op jit(solution)/shard_map/project/pallas_call | solution.py:718
  48.8 51.1 %attend.1 = (bf16[896,384]{1,0:T(8,128)(2,1)}, f32[3,128,896]{2,1,0:T(8,128)}, f32[3,1,896]{2,1,0:T(1,128)}, bf16[3,2,784,384]{3,2,1,0:T(8,128)(2,1)}) custom-call(s32[1]{0:T(128)} %dynamic_slice.11.length_ref, bf16[896,384]{1,0:T(8,128)(2,1)} %get-tuple-element.61.query_ref, bf16[2,784,384]{2,1,0:T(8,128)(2,1)} %get-tuple-element.62.kv_ref), custom_call_target="tpu_custom_call" | custom-call | flops 1000000000 | bytes 150000000 | tf_op jit(solution)/shard_map/attend/pallas_call | solution.py:479
  99.9 69.7 %line_sum_0.1 = bf16[784,1536]{1,0:T(8,128)(2,1)} custom-call(bf16[896,384]{1,0:T(8,128)(2,1)} %get-tuple-element.63.refs_0_, bf16[384,1536]{1,0:T(8,128)(2,1)} %refs_1_.5), custom_call_target="tpu_custom_call" | custom-call | flops 924844032 | bytes 230000000 | tf_op jit(solution)/shard_map/line_sum_0/pallas_call | solution.py:192
  169.7 4.2 fusion.93
  176.1 1.4 copy-done.11
  177.6 1.7 pad.35.rows_ref
  179.3 16.3 %cross_attend.1 = (f32[896,384]{1,0:T(8,128)}, f32[512,384]{1,0:T(8,128)}, bf16[896,384]{1,0:T(8,128)(2,1)}, bf16[2,512,384]{2,1,0:T(8,128)(2,1)}, f32[8,896]{1,...) custom-call(bf16[896,1536]{1,0:T(8,128)(2,1)} %pad.35.rows_ref, ...), custom_call_target="tpu_custom_call" | custom-call | tf_op jit(solution)/shard_map/cross_attend/pallas_call | solution.py:937
  195.6 67.1 %line_sum_1.1 = bf16[784,1536]{1,0:T(8,128)(2,1)} custom-call(bf16[896,384]{1,0:T(8,128)(2,1)} %get-tuple-element.64.refs_0_, bf16[384,1536]{1,0:T(8,128)(2,1)} %refs_1_.6), custom_call_target="tpu_custom_call" | custom-call | flops 924844032 | bytes 230000000 | tf_op jit(solution)/shard_map/line_sum_1/pallas_call | solution.py:192
  262.6 4.0 fusion.92
  268.1 10.2 %multiply_convert_fusion = (bf16[780,2240]{1,0:T(8,128)(2,1)S(1)}, f32[780,2240]{1,0:T(8,128)}) fusion(f32[2240]{0:T(1024)S(1)} %copy-done.42, bf16[1536,2240]{0,1:T(8,128)(2,1)S(1)} %bitcast.122, f32[780,1536]{1,0:T(8,128)S(1)} %get-tuple-element.167, f32[1536]{0:T(1024)S(1)} %get-tuple-element.148, f32[1536]{0:T(1024)S(1)} %get-tuple-element.146, ...), kind=kOutput, calls=%fused_computation.14 | convolution fusion | flops 5394452480 | bytes 22187408 | tf_op jit(solution)/shard_map/dot_general | solution.py:1335
  278.2 2.1 pad.36.refs_0_
  280.3 68.1 %line_sum_2.1 = bf16[784,1536]{1,0:T(8,128)(2,1)} custom-call(bf16[784,2240]{1,0:T(8,128)(2,1)} %pad.36.refs_0_, bf16[2240,1536]{1,0:T(8,128)(2,1)} %refs_1_.7), custom_call_target="tpu_custom_call" | custom-call | flops 5394923520 | bytes 230000000 | tf_op jit(solution)/shard_map/line_sum_2/pallas_call | solution.py:192
  348.5 6.8 fusion.13
  355.3 2.1 copy-done.2
  357.5 9.8 %convolution_convert_fusion.1 = bf16[1536,2240]{1,0:T(8,128)(2,1)} fusion(bf16[780,2240]{1,0:T(8,128)(2,1)S(1)} %get-tuple-element.196, f32[780,1536]{1,0:T(8,128)S(1)} %get-tuple-element.170, f32[1536]{0:T(1024)S(1)} %get-tuple-element.147, f32[780]{0:T(1024)S(1)} %get-tuple-element.200), kind=kOutput, calls=%fused_computation.1 | convolution fusion | flops 5374433280 | bytes 15177264 | tf_op jit(solution)/shard_map/dot_general | solution.py:1344
  367.3 17.0 %fusion.95 = (bf16[2240]{0:T(1024)(128)(2,1)S(1)}, bf16[780,2240]{1,0:T(8,128)(2,1)}) fusion(bf16[2240,1536]{1,0:T(8,128)(2,1)} %refs_1_.7, f32[780,1536]{1,0:T(8,128)} %copy-done.2, f32[1536]{0:T(1024)S(1)} %get-tuple-element.147, f32[780]{0:T(1024)S(1)} %get-tuple-element.200, f32[780,2240]{1,0:T(8,128)} %get-tuple-element.197, f32[2240]{0:T(1024)S(1)} %copy-done.42), kind=kOutput, calls=%fused_computation.193 | convolution fusion | flops 5416412160 | bytes 22179504 | tf_op jit(solution)/shard_map/dot_general | solution.py:1345
  384.3 9.9 %copy.57.refs_1_ = bf16[1536,2240]{1,0:T(8,128)(2,1)} copy(bf16[1536,2240]{0,1:T(8,128)(2,1)} %param.38) | data formatting | bytes 13762560 | tf_op args[17]
  394.2 4.6 pad.37.refs_0_
  398.8 73.0 %line_sum_3.1 = bf16[784,1536]{1,0:T(8,128)(2,1)} custom-call(bf16[784,2240]{1,0:T(8,128)(2,1)} %pad.37.refs_0_, bf16[1536,2240]{1,0:T(8,128)(2,1)} %copy.57.refs_1_), custom_call_target="tpu_custom_call" | custom-call | flops 5394923520 | bytes 230000000 | tf_op jit(solution)/shard_map/line_sum_3/pallas_call | solution.py:192
  471.8 4.6 multiply_reduce_fusion.2
  476.4 4.2 fusion.91
  485.2 1.6 constant_dynamic-slice_fusion.key_pre_ref
  487.4 21.9 %cross_back.1 = (bf16[896,384]{1,0:T(8,128)(2,1)}, bf16[2,128,384]{2,1,0:T(8,128)(2,1)}, f32[8,384]{1,0:T(8,128)}) custom-call(bf16[896,384]{1,0:T(8,128)(2,1)} %get-tuple-element.69.query_ref, bf16[2,512,384]{2,1,0:T(8,128)(2,1)} %get-tuple-element.70.kv_ref, f32[3,128,896]{2,1,0:T(8,128)} %get-tuple-element.71.turned_ref, ...), custom_call_target="tpu_custom_call" | custom-call | tf_op jit(solution)/shard_map/cross_back/pallas_call | solution.py:1091
  509.4 2.6 fusion.37
  512.0 13.4 %convolution_convert_fusion = bf16[1536,2240]{1,0:T(8,128)(2,1)} fusion(bf16[780,2240]{1,0:T(8,128)(2,1)} %get-tuple-element.68, f32[780,1536]{1,0:T(8,128)} %copy-done.1, f32[1536]{0:T(1024)S(1)} %get-tuple-element.148, f32[1536]{0:T(1024)S(1)} %get-tuple-element.146, f32[780]{0:T(1024)S(1)} %fusion.74, f32[780]{0:T(1024)S(1)} %broadcast_multiply_fusion.3, ...), kind=kOutput, calls=%fused_computation | convolution fusion | flops 5380423680 | bytes 15189648 | tf_op jit(solution)/shard_map/dot_general | solution.py:1352
  526.4 2.2 fusion.25
  528.7 5.3 fusion.28
  533.9 65.7 %line_sum_4.1 = bf16[784,1536]{1,0:T(8,128)(2,1)} custom-call(bf16[896,384]{1,0:T(8,128)(2,1)} %get-tuple-element.78.refs_0_, bf16[1536,384]{1,0:T(8,128)(2,1)} %refs_1_.8), custom_call_target="tpu_custom_call" | custom-call | flops 924844032 | bytes 230000000 | tf_op jit(solution)/shard_map/line_sum_4/pallas_call | solution.py:192
  599.7 4.2 fusion.7
  603.9 4.3 fusion.9
  608.3 3.9 add_add_fusion.3
  612.2 2.2 copy-done.3
  614.4 2.3 convolution_convert_fusion.9
  616.7 2.3 copy.58
  618.9 4.9 fusion.26
  623.8 3.0 fusion.27
  630.9 3.9 slice_bitcast_fusion.2
  634.8 9.9 %copy.68 = f32[1,780,1536]{2,0,1:T(1,128)} copy(f32[1,780,1536]{2,1,0:T(8,128)} %get-tuple-element.171) | data formatting | bytes 9584640
  644.7 2.3 fusion.50
  647.0 5.9 fusion.63
  652.9 2.2 fusion.59
  655.2 2.0 convert_element_type.241
  657.1 2.2 copy.64
  659.4 2.0 pad.39.grad_ref
  661.3 61.7 %attend_back.1 = (f32[896,384]{1,0:T(8,128)}, f32[2,896,384]{2,1,0:T(8,128)}) custom-call(s32[1]{0:T(128)} %dynamic_slice.11.length_ref, bf16[896,384]{1,0:T(8,128)(2,1)} %get-tuple-element.61.query_ref, bf16[2,784,384]{2,1,0:T(8,128)(2,1)} %get-tuple-element.62.kv_ref, bf16[3,2,784,384]{3,2,1,0:T(8,128)(2,1)} %get-tuple-element.65.got_ref, ...), custom_call_target="tpu_custom_call" | custom-call | flops 1000000000 | bytes 200000000 | tf_op jit(solution)/shard_map/attend_back/pallas_call | solution.py:595
  723.1 3.9 fusion.56
  728.3 13.8 %unproject.1 = (bf16[896,384]{1,0:T(8,128)(2,1)}, bf16[896,384]{1,0:T(8,128)(2,1)}, bf16[896,384]{1,0:T(8,128)(2,1)}, f32[8,384]{1,0:T(8,128)}) custom-call(f32[896,384]{1,0:T(8,128)} %get-tuple-element.83.query_grad_ref, f32[2,896,384]{2,1,0:T(8,128)} %get-tuple-element.84.kv_grad_ref, f32[2,896,384]{2,1,0:T(8,128)} %get-tuple-element.85.pre_ref, ...), custom_call_target="tpu_custom_call" | custom-call | tf_op jit(solution)/shard_map/unproject/pallas_call | solution.py:789
  742.2 2.9 convolution_convert_fusion.3
  745.1 1.7 convolution_convert_fusion.4
  746.9 1.8 convolution_convert_fusion.5
  748.7 2.0 pad_maximum_fusion
  751.2 67.7 %line_sum_5.1 = bf16[784,1536]{1,0:T(8,128)(2,1)} custom-call(bf16[896,384]{1,0:T(8,128)(2,1)} %get-tuple-element.91.refs_0_, bf16[896,384]{1,0:T(8,128)(2,1)} %get-tuple-element.92.refs_1_, bf16[896,384]{1,0:T(8,128)(2,1)} %get-tuple-element.93.refs_2_, bf16[1536,384]{1,0:T(8,128)(2,1)} %get-tuple-element.175.refs_3_, ...), custom_call_target="tpu_custom_call" | custom-call | flops 2774532096 | bytes 230000000 | tf_op jit(solution)/shard_map/line_sum_5/pallas_call | solution.py:192
  818.9 2.3 fusion.53
  821.2 5.5 fusion.62
  826.9 7.6 multiply_reduce_fusion.1
  836.1 10.1 %plane_sum.1 = (f32[192,128]{1,0:T(8,128)}, f32[192,128]{1,0:T(8,128)}) custom-call(bf16[192,128]{1,0:T(8,128)(2,1)} %pad_bitcast_fusion.value_ref), custom_call_target="tpu_custom_call" | custom-call | tf_op jit(solution)/shard_map/plane_sum/pallas_call | solution.py:267
  850.4 4.1 fusion.89
  854.6 5.1 add_bitcast_fusion
  859.6 9.6 %copy.69 = f32[1,780,1536]{2,0,1:T(1,128)} copy(f32[1,780,1536]{2,1,0:T(8,128)} %add_bitcast_fusion) | data formatting | bytes 9584640
  (226 shorter events, 39.9 us)
Async XLA Ops:
  7.2 172.1 %all-gather.2.cloned.1.call-start = ((), (), s32[]{:S(2)}) async-start(), calls=%async_computation.4 | async-start | bytes 1966080 | tf_op jit(solution)/shard_map/all_gather | solution.py:1282
  9.2 516.2 %reduce-scatter.5.cloned.1.call-start = ((), (), s32[]{:S(2)}) async-start(), calls=%async_computation.5 | async-start | bytes 7962624 | tf_op jit(solution)/shard_map/reduce_scatter | solution.py:213
  10.2 13.2 %copy-start.25 = (f32[1536]{0:T(1024)}, f32[1536]{0:T(1024)S(1)}, u32[]{:S(2)}) copy-start(f32[1536]{0:T(1024)S(1)} %get-tuple-element.151) | copy-start | bytes 18436
  10.2 9.4 %copy-start.37 = (s32[3,1,780]{2,1,0:T(1,128)S(1)}, s32[3,1,780]{2,1,0:T(1,128)}, u32[]{:S(2)}) copy-start(s32[3,1,780]{2,1,0:T(1,128)} %param.26) | copy-start | bytes 28084
  16.6 4.8 copy-start.43
  16.6 10.5 %copy-start.23 = (f32[780]{0:T(1024)}, f32[780]{0:T(1024)S(1)}, u32[]{:S(2)}) copy-start(f32[780]{0:T(1024)S(1)} %broadcast_multiply_fusion.5) | copy-start | bytes 9364
  19.6 7.5 copy-start.32
  19.6 7.5 copy-start.30
  20.9 6.3 copy-start.39
  27.2 21.6 %copy-start.8 = (bf16[780,1536]{1,0:T(8,128)(2,1)}, bf16[780,1536]{1,0:T(8,128)(2,1)S(1)}, u32[]{:S(2)}) copy-start(bf16[780,1536]{1,0:T(8,128)(2,1)S(1)} %add_convert_fusion.2) | copy-start | bytes 7188484
  48.8 120.8 %copy-start.34 = (f32[3,1536]{1,0:T(4,128)S(1)}, f32[3,1536]{1,0:T(4,128)}, u32[]{:S(2)}) copy-start(f32[3,1536]{1,0:T(4,128)} %param.41) | copy-start | bytes 55300
  169.7 4.2 copy-start.28
  173.9 2.2 copy-start
  173.9 0.7 copy-start.27
  173.9 0.8 copy-start.38
  176.1 1.4 copy-start.11
  262.6 4.7 slice-start.10
  262.6 5.4 slice-start.11
  266.6 11.6 %copy-start.1 = (f32[780,1536]{1,0:T(8,128)}, f32[780,1536]{1,0:T(8,128)S(1)}, u32[]{:S(2)}) copy-start(f32[780,1536]{1,0:T(8,128)S(1)} %get-tuple-element.167) | copy-start | bytes 14376964
  266.7 1.4 copy-start.42
  355.3 2.1 copy-start.2
  384.3 270.9 %all-reduce.11.cloned.1.call-start = ((), (), s32[]{:S(2)}) async-start(), calls=%async_computation.8 | async-start | bytes 786432 | tf_op jit(solution)/shard_map/psum | solution.py:1455
  471.8 4.6 copy-start.5
  471.8 8.8 slice-start
  476.4 4.3 slice-start.1
  480.7 1.3 copy-start.15
  481.3 2.2 copy-start.7
  483.6 25.8 %copy-start.12 = (bf16[2,1536,384]{2,1,0:T(8,128)(2,1)S(1)}, bf16[2,1536,384]{2,1,0:T(8,128)(2,1)}, u32[]{:S(2)}) copy-start(bf16[2,1536,384]{2,1,0:T(8,128)(2,1)} %text_weight_ref.1) | copy-start | bytes 7077892
  512.0 216.4 %reduce-scatter.7.cloned.1.call-start = ((), (), s32[]{:S(2)}) async-start(), calls=%async_computation.6 | async-start | bytes 7962624 | tf_op jit(solution)/shard_map/reduce_scatter | solution.py:213
  525.4 1.0 copy-start.14
  525.4 1.0 copy-start.19
  525.4 3.3 copy-start.22
  525.4 225.2 %reduce-scatter.9.cloned.1.call-start = ((), (), s32[]{:S(2)}) async-start(), calls=%async_computation.7 | async-start | bytes 6635520 | tf_op jit(solution)/shard_map/reduce_scatter | solution.py:213
  533.9 74.3 %slice-start.8 = ((s8[4816896]{0:T(1024)(128)(4,1)}), s8[622592]{0:T(1024)(128)(4,1)S(1)}, s32[]{:S(2)}) async-start(s8[4816896]{0:T(1024)(128)(4,1)} %bitcast.119), calls=%async_computation.18 | async-start | bytes 1245184
  599.7 4.2 copy-start.4
  599.7 8.6 slice-start.9
  608.3 6.1 copy-start.16
  612.2 2.2 copy-start.3
  616.7 7.1 slice-start.4
  618.9 4.9 slice-start.5
  618.9 4.9 copy-start.21
  623.8 3.0 copy-start.13
  626.8 2.7 copy-start.44
  629.3 5.5 copy-start.35
  629.3 250.3 %reduce-scatter.11.cloned.1.call-start = ((), (), s32[]{:S(2)}) async-start(), calls=%async_computation.9 | async-start | bytes 3981312 | tf_op jit(solution)/shard_map/reduce_scatter | solution.py:213
  634.8 18.1 %slice-start.2 = ((s8[4816896]{0:T(1024)(128)(4,1)}), s8[622592]{0:T(1024)(128)(4,1)S(1)}, s32[]{:S(2)}) async-start(s8[4816896]{0:T(1024)(128)(4,1)} %bitcast.113), calls=%async_computation.12 | async-start | bytes 1245184
  644.7 8.2 slice-start.3
  644.7 8.2 copy-start.10
  657.1 66.0 %slice-start.6 = ((s8[4816896]{0:T(1024)(128)(4,1)}), s8[622592]{0:T(1024)(128)(4,1)S(1)}, s32[]{:S(2)}) async-start(s8[4816896]{0:T(1024)(128)(4,1)} %bitcast.117), calls=%async_computation.16 | async-start | bytes 1245184
  657.1 66.0 %copy-start.29 = (f32[1536]{0:T(1024)S(1)}, f32[1536]{0:T(1024)}, u32[]{:S(2)}) copy-start(f32[1536]{0:T(1024)} %copy-done.28) | copy-start | bytes 18436
  661.3 61.8 %slice-start.7 = ((s8[4816896]{0:T(1024)(128)(4,1)}), s8[4194304]{0:T(1024)(128)(4,1)S(1)}, s32[]{:S(2)}) async-start(s8[4816896]{0:T(1024)(128)(4,1)} %bitcast.117), calls=%async_computation.17 | async-start | bytes 8388608
  723.1 3.9 copy-start.18
  728.3 13.8 %copy-start.9 = (bf16[780,1536]{1,0:T(8,128)(2,1)S(1)}, bf16[780,1536]{1,0:T(8,128)(2,1)}, u32[]{:S(2)}) copy-start(bf16[780,1536]{1,0:T(8,128)(2,1)} %copy-done.8) | copy-start | bytes 7188484
  742.2 2.9 copy-start.41
  745.1 1.8 copy-start.40
  748.7 2.4 copy-start.36
  751.2 70.0 %copy-start.24 = (f32[780]{0:T(1024)S(1)}, f32[780]{0:T(1024)}, u32[]{:S(2)}) copy-start(f32[780]{0:T(1024)} %copy-done.23) | copy-start | bytes 9364
  751.2 70.0 %copy-start.31 = (f32[780]{0:T(1024)S(1)}, f32[780]{0:T(1024)}, u32[]{:S(2)}) copy-start(f32[780]{0:T(1024)} %copy-done.30) | copy-start | bytes 9364
  818.8 8.0 copy-start.6
  818.9 8.0 copy-start.26
  826.9 23.6 %copy-start.33 = (f32[780]{0:T(1024)S(1)}, f32[780]{0:T(1024)}, u32[]{:S(2)}) copy-start(f32[780]{0:T(1024)} %copy-done.32) | copy-start | bytes 9364
  859.6 15.6 %copy-start.17 = (bf16[192,2240]{1,0:T(8,128)(2,1)S(1)}, bf16[192,2240]{1,0:T(8,128)(2,1)}, u32[]{:S(2)}) copy-start(bf16[192,2240]{1,0:T(8,128)(2,1)} %reduce-scatter.7.cloned.1.call-done) | copy-start | bytes 2580484
  859.6 18.2 %copy-start.20 = (bf16[192,1920]{1,0:T(8,128)(2,1)S(1)}, bf16[192,1920]{1,0:T(8,128)(2,1)}, u32[]{:S(2)}) copy-start(bf16[192,1920]{1,0:T(8,128)(2,1)} %reduce-scatter.9.cloned.1.call-done) | copy-start | bytes 2211844
Sparse Core Ops, SparseCore 0:
  10.4 33.5 all-gather.1
  384.4 64.7 reduce-scatter.4
  512.1 40.7 all-reduce.10
  556.2 65.0 reduce-scatter.6
  629.4 85.3 reduce-scatter.8
  750.8 48.5 reduce-scatter.10

commit v6 on v5

--- a/solution.py
+++ b/solution.py
@@ -59,8 +59,10 @@
 
 def line_kernel(count, block, group, lag, lag2, turned, *refs):
     lhs_refs = refs[:count]
-    rhs_refs = refs[count:2 * count]
-    out_ref, raw, part, stage, cross, raw_s, raw_r, mid_s, mid_r, far_s, far_r, near_s, near_r = refs[2 * count:]
+    stacked = len(refs[count].shape) == 3
+    rhs_count = 1 if stacked else count
+    rhs_refs = [refs[count].at[j] for j in range(count)] if stacked else refs[count : 2 * count]
+    out_ref, raw, part, stage, cross, raw_s, raw_r, mid_s, mid_r, far_s, far_r, near_s, near_r = refs[count + rhs_count :]
     steps = out_ref.shape[0] // block
     me = lax.axis_index("tensor")
     inner = (me == 1) | (me == 2)
@@ -179,20 +181,18 @@
 
     lax.fori_loop(0, steps, drain, 0)
 
-def line_sum(pairs, turned, ident, true_rows, block=16, group=7, lag=4, lag2=8):
-    width = pairs[0][1].shape[0 if turned else 1]
+def line_sum(sources, weights, turned, ident, true_rows, block=16, group=7, lag=4, lag2=8):
+    width = weights[0].shape[-2 if turned else -1]
     unit = block * group
     rows = -(-true_rows // unit) * unit
-    pairs = [
-        (jnp.pad(lhs, ((0, max(rows - lhs.shape[0], 0)), (0, 0))), rhs) for lhs, rhs in pairs
-    ]
+    sources = [jnp.pad(lhs, ((0, max(rows - lhs.shape[0], 0)), (0, 0))) for lhs in sources]
     steps = rows // block
     dma = pltpu.SemaphoreType.DMA
-    depth = sum(p[0].shape[1] for p in pairs)
+    depth = sum(lhs.shape[1] for lhs in sources)
     return pl.pallas_call(
-        functools.partial(line_kernel, len(pairs), block, group, lag, lag2, turned),
+        functools.partial(line_kernel, len(sources), block, group, lag, lag2, turned),
         out_shape=jax.ShapeDtypeStruct((rows, width), LOW),
-        in_specs=[pl.BlockSpec(memory_space=pltpu.VMEM)] * (2 * len(pairs)),
+        in_specs=[pl.BlockSpec(memory_space=pltpu.VMEM)] * (len(sources) + len(weights)),
         out_specs=pl.BlockSpec(memory_space=pltpu.VMEM),
         scratch_shapes=[
             pltpu.VMEM((rows, width), LOW),
@@ -203,7 +203,7 @@
         compiler_params=pltpu.CompilerParams(collective_id=ident, has_side_effects=True, vmem_limit_bytes=60 << 20),
         cost_estimate=pl.CostEstimate(flops=2 * rows * width * depth, bytes_accessed=230 * 10**6, transcendentals=0),
         name=f"line_sum_{ident}",
-    )(*[p[0] for p in pairs], *[p[1] for p in pairs])[:true_rows].astype(WIDE)
+    )(*sources, *weights)[:true_rows].astype(WIDE)
 
 def row_major(values):
     return with_layout_constraint(values, Layout((0, 1)))
@@ -1213,9 +1213,13 @@
     teacher_rows = teacher.reshape(flat_rows, model_width)
 
     def per_row(index_no):
+        if clip_count == 1:
+            return modulated[:, index_no]
         return jnp.dot(clip_table, modulated[:, index_no], precision=lax.Precision.HIGHEST)
 
     def per_clip(values):
+        if clip_count == 1:
+            return jnp.sum(values, axis=0, keepdims=True)
         return jnp.dot(clip_table.T, values, precision=lax.Precision.HIGHEST)
 
     scale_one = per_row(1)
@@ -1272,7 +1276,7 @@
         attn_low = pad_queries(attn_low)
         self_totals = jnp.stack(total_heads)
     branch_one = (
-        line_sum([(attn_low, self_out)], False, 0, flat_rows) + out_bias[0]
+        line_sum([attn_low], [self_out], False, 0, flat_rows) + out_bias[0]
     )
     after_one = hidden_rows + branch_one * gate_one
     normed_three = layer_norm(after_one)
@@ -1326,7 +1330,7 @@
         cross_att_low = jnp.stack(cross_heads, axis=2).astype(low_type).reshape(flat_rows, local_width)
         cross_totals = jnp.stack(cross_total_heads)
     branch_two = (
-        line_sum([(cross_att_low, cross_out)], False, 1, flat_rows)
+        line_sum([cross_att_low], [cross_out], False, 1, flat_rows)
         + out_bias[1]
     )
     after_two = after_one + branch_two
@@ -1335,7 +1339,7 @@
     pre_act = jnp.dot(ffn_input, ffn_in, preferred_element_type=wide_type) + ffn_in_bias
     act_low = gelu_tanh(pre_act).astype(low_type)
     branch_three = (
-        line_sum([(act_low, ffn_out)], False, 2, flat_rows) + out_bias[2]
+        line_sum([act_low], [ffn_out], False, 2, flat_rows) + out_bias[2]
     )
     result = after_two + branch_three * gate_two
     residue = jnp.where(valid_rows[:, None], result - teacher_rows, 0.0)
@@ -1351,7 +1355,7 @@
     part_ffn_out = scatter_rows(ffn_out_mix, 0)
     ffn_in_mix = jnp.dot(ffn_input.T, grad_pre_low, preferred_element_type=wide_type)
     grad_ffn_bias = jnp.sum(grad_pre, axis=0)
-    grad_ffn_input = line_sum([(grad_pre_low, ffn_in)], True, 3, flat_rows)
+    grad_ffn_input = line_sum([grad_pre_low], [ffn_in.T], False, 3, flat_rows)
     grad_after_two = (
         residue + jax.vjp(layer_norm, after_two)[1](grad_ffn_input * (1.0 + scale_two))[0]
     )
@@ -1448,7 +1452,7 @@
     )
     part_ffn_in = scatter_rows(ffn_in_mix, 0)
     cross_q_mix = jnp.dot(cross_in.T, grad_cross_query_low, preferred_element_type=wide_type)
-    grad_cross_in = line_sum([(grad_cross_query_low, cross_q)], True, 4, flat_rows)
+    grad_cross_in = line_sum([grad_cross_query_low], [cross_q], True, 4, flat_rows)
     cross_kv_mix = jnp.einsum(
         "ctd,kcte->kde", text_low, text_grad_low, preferred_element_type=wide_type
     )
@@ -1556,7 +1560,7 @@
         (grad_proj_low, row_major(self_in_mix), part_group)
     )
     part_self_in = scatter_rows(self_in_mix, 0)
-    grad_attn_in = line_sum([(grad_proj_low[j], self_in[j]) for j in range(3)], True, 5, flat_rows)
+    grad_attn_in = line_sum(grad_proj_low, [self_in], True, 5, flat_rows)
     grad_hidden = (
         grad_after_one + jax.vjp(layer_norm, hidden_rows)[1](grad_attn_in * (1.0 + scale_one))[0]
     )

time: 897 us -> 854 us (0.952)
  matrix products: 100 us -> 77.2 us
  Pallas kernels: 604 us -> 587 us
  local copies, waits for them, and re-layouts: 82.7 us -> 67.3 us
  other arithmetic: 84.4 us -> 93.7 us
    dot_general x6 -> x0, matrix products: 21.9 us -> none  [per_clip(): return jnp.dot(clip_table.T, values, precision=lax.Precision.HIGHEST)]
    reduce_sum x0 -> x4, other arithmetic: none -> 14.8 us  [the longest x3 8.6 us: per_clip(): return jnp.sum(values, axis=0, keepdims=True)]
    pallas_call x6, Pallas kernels: 411 us -> 400 us  [line_sum(): pl.pallas_call(functools.partial(line_kernel, len(sources), block, group,...]
    unnamed x118 -> x99, local copies, waits for them, and re-layouts: 39.9 us -> 31.4 us
    reduce_sum x5 -> x4, other arithmetic: 22.9 us -> 19.1 us  [layer_norm(): centred = values - jnp.mean(values, axis=-1, keepdims=True)]
  transfers between devices with their start and end apart: 6 -> 6, of which waited for: 0 -> 0; matrix products, arithmetic and copies ran while one was open for 23% -> 20% of each run, Pallas kernels for 51% -> 52%
where the time goes in v6:
time: 854 us; the launch traced here: 844 us
  Pallas kernels  587 us (69%)
  other arithmetic  93.7 us (11%)
  matrix products  77.2 us (9%)
  local copies, waits for them, and re-layouts  67.3 us (8%)
  between operations  18.1 us (2%)
    pallas_call x6, Pallas kernels, line_sum(): pl.pallas_call(functools.partial(line_kernel, len(sources), block, group,...  400 us
    pallas_call x1, Pallas kernels, attend_back(): pl.pallas_call(functools.partial(attend_back_kernel, true_rows), out_shap...  55.5 us
    pallas_call x1, Pallas kernels, attend(): pl.pallas_call(functools.partial(attend_kernel, true_rows), out_shape=(ja...  50.6 us
    unnamed x99, local copies, waits for them, and re-layouts  31.4 us
    pallas_call x1, Pallas kernels, cross_back(): pl.pallas_call(functools.partial(cross_back_kernel, model_width), out_sha...  21.8 us
    reduce_sum x4, other arithmetic, layer_norm(): centred = values - jnp.mean(values, axis=-1, keepdims=True)  19.1 us
    pallas_call x1, Pallas kernels, project(): pl.pallas_call(project_kernel, out_shape=(jax.ShapeDtypeStruct((2, rows,...  17.9 us
    dot_general x1, matrix products, shards(): jnp.dot(grad_three_low, ffn_out.T, preferred_element_type=wide_type)  17.2 us
  transfers between devices with their start and end apart: 6, of which 0 were waited for; matrix products, arithmetic and copies ran while one was open for 20% of the time, Pallas kernels for 52%

profile of v6, /device:TPU:0, one launch (start us, length us, event | category | flops | bytes accessed | tf_op | source)
XLA Modules:
  0.0 844.1 jit_solution(12654590488550033887)
XLA Ops:
  7.2 1.9 convert_element_type.209
  9.3 6.4 reduce_sum.237
  15.7 3.0 multiply_reduce_fusion.5
  24.1 3.2 add_convert_fusion.2
  27.3 1.4 copy-done.10
  28.8 1.7 pad.32.rows_ref
  30.5 17.9 %project.1 = (f32[2,896,384]{2,1,0:T(8,128)}, bf16[896,384]{1,0:T(8,128)(2,1)}, bf16[2,784,384]{2,1,0:T(8,128)(2,1)}, f32[8,896]{1,0:T(8,128)}) custom-call(bf16[896,1536]{1,0:T(8,128)(2,1)} %pad.32.rows_ref, bf16[3,1536,384]{2,1,0:T(8,128)(2,1)} %refs_3_.1, f32[3,384]{1,0:T(4,128)} %bias_ref.2, f32[2,384]{1,0:T(2,128)} %get-tuple-element.192.gain_ref, ...), custom_call_target="tpu_custom_call" | custom-call | tf_op jit(solution)/shard_map/project/pallas_call | solution.py:718
  48.4 50.6 %attend.1 = (bf16[896,384]{1,0:T(8,128)(2,1)}, f32[3,128,896]{2,1,0:T(8,128)}, f32[3,1,896]{2,1,0:T(1,128)}, bf16[3,2,784,384]{3,2,1,0:T(8,128)(2,1)}) custom-call(s32[1]{0:T(128)} %dynamic_slice.11.length_ref, bf16[896,384]{1,0:T(8,128)(2,1)} %get-tuple-element.61.query_ref, bf16[2,784,384]{2,1,0:T(8,128)(2,1)} %get-tuple-element.62.kv_ref), custom_call_target="tpu_custom_call" | custom-call | flops 1000000000 | bytes 150000000 | tf_op jit(solution)/shard_map/attend/pallas_call | solution.py:479
  99.0 70.5 %line_sum_0.1 = bf16[784,1536]{1,0:T(8,128)(2,1)} custom-call(bf16[896,384]{1,0:T(8,128)(2,1)} %get-tuple-element.63.refs_0_, bf16[384,1536]{1,0:T(8,128)(2,1)} %refs_1_.4), custom_call_target="tpu_custom_call" | custom-call | flops 924844032 | bytes 230000000 | tf_op jit(solution)/shard_map/line_sum_0/pallas_call | solution.py:192
  169.6 3.9 fusion.51
  175.8 1.5 copy-done.12
  177.3 1.7 pad.35.rows_ref
  179.7 16.3 %cross_attend.1 = (f32[896,384]{1,0:T(8,128)}, f32[512,384]{1,0:T(8,128)}, bf16[896,384]{1,0:T(8,128)(2,1)}, bf16[2,512,384]{2,1,0:T(8,128)(2,1)}, f32[8,896]{1,...) custom-call(bf16[896,1536]{1,0:T(8,128)(2,1)} %pad.35.rows_ref, ...), custom_call_target="tpu_custom_call" | custom-call | tf_op jit(solution)/shard_map/cross_attend/pallas_call | solution.py:937
  195.9 67.4 %line_sum_1.1 = bf16[784,1536]{1,0:T(8,128)(2,1)} custom-call(bf16[896,384]{1,0:T(8,128)(2,1)} %get-tuple-element.64.refs_0_, bf16[384,1536]{1,0:T(8,128)(2,1)} %refs_1_.5), custom_call_target="tpu_custom_call" | custom-call | flops 924844032 | bytes 230000000 | tf_op jit(solution)/shard_map/line_sum_1/pallas_call | solution.py:192
  263.4 4.0 fusion.50
  268.8 9.5 %multiply_convert_fusion = (bf16[780,2240]{1,0:T(8,128)(2,1)S(1)}, f32[780,2240]{1,0:T(8,128)}) fusion(f32[2240]{0:T(1024)S(1)} %copy-done.43, bf16[1536,2240]{0,1:T(8,128)(2,1)S(1)} %bitcast.108, f32[780,1536]{1,0:T(8,128)S(1)} %get-tuple-element.170, f32[1536]{0:T(1024)S(1)} %get-tuple-element.155, f32[1536]{0:T(1024)S(1)} %get-tuple-element.153, ...), kind=kOutput, calls=%fused_computation.14 | convolution fusion | flops 5390858240 | bytes 22184288 | tf_op jit(solution)/shard_map/dot_general | solution.py:1339
  278.4 2.1 pad.36.refs_0_
  280.5 68.0 %line_sum_2.1 = bf16[784,1536]{1,0:T(8,128)(2,1)} custom-call(bf16[784,2240]{1,0:T(8,128)(2,1)} %pad.36.refs_0_, bf16[2240,1536]{1,0:T(8,128)(2,1)} %refs_1_.6), custom_call_target="tpu_custom_call" | custom-call | flops 5394923520 | bytes 230000000 | tf_op jit(solution)/shard_map/line_sum_2/pallas_call | solution.py:192
  348.4 7.7 multiply_reduce_fusion
  356.2 2.1 copy-done.9
  358.3 9.6 %convolution_convert_fusion.1 = bf16[1536,2240]{1,0:T(8,128)(2,1)} fusion(bf16[780,2240]{1,0:T(8,128)(2,1)S(1)} %get-tuple-element.195, f32[780,1536]{1,0:T(8,128)S(1)} %get-tuple-element.167, f32[1536]{0:T(1024)S(1)} %get-tuple-element.154), kind=kOutput, calls=%fused_computation.1 | convolution fusion | flops 5373235200 | bytes 15174144 | tf_op jit(solution)/shard_map/dot_general | solution.py:1348
  367.9 17.2 %fusion.52 = (bf16[2240]{0:T(1024)(128)(2,1)S(1)}, bf16[780,2240]{1,0:T(8,128)(2,1)}) fusion(bf16[2240,1536]{1,0:T(8,128)(2,1)} %refs_1_.6, f32[780,1536]{1,0:T(8,128)} %copy-done.9, f32[1536]{0:T(1024)S(1)} %get-tuple-element.154, f32[780,2240]{1,0:T(8,128)} %get-tuple-element.196, f32[2240]{0:T(1024)S(1)} %copy-done.43), kind=kOutput, calls=%fused_computation.159 | convolution fusion | flops 5415214080 | bytes 22176384 | tf_op jit(solution)/shard_map/dot_general | solution.py:1349
  385.9 4.1 pad.37.refs_0_
  390.0 65.9 %line_sum_3.1 = bf16[784,1536]{1,0:T(8,128)(2,1)} custom-call(bf16[784,2240]{1,0:T(8,128)(2,1)} %pad.37.refs_0_, bf16[2240,1536]{1,0:T(8,128)(2,1)} %bitcast.106), custom_call_target="tpu_custom_call" | custom-call | flops 5394923520 | bytes 230000000 | tf_op jit(solution)/shard_map/line_sum_3/pallas_call | solution.py:192
  456.0 4.2 fusion.13
  460.2 4.3 fusion.14
  464.5 4.9 fusion.48
  469.4 1.4 convolution_convert_fusion.10
  472.5 1.7 constant_dynamic-slice_fusion.key_pre_ref
  474.7 21.8 %cross_back.1 = (bf16[896,384]{1,0:T(8,128)(2,1)}, bf16[2,128,384]{2,1,0:T(8,128)(2,1)}, f32[8,384]{1,0:T(8,128)}) custom-call(bf16[896,384]{1,0:T(8,128)(2,1)} %get-tuple-element.69.query_ref, bf16[2,512,384]{2,1,0:T(8,128)(2,1)} %get-tuple-element.70.kv_ref, f32[3,128,896]{2,1,0:T(8,128)} %get-tuple-element.71.turned_ref, ...), custom_call_target="tpu_custom_call" | custom-call | tf_op jit(solution)/shard_map/cross_back/pallas_call | solution.py:1091
  496.5 2.6 fusion.24
  499.4 12.9 %convolution_convert_fusion = bf16[1536,2240]{1,0:T(8,128)(2,1)} fusion(bf16[780,2240]{1,0:T(8,128)(2,1)} %get-tuple-element.68, f32[780,1536]{1,0:T(8,128)} %copy-done.1, f32[1536]{0:T(1024)S(1)} %get-tuple-element.155, f32[1536]{0:T(1024)S(1)} %get-tuple-element.153, f32[780]{0:T(1024)S(1)} %fusion.39, f32[780]{0:T(1024)S(1)} %broadcast_multiply_fusion.3), kind=kOutput, calls=%fused_computation | convolution fusion | flops 5376829440 | bytes 15186528 | tf_op jit(solution)/shard_map/dot_general | solution.py:1356
  513.3 2.2 fusion.18
  515.5 5.3 fusion.21
  520.8 63.6 %line_sum_4.1 = bf16[784,1536]{1,0:T(8,128)(2,1)} custom-call(bf16[896,384]{1,0:T(8,128)(2,1)} %get-tuple-element.78.refs_0_, bf16[1536,384]{1,0:T(8,128)(2,1)} %refs_1_.7), custom_call_target="tpu_custom_call" | custom-call | flops 924844032 | bytes 230000000 | tf_op jit(solution)/shard_map/line_sum_4/pallas_call | solution.py:192
  584.4 4.3 fusion.12
  588.7 4.6 fusion.15
  593.3 6.2 multiply_reduce_fusion.6
  599.6 2.2 copy-done.6
  601.8 2.2 convolution_convert_fusion.9
  604.0 1.4 copy.56
  605.5 4.9 fusion.19
  610.4 2.9 fusion.20
  617.6 2.1 slice_reduce_fusion.2
  619.7 10.0 %copy.66 = f32[1,780,1536]{2,0,1:T(1,128)} copy(f32[1,780,1536]{2,1,0:T(8,128)} %get-tuple-element.173) | data formatting | bytes 9584640
  629.7 2.0 convert_element_type.240
  632.8 2.0 pad.39.grad_ref
  634.7 55.5 %attend_back.1 = (f32[896,384]{1,0:T(8,128)}, f32[2,896,384]{2,1,0:T(8,128)}) custom-call(s32[1]{0:T(128)} %dynamic_slice.11.length_ref, bf16[896,384]{1,0:T(8,128)(2,1)} %get-tuple-element.61.query_ref, bf16[2,784,384]{2,1,0:T(8,128)(2,1)} %get-tuple-element.62.kv_ref, bf16[3,2,784,384]{3,2,1,0:T(8,128)(2,1)} %get-tuple-element.65.got_ref, ...), custom_call_target="tpu_custom_call" | custom-call | flops 1000000000 | bytes 200000000 | tf_op jit(solution)/shard_map/attend_back/pallas_call | solution.py:595
  690.3 13.4 %unproject.1 = (bf16[896,384]{1,0:T(8,128)(2,1)}, bf16[896,384]{1,0:T(8,128)(2,1)}, bf16[896,384]{1,0:T(8,128)(2,1)}, f32[8,384]{1,0:T(8,128)}) custom-call(f32[896,384]{1,0:T(8,128)} %get-tuple-element.83.query_grad_ref, f32[2,896,384]{2,1,0:T(8,128)} %get-tuple-element.84.kv_grad_ref, f32[2,896,384]{2,1,0:T(8,128)} %get-tuple-element.85.pre_ref, ...), custom_call_target="tpu_custom_call" | custom-call | tf_op jit(solution)/shard_map/unproject/pallas_call | solution.py:789
  703.8 2.9 convolution_convert_fusion.5
  706.7 1.7 convolution_convert_fusion.4
  708.5 1.7 convolution_convert_fusion.3
  710.2 1.9 pad_maximum_fusion
  712.7 1.3 convert_bitcast_fusion
  714.1 64.1 %line_sum_5.1 = bf16[784,1536]{1,0:T(8,128)(2,1)} custom-call(bf16[896,384]{1,0:T(8,128)(2,1)} %get-tuple-element.91.refs_0_, bf16[896,384]{1,0:T(8,128)(2,1)} %get-tuple-element.92.refs_1_, bf16[896,384]{1,0:T(8,128)(2,1)} %get-tuple-element.93.refs_2_, bf16[3,1536,384]{2,1,0:T(8,128)(2,1)} %refs_3_.1), custom_call_target="tpu_custom_call" | custom-call | flops 2774532096 | bytes 230000000 | tf_op jit(solution)/shard_map/line_sum_5/pallas_call | solution.py:192
  778.3 2.2 slice_reduce_fusion
  780.5 4.0 fusion.11
  784.6 4.8 fusion.46
  790.9 11.6 %plane_sum.1 = (f32[192,128]{1,0:T(8,128)}, f32[192,128]{1,0:T(8,128)}) custom-call(bf16[192,128]{1,0:T(8,128)(2,1)} %pad_bitcast_fusion.value_ref), custom_call_target="tpu_custom_call" | custom-call | tf_op jit(solution)/shard_map/plane_sum/pallas_call | solution.py:267
  806.7 6.8 add_bitcast_fusion
  813.6 9.6 %copy.67 = f32[1,780,1536]{2,0,1:T(1,128)} copy(f32[1,780,1536]{2,1,0:T(8,128)} %add_bitcast_fusion) | data formatting | bytes 9584640
  823.2 1.4 slice.191
  827.1 1.4 slice_bitcast_fusion.7
  829.7 1.3 convert_element_type.243
  (195 shorter events, 32.7 us)
Async XLA Ops:
  7.2 172.5 %all-gather.2.cloned.1.call-start = ((), (), s32[]{:S(2)}) async-start(), calls=%async_computation.4 | async-start | bytes 1966080 | tf_op jit(solution)/shard_map/all_gather | solution.py:1286
  9.2 503.1 %reduce-scatter.5.cloned.1.call-start = ((), (), s32[]{:S(2)}) async-start(), calls=%async_computation.5 | async-start | bytes 7962624 | tf_op jit(solution)/shard_map/reduce_scatter | solution.py:213
  9.2 9.5 %copy-start.40 = (f32[4,384]{1,0:T(4,128)S(1)}, f32[4,384]{1,0:T(4,128)}, u32[]{:S(2)}) copy-start(f32[4,384]{1,0:T(4,128)} %param.31) | copy-start | bytes 18436
  9.3 10.1 %copy-start.38 = (s32[3,1,780]{2,1,0:T(1,128)S(1)}, s32[3,1,780]{2,1,0:T(1,128)}, u32[]{:S(2)}) copy-start(s32[3,1,780]{2,1,0:T(1,128)} %param.26) | copy-start | bytes 28084
  9.3 10.1 %copy-start.31 = (f32[6,1536]{1,0:T(8,128)S(1)}, f32[6,1536]{1,0:T(8,128)}, u32[]{:S(2)}) copy-start(f32[6,1536]{1,0:T(8,128)} %param.27) | copy-start | bytes 110596
  9.3 10.1 %copy-start.34 = (f32[1,6,1536]{2,0,1:T(1,128)S(1)}, f32[1,6,1536]{2,0,1:T(1,128)}, u32[]{:S(2)}) copy-start(f32[1,6,1536]{2,0,1:T(1,128)} %param.24) | copy-start | bytes 110596
  15.7 8.4 copy-start.26
  15.7 7.0 copy-start.44
  18.7 8.5 %copy-start.32 = (f32[780]{0:T(1024)}, f32[780]{0:T(1024)S(1)}, u32[]{:S(2)}) copy-start(f32[780]{0:T(1024)S(1)} %multiply_reduce_fusion.5) | copy-start | bytes 9364
  18.8 8.5 %copy-start.29 = (f32[780]{0:T(1024)}, f32[780]{0:T(1024)S(1)}, u32[]{:S(2)}) copy-start(f32[780]{0:T(1024)S(1)} %fusion.37) | copy-start | bytes 9364
  19.6 7.7 copy-start.24
  27.3 1.5 copy-start.10
  48.4 121.2 %copy-start.35 = (f32[3,1536]{1,0:T(4,128)S(1)}, f32[3,1536]{1,0:T(4,128)}, u32[]{:S(2)}) copy-start(f32[3,1536]{1,0:T(4,128)} %param.41) | copy-start | bytes 55300
  173.6 2.2 copy-start
  173.6 0.7 copy-start.28
  173.6 0.8 copy-start.39
  175.8 1.5 copy-start.12
  263.4 4.7 slice-start
  263.4 5.4 slice-start.1
  267.4 11.0 %copy-start.1 = (f32[780,1536]{1,0:T(8,128)}, f32[780,1536]{1,0:T(8,128)S(1)}, u32[]{:S(2)}) copy-start(f32[780,1536]{1,0:T(8,128)S(1)} %get-tuple-element.170) | copy-start | bytes 14376964
  267.4 1.4 copy-start.43
  356.2 2.1 copy-start.9
  385.1 244.6 %all-reduce.11.cloned.1.call-start = ((), (), s32[]{:S(2)}) async-start(), calls=%async_computation.8 | async-start | bytes 786432 | tf_op jit(solution)/shard_map/psum | solution.py:1459
  455.9 4.2 copy-start.3
  464.5 4.9 copy-start.16
  469.4 2.1 copy-start.8
  471.5 25.0 %copy-start.13 = (bf16[2,1536,384]{2,1,0:T(8,128)(2,1)S(1)}, bf16[2,1536,384]{2,1,0:T(8,128)(2,1)}, u32[]{:S(2)}) copy-start(bf16[2,1536,384]{2,1,0:T(8,128)(2,1)} %text_weight_ref.1) | copy-start | bytes 7077892
  499.1 191.2 %reduce-scatter.7.cloned.1.call-start = ((), (), s32[]{:S(2)}) async-start(), calls=%async_computation.6 | async-start | bytes 7962624 | tf_op jit(solution)/shard_map/reduce_scatter | solution.py:213
  512.3 1.0 copy-start.15
  512.3 1.0 copy-start.20
  512.3 3.3 copy-start.23
  512.3 199.9 %reduce-scatter.9.cloned.1.call-start = ((), (), s32[]{:S(2)}) async-start(), calls=%async_computation.7 | async-start | bytes 6635520 | tf_op jit(solution)/shard_map/reduce_scatter | solution.py:213
  584.4 4.3 copy-start.2
  588.7 4.6 copy-start.5
  593.3 8.5 %copy-start.17 = (bf16[384,1536]{1,0:T(8,128)(2,1)S(1)}, bf16[384,1536]{1,0:T(8,128)(2,1)}, u32[]{:S(2)}) copy-start(bf16[384,1536]{1,0:T(8,128)(2,1)} %refs_1_.4) | copy-start | bytes 3538948
  599.5 2.2 copy-start.6
  605.4 4.9 copy-start.7
  605.4 4.9 copy-start.22
  610.3 2.9 copy-start.14
  613.3 3.0 copy-start.45
  613.3 4.3 copy-start.36
  615.7 217.8 %reduce-scatter.11.cloned.1.call-start = ((), (), s32[]{:S(2)}) async-start(), calls=%async_computation.9 | async-start | bytes 3981312 | tf_op jit(solution)/shard_map/reduce_scatter | solution.py:213
  690.3 13.4 %copy-start.11 = (bf16[780,1536]{1,0:T(8,128)(2,1)S(1)}, bf16[780,1536]{1,0:T(8,128)(2,1)}, u32[]{:S(2)}) copy-start(bf16[780,1536]{1,0:T(8,128)(2,1)} %copy-done.10) | copy-start | bytes 7188484
  703.8 2.9 copy-start.41
  706.7 1.8 copy-start.42
  710.2 2.4 copy-start.19
  712.2 1.8 copy-start.37
  714.1 66.4 %copy-start.25 = (f32[1536]{0:T(1024)S(1)}, f32[1536]{0:T(1024)}, u32[]{:S(2)}) copy-start(f32[1536]{0:T(1024)} %copy-done.24) | copy-start | bytes 18436
  714.1 66.4 %copy-start.27 = (f32[780]{0:T(1024)S(1)}, f32[780]{0:T(1024)}, u32[]{:S(2)}) copy-start(f32[780]{0:T(1024)} %copy-done.26) | copy-start | bytes 9364
  778.2 6.3 copy-start.33
  778.2 6.4 copy-start.4
  778.3 6.4 copy-start.30
  813.6 16.2 %copy-start.18 = (bf16[192,2240]{1,0:T(8,128)(2,1)S(1)}, bf16[192,2240]{1,0:T(8,128)(2,1)}, u32[]{:S(2)}) copy-start(bf16[192,2240]{1,0:T(8,128)(2,1)} %reduce-scatter.7.cloned.1.call-done) | copy-start | bytes 2580484
  813.6 18.2 %copy-start.21 = (bf16[192,1920]{1,0:T(8,128)(2,1)S(1)}, bf16[192,1920]{1,0:T(8,128)(2,1)}, u32[]{:S(2)}) copy-start(bf16[192,1920]{1,0:T(8,128)(2,1)} %reduce-scatter.9.cloned.1.call-done) | copy-start | bytes 2211844
Sparse Core Ops, SparseCore 0:
  10.4 33.5 all-gather.1
  385.3 64.7 reduce-scatter.4
  499.2 40.6 all-reduce.10
  543.3 64.6 reduce-scatter.6
  615.8 76.6 reduce-scatter.8
  712.3 49.0 reduce-scatter.10

commit v7 on v6

--- a/solution.py
+++ b/solution.py
@@ -1549,13 +1549,9 @@
         9,
     )
     grad_self_bias = proj_sums[:3]
-    self_in_mix = jnp.concatenate(
-        [
-            jnp.dot(attn_in.T, grad_proj_low[j], preferred_element_type=wide_type).astype(low_type)
-            for j in range(3)
-        ],
-        axis=-1,
-    )
+    self_in_mix = jnp.dot(
+        attn_in.T, jnp.concatenate(grad_proj_low, axis=-1), preferred_element_type=wide_type
+    ).astype(low_type)
     grad_proj_low, self_in_mix, part_group = lax.optimization_barrier(
         (grad_proj_low, row_major(self_in_mix), part_group)
     )

time: 854 us -> 854 us (level)
    unnamed x99 -> x95, local copies, waits for them, and re-layouts: 31.4 us -> 32 us
where the time goes in v7:
time: 854 us; the launch traced here: 844 us
  Pallas kernels  588 us (69%)
  other arithmetic  91.8 us (11%)
  matrix products  78.2 us (9%)
  local copies, waits for them, and re-layouts  67.9 us (8%)
  between operations  17.8 us (2%)
    pallas_call x6, Pallas kernels, line_sum(): pl.pallas_call(functools.partial(line_kernel, len(sources), block, group,...  400 us
    pallas_call x1, Pallas kernels, attend_back(): pl.pallas_call(functools.partial(attend_back_kernel, true_rows), out_shap...  56.8 us
    pallas_call x1, Pallas kernels, attend(): pl.pallas_call(functools.partial(attend_kernel, true_rows), out_shape=(ja...  50.6 us
    unnamed x95, local copies, waits for them, and re-layouts  32 us
    pallas_call x1, Pallas kernels, cross_back(): pl.pallas_call(functools.partial(cross_back_kernel, model_width), out_sha...  21.7 us
    reduce_sum x4, other arithmetic, layer_norm(): centred = values - jnp.mean(values, axis=-1, keepdims=True)  19.1 us
    pallas_call x1, Pallas kernels, project(): pl.pallas_call(project_kernel, out_shape=(jax.ShapeDtypeStruct((2, rows,...  18.2 us
    dot_general x1, matrix products, shards(): jnp.dot(grad_three_low, ffn_out.T, preferred_element_type=wide_type)  17.2 us
  transfers between devices with their start and end apart: 6, of which 0 were waited for; matrix products, arithmetic and copies ran while one was open for 20% of the time, Pallas kernels for 52%

profile of v7, /device:TPU:0, one launch (start us, length us, event | category | flops | bytes accessed | tf_op | source)
XLA Modules:
  0.0 844.1 jit_solution(9910581821965241560)
XLA Ops:
  7.2 1.9 convert_element_type.203
  9.3 6.4 reduce_sum.237
  15.7 3.0 multiply_reduce_fusion.5
  24.1 3.2 add_convert_fusion.2
  27.3 1.4 copy-done.10
  28.8 1.7 pad.32.rows_ref
  30.5 18.2 %project.1 = (f32[2,896,384]{2,1,0:T(8,128)}, bf16[896,384]{1,0:T(8,128)(2,1)}, bf16[2,784,384]{2,1,0:T(8,128)(2,1)}, f32[8,896]{1,0:T(8,128)}) custom-call(bf16[896,1536]{1,0:T(8,128)(2,1)} %pad.32.rows_ref, bf16[3,1536,384]{2,1,0:T(8,128)(2,1)} %refs_3_.1, f32[3,384]{1,0:T(4,128)} %bias_ref.2, f32[2,384]{1,0:T(2,128)} %get-tuple-element.192.gain_ref, ...), custom_call_target="tpu_custom_call" | custom-call | tf_op jit(solution)/shard_map/project/pallas_call | solution.py:718
  48.7 50.6 %attend.1 = (bf16[896,384]{1,0:T(8,128)(2,1)}, f32[3,128,896]{2,1,0:T(8,128)}, f32[3,1,896]{2,1,0:T(1,128)}, bf16[3,2,784,384]{3,2,1,0:T(8,128)(2,1)}) custom-call(s32[1]{0:T(128)} %dynamic_slice.11.length_ref, bf16[896,384]{1,0:T(8,128)(2,1)} %get-tuple-element.61.query_ref, bf16[2,784,384]{2,1,0:T(8,128)(2,1)} %get-tuple-element.62.kv_ref), custom_call_target="tpu_custom_call" | custom-call | flops 1000000000 | bytes 150000000 | tf_op jit(solution)/shard_map/attend/pallas_call | solution.py:479
  99.4 70.5 %line_sum_0.1 = bf16[784,1536]{1,0:T(8,128)(2,1)} custom-call(bf16[896,384]{1,0:T(8,128)(2,1)} %get-tuple-element.63.refs_0_, bf16[384,1536]{1,0:T(8,128)(2,1)} %refs_1_.4), custom_call_target="tpu_custom_call" | custom-call | flops 924844032 | bytes 230000000 | tf_op jit(solution)/shard_map/line_sum_0/pallas_call | solution.py:192
  169.9 3.9 fusion.55
  176.1 1.5 copy-done.12
  177.6 1.7 pad.35.rows_ref
  180.0 16.3 %cross_attend.1 = (f32[896,384]{1,0:T(8,128)}, f32[512,384]{1,0:T(8,128)}, bf16[896,384]{1,0:T(8,128)(2,1)}, bf16[2,512,384]{2,1,0:T(8,128)(2,1)}, f32[8,896]{1,...) custom-call(bf16[896,1536]{1,0:T(8,128)(2,1)} %pad.35.rows_ref, ...), custom_call_target="tpu_custom_call" | custom-call | tf_op jit(solution)/shard_map/cross_attend/pallas_call | solution.py:937
  196.2 67.4 %line_sum_1.1 = bf16[784,1536]{1,0:T(8,128)(2,1)} custom-call(bf16[896,384]{1,0:T(8,128)(2,1)} %get-tuple-element.64.refs_0_, bf16[384,1536]{1,0:T(8,128)(2,1)} %refs_1_.5), custom_call_target="tpu_custom_call" | custom-call | flops 924844032 | bytes 230000000 | tf_op jit(solution)/shard_map/line_sum_1/pallas_call | solution.py:192
  263.7 4.0 fusion.54
  269.1 9.5 %multiply_convert_fusion = (bf16[780,2240]{1,0:T(8,128)(2,1)S(1)}, f32[780,2240]{1,0:T(8,128)}) fusion(f32[2240]{0:T(1024)S(1)} %copy-done.41, bf16[1536,2240]{0,1:T(8,128)(2,1)S(1)} %bitcast.105, f32[780,1536]{1,0:T(8,128)S(1)} %get-tuple-element.170, f32[1536]{0:T(1024)S(1)} %get-tuple-element.155, f32[1536]{0:T(1024)S(1)} %get-tuple-element.153, ...), kind=kOutput, calls=%fused_computation.15 | convolution fusion | flops 5390858240 | bytes 22184288 | tf_op jit(solution)/shard_map/dot_general | solution.py:1339
  278.6 2.1 pad.36.refs_0_
  280.7 67.7 %line_sum_2.1 = bf16[784,1536]{1,0:T(8,128)(2,1)} custom-call(bf16[784,2240]{1,0:T(8,128)(2,1)} %pad.36.refs_0_, bf16[2240,1536]{1,0:T(8,128)(2,1)} %refs_1_.6), custom_call_target="tpu_custom_call" | custom-call | flops 5394923520 | bytes 230000000 | tf_op jit(solution)/shard_map/line_sum_2/pallas_call | solution.py:192
  348.5 7.7 multiply_reduce_fusion
  356.2 2.1 copy-done.9
  358.4 9.6 %convolution_convert_fusion.1 = bf16[1536,2240]{1,0:T(8,128)(2,1)} fusion(bf16[780,2240]{1,0:T(8,128)(2,1)S(1)} %get-tuple-element.195, f32[780,1536]{1,0:T(8,128)S(1)} %get-tuple-element.167, f32[1536]{0:T(1024)S(1)} %get-tuple-element.154), kind=kOutput, calls=%fused_computation.1 | convolution fusion | flops 5373235200 | bytes 15174144 | tf_op jit(solution)/shard_map/dot_general | solution.py:1348
  368.0 17.2 %fusion.56 = (bf16[2240]{0:T(1024)(128)(2,1)S(1)}, bf16[780,2240]{1,0:T(8,128)(2,1)}) fusion(bf16[2240,1536]{1,0:T(8,128)(2,1)} %refs_1_.6, f32[780,1536]{1,0:T(8,128)} %copy-done.9, f32[1536]{0:T(1024)S(1)} %get-tuple-element.154, f32[780,2240]{1,0:T(8,128)} %get-tuple-element.196, f32[2240]{0:T(1024)S(1)} %copy-done.41), kind=kOutput, calls=%fused_computation.160 | convolution fusion | flops 5415214080 | bytes 22176384 | tf_op jit(solution)/shard_map/dot_general | solution.py:1349
  386.0 4.1 pad.37.refs_0_
  390.1 66.2 %line_sum_3.1 = bf16[784,1536]{1,0:T(8,128)(2,1)} custom-call(bf16[784,2240]{1,0:T(8,128)(2,1)} %pad.37.refs_0_, bf16[2240,1536]{1,0:T(8,128)(2,1)} %bitcast.103), custom_call_target="tpu_custom_call" | custom-call | flops 5394923520 | bytes 230000000 | tf_op jit(solution)/shard_map/line_sum_3/pallas_call | solution.py:192
  456.3 4.2 fusion.13
  460.5 4.3 fusion.14
  464.9 4.9 fusion.52
  469.8 1.4 convolution_convert_fusion.8
  472.8 1.7 constant_dynamic-slice_fusion.key_pre_ref
  475.1 21.7 %cross_back.1 = (bf16[896,384]{1,0:T(8,128)(2,1)}, bf16[2,128,384]{2,1,0:T(8,128)(2,1)}, f32[8,384]{1,0:T(8,128)}) custom-call(bf16[896,384]{1,0:T(8,128)(2,1)} %get-tuple-element.69.query_ref, bf16[2,512,384]{2,1,0:T(8,128)(2,1)} %get-tuple-element.70.kv_ref, f32[3,128,896]{2,1,0:T(8,128)} %get-tuple-element.71.turned_ref, ...), custom_call_target="tpu_custom_call" | custom-call | tf_op jit(solution)/shard_map/cross_back/pallas_call | solution.py:1091
  496.8 2.6 fusion.24
  499.7 12.9 %convolution_convert_fusion = bf16[1536,2240]{1,0:T(8,128)(2,1)} fusion(bf16[780,2240]{1,0:T(8,128)(2,1)} %get-tuple-element.68, f32[780,1536]{1,0:T(8,128)} %copy-done.1, f32[1536]{0:T(1024)S(1)} %get-tuple-element.155, f32[1536]{0:T(1024)S(1)} %get-tuple-element.153, f32[780]{0:T(1024)S(1)} %fusion.44, f32[780]{0:T(1024)S(1)} %broadcast_multiply_fusion.3), kind=kOutput, calls=%fused_computation | convolution fusion | flops 5376829440 | bytes 15186528 | tf_op jit(solution)/shard_map/dot_general | solution.py:1356
  513.6 2.2 fusion.18
  515.8 5.3 fusion.21
  521.1 63.5 %line_sum_4.1 = bf16[784,1536]{1,0:T(8,128)(2,1)} custom-call(bf16[896,384]{1,0:T(8,128)(2,1)} %get-tuple-element.78.refs_0_, bf16[1536,384]{1,0:T(8,128)(2,1)} %refs_1_.7), custom_call_target="tpu_custom_call" | custom-call | flops 924844032 | bytes 230000000 | tf_op jit(solution)/shard_map/line_sum_4/pallas_call | solution.py:192
  584.6 4.3 fusion.12
  589.0 4.6 fusion.15
  593.6 6.2 multiply_reduce_fusion.6
  599.8 2.2 copy-done.6
  602.0 2.2 convolution_convert_fusion.7
  604.3 1.4 copy.53
  605.7 4.9 fusion.19
  610.6 2.9 fusion.20
  613.5 1.2 fusion.33
  617.6 2.1 slice_reduce_fusion.2
  619.8 10.0 %copy.60 = f32[1,780,1536]{2,0,1:T(1,128)} copy(f32[1,780,1536]{2,1,0:T(8,128)} %get-tuple-element.173) | data formatting | bytes 9584640
  629.7 2.0 convert_element_type.232
  632.8 2.0 pad.39.grad_ref
  634.8 56.8 %attend_back.1 = (f32[896,384]{1,0:T(8,128)}, f32[2,896,384]{2,1,0:T(8,128)}) custom-call(s32[1]{0:T(128)} %dynamic_slice.11.length_ref, bf16[896,384]{1,0:T(8,128)(2,1)} %get-tuple-element.61.query_ref, bf16[2,784,384]{2,1,0:T(8,128)(2,1)} %get-tuple-element.62.kv_ref, bf16[3,2,784,384]{3,2,1,0:T(8,128)(2,1)} %get-tuple-element.65.got_ref, ...), custom_call_target="tpu_custom_call" | custom-call | flops 1000000000 | bytes 200000000 | tf_op jit(solution)/shard_map/attend_back/pallas_call | solution.py:595
  691.6 13.7 %unproject.1 = (bf16[896,384]{1,0:T(8,128)(2,1)}, bf16[896,384]{1,0:T(8,128)(2,1)}, bf16[896,384]{1,0:T(8,128)(2,1)}, f32[8,384]{1,0:T(8,128)}) custom-call(f32[896,384]{1,0:T(8,128)} %get-tuple-element.83.query_grad_ref, f32[2,896,384]{2,1,0:T(8,128)} %get-tuple-element.84.kv_grad_ref, f32[2,896,384]{2,1,0:T(8,128)} %get-tuple-element.85.pre_ref, ...), custom_call_target="tpu_custom_call" | custom-call | tf_op jit(solution)/shard_map/unproject/pallas_call | solution.py:789
  705.4 7.4 convolution_convert_fusion.2
  713.9 1.3 convert_bitcast_fusion
  715.3 64.4 %line_sum_5.1 = bf16[784,1536]{1,0:T(8,128)(2,1)} custom-call(bf16[896,384]{1,0:T(8,128)(2,1)} %get-tuple-element.91.refs_0_, bf16[896,384]{1,0:T(8,128)(2,1)} %get-tuple-element.92.refs_1_, bf16[896,384]{1,0:T(8,128)(2,1)} %get-tuple-element.93.refs_2_, bf16[3,1536,384]{2,1,0:T(8,128)(2,1)} %refs_3_.1), custom_call_target="tpu_custom_call" | custom-call | flops 2774532096 | bytes 230000000 | tf_op jit(solution)/shard_map/line_sum_5/pallas_call | solution.py:192
  779.7 2.2 slice_reduce_fusion
  782.0 4.0 fusion.11
  786.1 4.8 fusion.50
  792.4 10.6 %plane_sum.1 = (f32[192,128]{1,0:T(8,128)}, f32[192,128]{1,0:T(8,128)}) custom-call(bf16[192,128]{1,0:T(8,128)(2,1)} %pad_bitcast_fusion.value_ref), custom_call_target="tpu_custom_call" | custom-call | tf_op jit(solution)/shard_map/plane_sum/pallas_call | solution.py:267
  803.0 1.3 slice.222
  804.2 1.3 slice.226
  807.1 6.8 add_bitcast_fusion
  813.9 9.6 %copy.61 = f32[1,780,1536]{2,0,1:T(1,128)} copy(f32[1,780,1536]{2,1,0:T(8,128)} %add_bitcast_fusion) | data formatting | bytes 9584640
  823.5 1.4 slice.191
  827.4 1.4 slice_bitcast_fusion.7
  830.1 1.3 convert_element_type.235
  (188 shorter events, 29.3 us)
Async XLA Ops:
  7.2 172.8 %all-gather.2.cloned.1.call-start = ((), (), s32[]{:S(2)}) async-start(), calls=%async_computation.4 | async-start | bytes 1966080 | tf_op jit(solution)/shard_map/all_gather | solution.py:1286
  9.2 503.4 %reduce-scatter.5.cloned.1.call-start = ((), (), s32[]{:S(2)}) async-start(), calls=%async_computation.5 | async-start | bytes 7962624 | tf_op jit(solution)/shard_map/reduce_scatter | solution.py:213
  9.2 9.5 %copy-start.40 = (f32[4,384]{1,0:T(4,128)S(1)}, f32[4,384]{1,0:T(4,128)}, u32[]{:S(2)}) copy-start(f32[4,384]{1,0:T(4,128)} %param.31) | copy-start | bytes 18436
  9.3 10.1 %copy-start.38 = (s32[3,1,780]{2,1,0:T(1,128)S(1)}, s32[3,1,780]{2,1,0:T(1,128)}, u32[]{:S(2)}) copy-start(s32[3,1,780]{2,1,0:T(1,128)} %param.26) | copy-start | bytes 28084
  9.3 10.1 %copy-start.31 = (f32[6,1536]{1,0:T(8,128)S(1)}, f32[6,1536]{1,0:T(8,128)}, u32[]{:S(2)}) copy-start(f32[6,1536]{1,0:T(8,128)} %param.27) | copy-start | bytes 110596
  9.3 10.1 %copy-start.34 = (f32[1,6,1536]{2,0,1:T(1,128)S(1)}, f32[1,6,1536]{2,0,1:T(1,128)}, u32[]{:S(2)}) copy-start(f32[1,6,1536]{2,0,1:T(1,128)} %param.24) | copy-start | bytes 110596
  15.7 8.4 copy-start.26
  15.7 7.0 copy-start.42
  18.7 8.5 %copy-start.32 = (f32[780]{0:T(1024)}, f32[780]{0:T(1024)S(1)}, u32[]{:S(2)}) copy-start(f32[780]{0:T(1024)S(1)} %multiply_reduce_fusion.5) | copy-start | bytes 9364
  18.8 8.5 %copy-start.29 = (f32[780]{0:T(1024)}, f32[780]{0:T(1024)S(1)}, u32[]{:S(2)}) copy-start(f32[780]{0:T(1024)S(1)} %fusion.42) | copy-start | bytes 9364
  19.6 7.7 copy-start.24
  27.3 1.5 copy-start.10
  48.7 121.1 %copy-start.35 = (f32[3,1536]{1,0:T(4,128)S(1)}, f32[3,1536]{1,0:T(4,128)}, u32[]{:S(2)}) copy-start(f32[3,1536]{1,0:T(4,128)} %param.41) | copy-start | bytes 55300
  173.9 2.2 copy-start
  173.9 0.7 copy-start.28
  173.9 0.8 copy-start.39
  176.1 1.5 copy-start.12
  263.6 4.7 slice-start
  263.7 5.4 slice-start.1
  267.7 11.0 %copy-start.1 = (f32[780,1536]{1,0:T(8,128)}, f32[780,1536]{1,0:T(8,128)S(1)}, u32[]{:S(2)}) copy-start(f32[780,1536]{1,0:T(8,128)S(1)} %get-tuple-element.170) | copy-start | bytes 14376964
  267.7 1.4 copy-start.41
  356.2 2.1 copy-start.9
  385.2 244.6 %all-reduce.11.cloned.1.call-start = ((), (), s32[]{:S(2)}) async-start(), calls=%async_computation.8 | async-start | bytes 786432 | tf_op jit(solution)/shard_map/psum | solution.py:1459
  456.3 4.2 copy-start.3
  464.9 4.9 copy-start.16
  469.8 2.1 copy-start.8
  471.9 24.9 %copy-start.13 = (bf16[2,1536,384]{2,1,0:T(8,128)(2,1)S(1)}, bf16[2,1536,384]{2,1,0:T(8,128)(2,1)}, u32[]{:S(2)}) copy-start(bf16[2,1536,384]{2,1,0:T(8,128)(2,1)} %text_weight_ref.1) | copy-start | bytes 7077892
  499.4 192.1 %reduce-scatter.7.cloned.1.call-start = ((), (), s32[]{:S(2)}) async-start(), calls=%async_computation.6 | async-start | bytes 7962624 | tf_op jit(solution)/shard_map/reduce_scatter | solution.py:213
  512.6 1.0 copy-start.15
  512.6 1.0 copy-start.20
  512.6 3.3 copy-start.23
  512.6 200.1 %reduce-scatter.9.cloned.1.call-start = ((), (), s32[]{:S(2)}) async-start(), calls=%async_computation.7 | async-start | bytes 6635520 | tf_op jit(solution)/shard_map/reduce_scatter | solution.py:213
  584.6 4.4 copy-start.2
  588.9 4.6 copy-start.5
  593.5 8.5 %copy-start.17 = (bf16[384,1536]{1,0:T(8,128)(2,1)S(1)}, bf16[384,1536]{1,0:T(8,128)(2,1)}, u32[]{:S(2)}) copy-start(bf16[384,1536]{1,0:T(8,128)(2,1)} %refs_1_.4) | copy-start | bytes 3538948
  599.8 2.2 copy-start.6
  605.7 4.9 copy-start.7
  605.7 4.9 copy-start.22
  610.6 2.9 copy-start.14
  613.5 2.8 copy-start.43
  613.5 4.1 copy-start.36
  616.0 217.9 %reduce-scatter.11.cloned.1.call-start = ((), (), s32[]{:S(2)}) async-start(), calls=%async_computation.9 | async-start | bytes 3981312 | tf_op jit(solution)/shard_map/reduce_scatter | solution.py:213
  691.6 13.8 %copy-start.11 = (bf16[780,1536]{1,0:T(8,128)(2,1)S(1)}, bf16[780,1536]{1,0:T(8,128)(2,1)}, u32[]{:S(2)}) copy-start(bf16[780,1536]{1,0:T(8,128)(2,1)} %copy-done.10) | copy-start | bytes 7188484
  712.7 1.2 copy-start.19
  712.7 2.5 copy-start.37
  715.3 66.7 %copy-start.25 = (f32[1536]{0:T(1024)S(1)}, f32[1536]{0:T(1024)}, u32[]{:S(2)}) copy-start(f32[1536]{0:T(1024)} %copy-done.24) | copy-start | bytes 18436
  715.3 66.7 %copy-start.27 = (f32[780]{0:T(1024)S(1)}, f32[780]{0:T(1024)}, u32[]{:S(2)}) copy-start(f32[780]{0:T(1024)} %copy-done.26) | copy-start | bytes 9364
  779.7 6.3 copy-start.33
  779.7 6.4 copy-start.4
  779.7 6.4 copy-start.30
  813.9 16.2 %copy-start.18 = (bf16[192,2240]{1,0:T(8,128)(2,1)S(1)}, bf16[192,2240]{1,0:T(8,128)(2,1)}, u32[]{:S(2)}) copy-start(bf16[192,2240]{1,0:T(8,128)(2,1)} %reduce-scatter.7.cloned.1.call-done) | copy-start | bytes 2580484
  813.9 18.2 %copy-start.21 = (bf16[192,1920]{1,0:T(8,128)(2,1)S(1)}, bf16[192,1920]{1,0:T(8,128)(2,1)}, u32[]{:S(2)}) copy-start(bf16[192,1920]{1,0:T(8,128)(2,1)} %reduce-scatter.9.cloned.1.call-done) | copy-start | bytes 2211844
Sparse Core Ops, SparseCore 0:
  10.4 33.5 all-gather.1
  385.3 64.7 reduce-scatter.4
  499.6 40.6 all-reduce.10
  543.6 64.7 reduce-scatter.6
  616.1 76.6 reduce-scatter.8
  712.9 48.1 reduce-scatter.10
